TPU v7x, 32 devices: a whole 2x2x4 slice. The times are simulated.
32 devices in a mesh: groups: 2 (over y), patch: 4 (over z), view: 2 (over x), head: 2 (over core).
Axes of the slice: x: 2, y: 2, z: 4, core: 2. Of those that a mesh axis runs over, the one named last changes fastest.
Arguments:
- tokens: bfloat16 [8192, 768], P(('groups', 'patch', 'view', 'head')), parts along dimension 0, may hold values from -6 to 6
- w_kv: bfloat16 [768, 1536], replicated, may hold values from -0.21875 to 0.21875
- w_rate: bfloat16 [3, 768], replicated, may hold values from -0.21875 to 0.21875
- fast_weights: bfloat16 [512, 3, 3, 256], replicated, as said below
- queries: bfloat16 [8192, 768], P(('groups', 'patch', 'view', 'head')), parts along dimension 0, may hold values from -6 to 6
- w_query: bfloat16 [768, 768], replicated, may hold values from -0.21875 to 0.21875
- out_gain: bfloat16 [768], replicated, may hold values from 0.25 to 1.75
- w_out: bfloat16 [768, 768], replicated, may hold values from -0.21875 to 0.21875
Outputs:
- decoded: bfloat16 [8192, 768], P(('groups', 'patch', 'view', 'head')), parts along dimension 0
There are 2 independent parts, one for each index of `groups`. A program takes and returns all parts, laid end to end along the dimension named above; an argument that names none is the same for every part. Nothing has to cross between parts.
Inputs may be any that keep to these rules, and one draw needn't show every extreme that they name: `fast_weights`: Real-valued entries.
All inputs are finite; a program needn't handle non-finite values.
Results may differ from a plain program's by a relative error of at most 0.035.
Values may be sent and summed in bfloat16 or wider, within the bound.
No kernel may reach another device: no remote copies, remote signals or barrier semaphores. Data moves between devices by JAX's collectives and lax.ppermute only.
A program may use at most 64 MiB of HBM per device.

v0:
```python
import jax
import jax.numpy as jnp
from jax import lax
from jax.sharding import PartitionSpec as P

HEADS = 3
HD = 256
FF = 512
STEPS = 3


coef_a = 3.4445
coef_b = -4.775
coef_c = 2.0315
eta_rate = 3.0
eps_small = 1e-06


def unit_heads(raw):
    shaped = raw.reshape(raw.shape[0], HEADS, HD)
    return shaped / jnp.sqrt(jnp.sum(shaped * shaped, -1, keepdims=True) + eps_small)


def grad_term(keys, scaled, fast_weights):
    fp = jnp.float32
    gate_pre = jnp.einsum("thd,nhd->hnt", keys, fast_weights[:, 0], preferred_element_type=fp)
    up_pre = jnp.einsum("thd,nhd->hnt", keys, fast_weights[:, 1], preferred_element_type=fp)
    sig = jax.nn.sigmoid(gate_pre)
    act = gate_pre * sig
    hidden = (act * up_pre).astype(jnp.bfloat16)
    back = jnp.einsum("thd,nhd->hnt", scaled, fast_weights[:, 2], preferred_element_type=fp)
    d_gate = (back * up_pre * sig * (1.0 + gate_pre * (1.0 - sig))).astype(jnp.bfloat16)
    d_up = (back * act).astype(jnp.bfloat16)
    g_gate = jnp.einsum("hnt,thd->nhd", d_gate, keys, preferred_element_type=fp)
    g_up = jnp.einsum("hnt,thd->nhd", d_up, keys, preferred_element_type=fp)
    g_down = jnp.einsum("hnt,thd->nhd", hidden, scaled, preferred_element_type=fp)
    return jnp.stack([g_gate, g_up, g_down], 1)


def start_point(shard, total):
    return (shard / (jnp.sqrt(total) + eps_small)[None, :, :, None]).astype(jnp.bfloat16)


def newton(ortho, gram_total):
    fp = jnp.float32
    for step in range(STEPS):
        partial_gram = jnp.einsum("nkhi,nkhj->khij", ortho, ortho, preferred_element_type=fp)
        gram = gram_total(partial_gram).astype(jnp.bfloat16)
        square = jnp.einsum("khij,khjl->khil", gram, gram, preferred_element_type=fp)
        poly = (coef_b * gram.astype(fp) + coef_c * square).astype(jnp.bfloat16)
        mixed = jnp.einsum("nkhi,khij->nkhj", ortho, poly, preferred_element_type=fp)
        ortho = (coef_a * ortho.astype(fp) + mixed).astype(jnp.bfloat16)
    return ortho


def renorm(old_rows, ortho):
    fp = jnp.float32
    old_f = old_rows.astype(fp)
    moved = old_f + eta_rate * ortho.astype(fp)
    old_norm = jnp.sqrt(jnp.sum(old_f * old_f, -1, keepdims=True))
    new_norm = jnp.sqrt(jnp.sum(moved * moved, -1, keepdims=True)) + eps_small
    return (moved * old_norm / new_norm).astype(jnp.bfloat16)


def local(tokens, w_kv, w_rate, fast_weights, queries, w_query, out_gain, w_out):
    fp = jnp.float32
    width = tokens.shape[1]
    both = jnp.dot(tokens, w_kv, preferred_element_type=fp)
    keys = unit_heads(both[:, :width]).astype(jnp.bfloat16)
    rate = jax.nn.softplus(jnp.einsum("td,hd->th", tokens, w_rate, preferred_element_type=fp))
    scaled = (rate[:, :, None] * both[:, width:].reshape(-1, HEADS, HD)).astype(jnp.bfloat16)
    qry = unit_heads(jnp.dot(queries, w_query, preferred_element_type=fp)).astype(jnp.bfloat16)
    rows = FF // lax.axis_size("patch")
    scattered = lax.psum_scatter(
        grad_term(keys, scaled, fast_weights), "patch", scatter_dimension=0, tiled=True
    )
    shard = lax.psum(scattered, ("view", "head"))
    total = lax.psum(jnp.sum(shard * shard, axis=(0, 3)), "patch")
    begin = start_point(shard, total)
    ortho = newton(begin, lambda part: lax.psum(part, "patch"))
    own = lax.dynamic_slice_in_dim(fast_weights, lax.axis_index("patch") * rows, rows, 0)
    fresh = renorm(own, ortho)
    piece = lax.all_gather(fresh, "patch", axis=0, tiled=True)
    gate_pre = jnp.einsum("thd,nhd->hnt", qry, piece[:, 0], preferred_element_type=fp)
    up_pre = jnp.einsum("thd,nhd->hnt", qry, piece[:, 1], preferred_element_type=fp)
    q_hidden = (jax.nn.silu(gate_pre) * up_pre).astype(jnp.bfloat16)
    read = jnp.einsum("hnt,nhd->thd", q_hidden, piece[:, 2], preferred_element_type=fp)
    normed = read * lax.rsqrt(jnp.mean(read * read, -1, keepdims=True) + eps_small)
    normed = normed * out_gain.astype(fp).reshape(HEADS, HD)
    normed = normed.reshape(read.shape[0], width).astype(jnp.bfloat16)
    return jnp.dot(normed, w_out, preferred_element_type=fp).astype(jnp.bfloat16)


def solution(mesh):
    in_specs = (
        P(("groups", "patch", "view", "head"), None),
        P(),
        P(),
        P(),
        P(("groups", "patch", "view", "head"), None),
        P(),
        P(),
        P(),
    )
    out_specs = P(("groups", "patch", "view", "head"), None)
    return jax.shard_map(local, mesh=mesh, in_specs=in_specs, out_specs=out_specs, check_vma=False)
```

profile of v0, /device:TPU:11, one launch (start us, length us, event | category | flops | bytes accessed | tf_op | source)
XLA Modules:
  0.0 494.6 jit_solution(17543853494368263222)
XLA Ops:
  6.5 0.0 reduce-scatter.2.cloned.1.call-start
  6.5 1.7 copy-done
  8.2 1.8 fusion.56
  10.0 1.3 fusion.55
  11.2 1.4 copy.33
  12.6 0.1 multiply_reduce_fusion.4
  12.7 0.1 divide_convert_fusion.3
  12.8 2.7 fusion.33
  15.5 2.8 fusion.35
  18.3 1.1 copy.34
  19.4 0.0 copy-done.8
  19.4 1.3 compare_select_fusion
  20.7 1.9 fusion.37
  22.7 0.7 convolution_bitcast_fusion.1
  23.3 0.7 copy-done.6
  24.1 0.8 convolution_bitcast_fusion.2
  24.9 0.3 copy-done.2
  25.2 0.7 convolution_bitcast_fusion
  25.9 2.6 pad_maximum_fusion
  28.5 0.0 reduce-scatter.2.cloned.1.call-update
  28.5 0.0 all-reduce.5.cloned.1.call-start
  28.6 86.6 %reduce-scatter.2.cloned.1.call-done = f32[128,3,3,256]{0,3,2,1:T(8,128)} async-done(((f32[512,3,3,256]{0,3,2,1:T(8,128)}), f32[128,3,3,256]{0,3,2,1:T(8,128)}) %reduce-scatter.2.cloned.1.call-update) | async-done | bytes 1179664 | tf_op jit(solution)/shard_map/reduce_scatter | solution.py:74
  115.1 0.0 all-reduce.5.cloned.1.call-update
  115.1 0.0 all-gather.2.cloned.1.call-start
  115.2 1.1 constant_dynamic-slice_fusion
  116.3 0.3 copy.76
  116.6 0.1 fusion.17
  116.8 37.8 %all-reduce.5.cloned.1.call-done = f32[128,3,3,256]{0,3,2,1:T(8,128)} async-done(((f32[128,3,3,256]{0,3,2,1:T(8,128)}), f32[128,3,3,256]{0,3,2,1:T(8,128)}) %all-reduce.5.cloned.1.call-update) | async-done | bytes 1179664 | tf_op jit(solution)/shard_map/psum | solution.py:77
  154.6 1.5 multiply_reduce_fusion.1
  156.0 7.0 %psum.36 = f32[3,3]{1,0:T(4,128)S(1)} all-reduce(f32[3,3]{1,0:T(4,128)S(1)} %multiply_reduce_fusion.1), channel_id=1, replica_groups=mesh['groups'=2,'patch'=4,'view'=2,'head'=2] {'patch'}, use_global_device_ids=true, to_apply=%region_4.5 | all-reduce | flops 9 | bytes 72 | tf_op jit(solution)/shard_map/psum | solution.py:78
  163.0 3.6 fusion.54
  166.6 79.5 %all-reduce.6 = bf16[3,3,256,256]{3,2,1,0:T(8,128)(2,1)} all-reduce(f32[3,3,256,256]{3,2,1,0:T(8,128)} %fusion.54), channel_id=1, replica_groups=mesh['groups'=2,'patch'=4,'view'=2,'head'=2] {'patch'}, use_global_device_ids=true, to_apply=%region_5.6 | all-reduce | flops 589824 | bytes 3538944 | tf_op jit(solution)/shard_map/psum | solution.py:80
  246.1 3.7 fusion.12
  249.9 1.9 fusion.57
  251.7 79.9 %all-reduce.7 = bf16[3,3,256,256]{3,2,1,0:T(8,128)(2,1)} all-reduce(f32[3,3,256,256]{3,2,1,0:T(8,128)} %fusion.57), channel_id=1, replica_groups=mesh['groups'=2,'patch'=4,'view'=2,'head'=2] {'patch'}, use_global_device_ids=true, to_apply=%region_6.7 | all-reduce | flops 589824 | bytes 3538944 | tf_op jit(solution)/shard_map/psum | solution.py:80
  331.6 3.0 fusion.13
  334.7 1.9 fusion.58
  336.6 78.8 %all-reduce.8 = bf16[3,3,256,256]{3,2,1,0:T(8,128)(2,1)} all-reduce(f32[3,3,256,256]{3,2,1,0:T(8,128)} %fusion.58), channel_id=1, replica_groups=mesh['groups'=2,'patch'=4,'view'=2,'head'=2] {'patch'}, use_global_device_ids=true, to_apply=%region_7.8 | all-reduce | flops 589824 | bytes 3538944 | tf_op jit(solution)/shard_map/psum | solution.py:80
  415.4 4.1 multiply_reduce_fusion
  419.6 2.3 divide_convert_fusion
  421.9 0.0 all-gather.2.cloned.1.call-update
  421.9 1.9 fusion.59
  423.8 0.1 multiply_reduce_fusion.3
  423.9 54.1 %all-gather.2.cloned.1.call-done = bf16[512,3,3,256]{0,3,2,1:T(8,128)(2,1)} async-done(((bf16[128,3,3,256]{0,3,2,1:T(8,128)(2,1)}), bf16[512,3,3,256]{0,3,2,1:T(8,128)(2,1)}) %all-gather.2.cloned.1.call-update) | async-done | bytes 2359312 | tf_op jit(solution)/shard_map/all_gather | solution.py:83
  477.9 2.7 fusion.32
  480.7 3.6 multiply_reduce_fusion.2
  484.2 1.3 multiply_convert_fusion.1
  485.6 2.5 convolution_convert_fusion
  (23 shorter events, 0.1 us)
Async XLA Ops:
  6.5 1.7 copy-start
  6.5 108.6 %reduce-scatter.2.cloned.1.call-start = ((), (), s32[]{:S(2)}) async-start(), calls=%async_computation.1 | async-start | bytes 5898240 | tf_op jit(solution)/shard_map/reduce_scatter | solution.py:74
  15.5 2.8 copy-start.1
  15.5 3.9 copy-start.8
  20.7 1.9 copy-start.5
  22.6 1.4 copy-start.6
  24.1 1.1 copy-start.2
  28.5 126.0 %all-reduce.5.cloned.1.call-start = ((), (), s32[]{:S(2)}) async-start(), calls=%async_computation.2 | async-start | bytes 2359296 | tf_op jit(solution)/shard_map/psum | solution.py:77
  115.1 362.8 %all-gather.2.cloned.1.call-start = ((), (), s32[]{:S(2)}) async-start(), calls=%async_computation.3 | async-start | bytes 2949120 | tf_op jit(solution)/shard_map/all_gather | solution.py:83
  116.6 50.0 %copy-start.3 = (bf16[128,3,3,256]{0,3,2,1:T(8,128)(2,1)}, bf16[128,3,3,256]{0,3,2,1:T(8,128)(2,1)S(1)}, u32[]{:S(2)}) copy-start(bf16[128,3,3,256]{0,3,2,1:T(8,128)(2,1)S(1)} %copy.76) | copy-start | bytes 1769476
  336.6 78.8 %copy-start.4 = (bf16[128,3,3,256]{0,3,2,1:T(8,128)(2,1)S(1)}, bf16[128,3,3,256]{0,3,2,1:T(8,128)(2,1)}, u32[]{:S(2)}) copy-start(bf16[128,3,3,256]{0,3,2,1:T(8,128)(2,1)} %copy-done.3) | copy-start | bytes 1769476
  419.6 2.3 copy-start.9
  419.6 2.4 copy-start.7
Sparse Core Ops, SparseCore 0:
  28.6 86.4 reduce-scatter.1
  117.5 37.0 all-reduce.4
  422.0 55.8 all-gather.1
where the time goes:
time: 500 us; the launch traced here: 495 us
  blocking collectives  245 us (49%)
  waiting for transfers between devices  178 us (36%)
  matrix products  41.6 us (8%)
  between operations  13.3 us (3%)
  other arithmetic  8.07 us (2%)
  local copies, waits for them, and re-layouts  7.94 us (2%)
    psum x3, blocking collectives, local(): ortho = newton(begin, lambda part: lax.psum(part, 'patch'))  238 us
    reduce_scatter x1, waiting for transfers between devices, local(): lax.psum_scatter(grad_term(keys, scaled, fast_weights), 'patch', scatter_...  86.6 us
    all_gather x1, waiting for transfers between devices, local(): piece = lax.all_gather(fresh, 'patch', axis=0, tiled=True)  54.1 us
    psum x1, waiting for transfers between devices, local(): shard = lax.psum(scattered, ('view', 'head'))  37.8 us
    dot_general x3, matrix products, newton(): jnp.einsum('nkhi,khij->nkhj', ortho, poly, preferred_element_type=fp)  10.9 us
  transfers between devices with their start and end apart: 3, of which 3 were waited for; matrix products, arithmetic and copies ran while one was open for 1% of the time, Pallas kernels for 0%

commit v1 on v0

v1 whole, which is shorter than its diff:
```python
import functools
import jax
import jax.numpy as jnp
from jax import lax
from jax.experimental import pallas as pl
from jax.experimental.pallas import tpu as pltpu
from jax.sharding import PartitionSpec as P

HEADS = 3
HD = 256
FF = 512
STEPS = 3

coef_a = 3.4445
coef_b = -4.775
coef_c = 2.0315
eta_rate = 3.0
eps_small = 1e-06

FP = jnp.float32
BF = jnp.bfloat16
NT = (((1,), (1,)), ((), ()))
TN = (((0,), (0,)), ((), ()))
ROWS = 3 * FF


def mm(a, b, dims=(((1,), (0,)), ((), ()))):
    return lax.dot_general(a, b, dims, preferred_element_type=FP)


def unit(raw):
    return raw * lax.rsqrt(jnp.sum(raw * raw, -1, keepdims=True) + eps_small)


def add_gradient(tok, head, w_k, w_v, w_rate, fast, acc):
    rows = tok[...]
    keys = unit(mm(rows, w_k[...])).astype(BF)
    rates = mm(rows, w_rate[...], NT)
    pick = lax.broadcasted_iota(jnp.int32, rates.shape, 1) == head
    rate = jnp.sum(jnp.where(pick, rates, 0.0), -1, keepdims=True)
    rate = jnp.maximum(rate, 0.0) + jnp.log1p(jnp.exp(-jnp.abs(rate)))
    scaled = (rate * mm(rows, w_v[...])).astype(BF)
    gate_pre = mm(fast[0], keys, NT)
    up_pre = mm(fast[1], keys, NT)
    back = mm(fast[2], scaled, NT)
    sig = jax.nn.sigmoid(gate_pre)
    act = gate_pre * sig
    hidden = (act * up_pre).astype(BF)
    d_gate = (back * up_pre * sig * (1.0 + gate_pre * (1.0 - sig))).astype(BF)
    d_up = (back * act).astype(BF)
    acc[0:FF] += mm(d_gate, keys)
    acc[FF : 2 * FF] += mm(d_up, keys)
    acc[2 * FF : ROWS] += mm(hidden, scaled)


def first_kernel(n_tok, where, *refs):
    toks, (w_k, w_v, w_rate, fast, acc) = refs[:n_tok], refs[n_tok:]
    acc[...] = jnp.zeros_like(acc)
    for tok in toks:
        add_gradient(tok, where[0], w_k, w_v, w_rate, fast, acc)


def second_kernel(n_tok, n_patch, where, *refs):
    toks, (w_k, w_v, w_rate, fast, begun) = refs[:n_tok], refs[n_tok : n_tok + 5]
    outs, acc = refs[n_tok + 5 : -1], refs[-1]
    acc[...] = begun[...]
    for tok in toks:
        add_gradient(tok, where[0], w_k, w_v, w_rate, fast, acc)
    size = ROWS // n_patch
    for shift, out in enumerate(outs):
        chunk = lax.rem(where[1] + shift, n_patch)
        out[...] = acc[pl.ds(pl.multiple_of(chunk * size, size), size)].astype(out.dtype)


def decode_kernel(n_patch, where, *refs):
    parts, (fast, gain, qry, out, grads, fresh) = refs[:n_patch], refs[n_patch:]
    size = ROWS // n_patch
    for shift, part in enumerate(parts):
        chunk = lax.rem(where[1] + n_patch - shift, n_patch)
        grads[pl.ds(pl.multiple_of(chunk * size, size), size)] = part[...]
    ortho = []
    for kind in range(3):
        grad = grads[kind * FF : (kind + 1) * FF].astype(FP)
        total = jnp.sum(jnp.sum(grad * grad, -1, keepdims=True), 0, keepdims=True)
        ortho.append((grad / (jnp.sqrt(total) + eps_small)).astype(BF))
    for step in range(STEPS):
        gram = [mm(x, x, TN).astype(BF) for x in ortho]
        square = [mm(g, g) for g in gram]
        poly = [(coef_b * g.astype(FP) + coef_c * s).astype(BF) for g, s in zip(gram, square)]
        mixed = [mm(x, p) for x, p in zip(ortho, poly)]
        ortho = [(coef_a * x.astype(FP) + m).astype(BF) for x, m in zip(ortho, mixed)]
    for kind in range(3):
        old = fast[kind].astype(FP)
        moved = old + eta_rate * ortho[kind].astype(FP)
        old_norm = jnp.sqrt(jnp.sum(old * old, -1, keepdims=True))
        new_norm = jnp.sqrt(jnp.sum(moved * moved, -1, keepdims=True)) + eps_small
        fresh[kind] = (moved * (old_norm / new_norm)).astype(BF)
    block = HD
    for start in range(0, qry.shape[0], block):
        rows = qry[start : start + block]
        gate_pre = mm(rows, fresh[0], NT)
        up_pre = mm(rows, fresh[1], NT)
        hidden = (gate_pre * jax.nn.sigmoid(gate_pre) * up_pre).astype(BF)
        read = mm(hidden, fresh[2])
        normed = read * lax.rsqrt(jnp.mean(read * read, -1, keepdims=True) + eps_small)
        out[start : start + block] = (normed * gain[...].astype(FP)).astype(BF)


def whole(*shape):
    return pl.BlockSpec(shape, lambda i, where: (0,) * len(shape))


def call(kernel, where, args, specs, outs, scratch=()):
    return pl.pallas_call(
        kernel,
        out_shape=outs,
        grid_spec=pltpu.PrefetchScalarGridSpec(
            num_scalar_prefetch=1,
            grid=(1,),
            in_specs=specs,
            out_specs=jax.tree.map(lambda o: whole(*o.shape), outs),
            scratch_shapes=scratch,
        ),
        compiler_params=pltpu.CompilerParams(vmem_limit_bytes=40 << 20),
    )(where, *args)


def unit_heads(raw):
    return unit(raw.reshape(raw.shape[0], HEADS, HD))


def local(tokens, w_kv, w_rate, fast_weights, queries, w_query, out_gain, w_out):
    n_patch, n_view, n_head = (lax.axis_size(a) for a in ("patch", "view", "head"))
    patch, view, core = (lax.axis_index(a) for a in ("patch", "view", "head"))
    n_tok, width = tokens.shape
    n_qry = queries.shape[0]
    side = view % 2
    head = jnp.where(core == 1, 1, 2 * side).astype(jnp.int32)
    where = jnp.stack([head, patch.astype(jnp.int32)])
    swap = [(0, 1), (1, 0)]
    flip = [(i, i ^ 1) for i in range(n_view)]
    first = [(v * n_head, (v ^ 1) * n_head) for v in range(n_view)]

    def rotate(n, shift):
        return [(i, (i + shift) % n) for i in range(n)]

    far = [lax.ppermute(tokens, "view", rotate(n_view, s)) for s in range(1, n_view)]
    near = [tokens, lax.ppermute(tokens, "head", swap)]
    far = far + [lax.ppermute(f, "head", swap) for f in far]
    mine = lax.dynamic_index_in_dim(fast_weights, head, 2, keepdims=False).transpose(1, 0, 2)

    weights = [w_kv, w_kv, w_rate, mine]
    weight_specs = [
        pl.BlockSpec((width, HD), lambda i, where: (0, where[0])),
        pl.BlockSpec((width, HD), lambda i, where: (0, HEADS + where[0])),
        whole(HEADS, width),
        whole(3, FF, HD),
    ]
    begun = call(
        functools.partial(first_kernel, len(near)),
        where,
        near + weights,
        [whole(n_tok, width)] * len(near) + weight_specs,
        jax.ShapeDtypeStruct((ROWS, HD), FP),
    )
    size = ROWS // n_patch
    chunks = call(
        functools.partial(second_kernel, len(far), n_patch),
        where,
        far + weights + [begun],
        [whole(n_tok, width)] * len(far) + weight_specs + [whole(ROWS, HD)],
        [jax.ShapeDtypeStruct((size, HD), BF if s else FP) for s in range(n_patch)],
        [pltpu.VMEM((ROWS, HD), FP)],
    )
    order = sorted(range(1, n_patch), key=lambda s: -min(s, n_patch - s))
    got = {s: lax.ppermute(chunks[s], "patch", rotate(n_patch, s)) for s in order}
    own = chunks[0]
    for s in order:
        own = own + got[s].astype(FP)
    own = own.astype(BF)
    parts = {s: lax.ppermute(own, "patch", rotate(n_patch, s)) for s in order}

    qry = unit_heads(jnp.dot(queries, w_query, preferred_element_type=FP)).astype(BF)
    pair = jnp.where(side == 0, qry[:, 0], qry[:, 2])
    other = jnp.where(side == 0, qry[:, 2], qry[:, 0])
    out_first = jnp.where(core == 0, qry[:, 1], pair)
    own_qry = jnp.where(core == 0, pair, qry[:, 1])
    swapped = lax.ppermute(jnp.concatenate([out_first, other]), "head", swap)
    across = lax.ppermute(jnp.concatenate([other, swapped[n_qry:]]), ("view", "head"), first)
    all_qry = jnp.concatenate([own_qry, swapped[:n_qry], across])

    normed = call(
        functools.partial(decode_kernel, n_patch),
        where,
        [own] + [parts[s] for s in range(1, n_patch)] + [mine, out_gain.reshape(1, width), all_qry],
        [whole(size, HD)] * n_patch
        + [
            whole(3, FF, HD),
            pl.BlockSpec((1, HD), lambda i, where: (0, where[0])),
            whole(4 * n_qry, HD),
        ],
        jax.ShapeDtypeStruct((4 * n_qry, HD), BF),
        [pltpu.VMEM((ROWS, HD), BF), pltpu.VMEM((3, FF, HD), BF)],
    )
    back = lax.ppermute(normed[2 * n_qry :], ("view", "head"), first)
    sib = lax.ppermute(normed[n_qry : 2 * n_qry], "head", swap)
    relayed = lax.ppermute(back[n_qry:], "head", swap)
    own_out = normed[:n_qry]
    one = jnp.where(core == 0, sib, own_out)
    same = jnp.where(core == 0, own_out, sib)
    cross = jnp.where(core == 0, back[:n_qry], relayed)
    zero = jnp.where(side == 0, same, cross)
    two = jnp.where(side == 0, cross, same)
    joined = jnp.concatenate([zero, one, two], 1)
    return jnp.dot(joined, w_out, preferred_element_type=FP).astype(BF)


def solution(mesh):
    split = P(("groups", "patch", "view", "head"), None)
    in_specs = (split, P(), P(), P(), split, P(), P(), P())
    return jax.shard_map(local, mesh=mesh, in_specs=in_specs, out_specs=split, check_vma=False)
```

time: 500 us -> 78.4 us (0.16)
  blocking collectives: 245 us -> 0 us
  waiting for transfers between devices: 178 us -> 28.5 us
  matrix products: 41.6 us -> 4.1 us
  starting transfers between devices: 0.08 us -> 23.5 us
  between operations: 13.3 us -> 0.25 us
  Pallas kernels: 0 us -> 11.7 us
    psum x4 -> x0, blocking collectives: 245 us -> none  [the longest x3 238 us: local(): ortho = newton(begin, lambda part: lax.psum(part, 'patch'))]
    reduce_scatter x1 -> x0, waiting for transfers between devices: 86.6 us -> none  [local(): lax.psum_scatter(grad_term(keys, scaled, fast_weights), 'patch', scatter_...]
    all_gather x1 -> x0, waiting for transfers between devices: 54.1 us -> none  [local(): piece = lax.all_gather(fresh, 'patch', axis=0, tiled=True)]
    psum x1 -> x0, waiting for transfers between devices: 37.8 us -> none  [local(): shard = lax.psum(scattered, ('view', 'head'))]
    dot_general x18 -> x2, matrix products: 41.6 us -> 4.1 us  [the longest x1 2.87 us: local(): jnp.dot(queries, w_query, preferred_element_type=FP)]
    ppermute x0 -> x14, waiting for transfers between devices: none -> 28.5 us  [the longest x3 16 us: local(): parts = {s: lax.ppermute(own, 'patch', rotate(n_patch, s)) for s in order}]
    ppermute x0 -> x14, starting transfers between devices: none -> 23.5 us  [the longest x1 5.8 us: local(): relayed = lax.ppermute(back[n_qry:], 'head', swap)]
    pallas_call x0 -> x3, Pallas kernels: none -> 11.7 us  [call(): pl.pallas_call(kernel, out_shape=outs, grid_spec=pltpu.PrefetchScalarGrid...]
  transfers between devices with their start and end apart: 3 -> 14, of which waited for: 3 -> 7; matrix products, arithmetic and copies ran while one was open for 1% -> 13% of each run, Pallas kernels for 0% -> 8%
where the time goes in v1:
time: 78.4 us; the launch traced here: 78 us
  waiting for transfers between devices  28.5 us (36%)
  starting transfers between devices  23.5 us (30%)
  Pallas kernels  11.7 us (15%)
  local copies, waits for them, and re-layouts  5.76 us (7%)
  other arithmetic  4.18 us (5%)
  matrix products  4.1 us (5%)
    ppermute x3, waiting for transfers between devices, local(): parts = {s: lax.ppermute(own, 'patch', rotate(n_patch, s)) for s in order}  16 us
    pallas_call x3, Pallas kernels, call(): pl.pallas_call(kernel, out_shape=outs, grid_spec=pltpu.PrefetchScalarGrid...  11.7 us
    ppermute x3, waiting for transfers between devices, local(): lax.ppermute(chunks[s], 'patch', rotate(n_patch, s))  10.2 us
    ppermute x1, starting transfers between devices, local(): relayed = lax.ppermute(back[n_qry:], 'head', swap)  5.8 us
    ppermute x3, starting transfers between devices, local(): lax.ppermute(chunks[s], 'patch', rotate(n_patch, s))  5.62 us
    ppermute x3, starting transfers between devices, local(): parts = {s: lax.ppermute(own, 'patch', rotate(n_patch, s)) for s in order}  4.62 us
    ppermute x1, starting transfers between devices, local(): sib = lax.ppermute(normed[n_qry:2 * n_qry], 'head', swap)  3.21 us
    dot_general x1, matrix products, local(): jnp.dot(queries, w_query, preferred_element_type=FP)  2.87 us
  transfers between devices with their start and end apart: 14, of which 7 were waited for; matrix products, arithmetic and copies ran while one was open for 13% of the time, Pallas kernels for 8%

profile of v1, /device:TPU:11, one launch (start us, length us, event | category | flops | bytes accessed | tf_op | source)
XLA Modules:
  0.0 78.0 jit_solution(6460583818573545362)
XLA Ops:
  0.0 0.3 collective-permute-start
  0.3 1.0 %collective-permute-start.2 = (bf16[256,768]{1,0:T(8,128)(2,1)}, bf16[256,768]{1,0:T(8,128)(2,1)S(1)}, u32[]{:S(2)}, u32[]{:S(2)}) collective-permute-start(bf16[256,768]{1,0:T(8,128)(2,1)} %refs_0_.1), channel_id=1, source_target_pairs={{0,1},{1,0},{2,3},{3,2},{4,5},{5,4},{6,7},{7,6},{8,9},{9,8},{10,11... | collective-permute-start | bytes 1179656 | tf_op jit(solution)/shard_map/ppermute | solution.py:148
  1.2 2.9 %fusion.7 = f32[256,768]{0,1:T(8,128)} fusion(bf16[256,768]{1,0:T(8,128)(2,1)} %param.12, bf16[768,768]{1,0:T(8,128)(2,1)} %param.13), kind=kOutput, calls=%fused_computation.26 | convolution fusion | flops 301989888 | bytes 2359296 | tf_op jit(solution)/shard_map/dot_general | solution.py:183
  4.1 2.3 %copy.10 = f32[256,3,256]{2,0,1:T(8,128)} copy(f32[256,3,256]{0,2,1:T(8,128)} %bitcast.16) | data formatting | bytes 1572864 | tf_op jit(solution)/shard_map/reshape | solution.py:129
  6.4 1.2 %multiply_reduce_fusion = f32[256,3]{0,1:T(4,128)S(1)} fusion(f32[256,3,256]{0,2,1:T(8,128)} %bitcast.17), kind=kLoop, calls=%fused_computation.2 | loop fusion | flops 392448 | bytes 789504 | tf_op jit(solution)/shard_map/reduce_sum | solution.py:32
  7.7 1.3 %multiply_convert_fusion = bf16[256,3,256]{2,0,1:T(8,128)(2,1)S(1)} fusion(f32[256,3,256]{2,0,1:T(8,128)} %copy.10, f32[256,3]{0,1:T(4,128)S(1)} %add_rsqrt_fusion), kind=kLoop, calls=%fused_computation.1 | loop fusion | flops 393216 | bytes 1182720 | tf_op jit(solution)/shard_map/convert_element_type | solution.py:183
  9.0 1.2 %collective-permute-done.refs_0_ = bf16[256,768]{1,0:T(8,128)(2,1)S(1)} collective-permute-done((bf16[256,768]{1,0:T(8,128)(2,1)}, bf16[256,768]{1,0:T(8,128)(2,1)S(1)}, u32[]{:S(2)}, u32[]{:S(2)}) %collective-permute-start) | collective-permute-done | bytes 393248 | tf_op jit(solution)/shard_map/ppermute | solution.py:147
  10.2 1.5 %collective-permute-start.1 = (bf16[256,768]{1,0:T(8,128)(2,1)S(1)}, bf16[256,768]{1,0:T(8,128)(2,1)}, u32[]{:S(2)}, u32[]{:S(2)}) collective-permute-start(bf16[256,768]{1,0:T(8,128)(2,1)S(1)} %collective-permute-done.refs_0_), channel_id=1, source_target_pairs={{0,1},{1,0},{2,3},{3,2},{4,5},{5,4},{6,7},{7,6},{8,9},{9,8},{10,11... | collective-permute-start | bytes 1179656 | tf_op jit(solution)/shard_map/ppermute | solution.py:149
  11.7 0.7 select_bitcast_fusion.2
  12.4 0.7 copy-done.5
  13.1 0.7 pad_maximum_fusion.1
  13.8 0.0 collective-permute-start.9
  13.8 0.1 pad_add_fusion.where
  13.9 0.1 dynamic-slice_bitcast_fusion.refs_5_.refs_4_
  13.9 0.0 collective-permute-done.2.refs_1_
  13.9 0.0 copy-done.3
  14.0 0.0 copy-start.1
  14.0 1.7 %copy-done.1 = bf16[768,1536]{1,0:T(8,128)(2,1)S(1)} copy-done((bf16[768,1536]{1,0:T(8,128)(2,1)S(1)}, bf16[768,1536]{1,0:T(8,128)(2,1)}, u32[]{:S(2)}) %copy-start.1) | copy-done | bytes 2359320
  15.6 2.7 %shard_map.82.refs_6_ = f32[1536,256]{1,0:T(8,128)S(1)} custom-call(s32[2]{0:T(128)S(1)} %pad_add_fusion.where, bf16[256,768]{1,0:T(8,128)(2,1)S(1)} %copy-done.3, bf16[256,768]{1,0:T(8,128)(2,1)S(1)} %collective-permute-done.2.refs_1_, bf16[768,1536]{1,0:T(8,128)(2,1)S(1)} %copy-done.1, bf16[768,1536]{1,0:T(8,128)(2,1)S(1)} %copy-done.1, ...), custom_call_target="tpu_custom_call" | custom-call | tf_op jit(solution)/shard_map/pallas_call | solution.py:114
  18.3 0.0 collective-permute-done.1.refs_1_
  18.3 3.9 %shard_map.83 = (f32[384,256]{1,0:T(8,128)S(1)}, bf16[384,256]{1,0:T(8,128)(2,1)S(1)}, bf16[384,256]{1,0:T(8,128)(2,1)S(1)}, bf16[384,256]{1,0:T(8,128)(2,1)S(1)}) custom-call(s32[2]{0:T(128)S(1)} %pad_add_fusion.where, bf16[256,768]{1,0:T(8,128)(2,1)S(1)} %collective-permute-done.refs_0_, bf16[256,768]{1,0:T(8,128)(2,1)} %collective-permute-done.1.refs_1_, ...), custom_call_target="tpu_custom_call" | custom-call | tf_op jit(solution)/shard_map/pallas_call | solution.py:114
  22.2 0.0 copy-start.8
  22.2 0.2 collective-permute-start.5
  22.4 1.3 %collective-permute-start.4 = (bf16[384,256]{1,0:T(8,128)(2,1)S(1)}, bf16[384,256]{1,0:T(8,128)(2,1)S(1)}, u32[]{:S(2)}, u32[]{:S(2)}) collective-permute-start(bf16[384,256]{1,0:T(8,128)(2,1)S(1)} %get-tuple-element.11), channel_id=1, source_target_pairs={{0,4},{4,8},{8,12},{12,0},{1,5},{5,9},{9,13},{13,1},{2,6},{6,10},{... | collective-permute-start | bytes 589832 | tf_op jit(solution)/shard_map/ppermute | solution.py:176
  23.7 4.1 %collective-permute-start.3 = (bf16[384,256]{1,0:T(8,128)(2,1)S(1)}, bf16[384,256]{1,0:T(8,128)(2,1)S(1)}, u32[]{:S(2)}, u32[]{:S(2)}) collective-permute-start(bf16[384,256]{1,0:T(8,128)(2,1)S(1)} %get-tuple-element.10), channel_id=1, source_target_pairs={{0,8},{4,12},{8,0},{12,4},{1,9},{5,13},{9,1},{13,5},{2,10},{6,14},... | collective-permute-start | bytes 589832 | tf_op jit(solution)/shard_map/ppermute | solution.py:176
  27.8 0.0 collective-permute-done.9
  27.9 1.0 %fusion.6 = (bf16[256,256]{1,0:T(8,128)(2,1)S(1)}, bf16[256,256]{1,0:T(8,128)(2,1)S(1)}) fusion(bf16[512,256]{1,0:T(8,128)(2,1)} %collective-permute-done.9), kind=kLoop, calls=%fused_computation.25 | loop fusion | bytes 524288 | tf_op jit(solution)/shard_map/slice | solution.py:190
  28.9 0.7 collective-permute-start.10
  29.6 0.0 collective-permute-done.5
  29.6 4.9 %collective-permute-done.4 = bf16[384,256]{1,0:T(8,128)(2,1)S(1)} collective-permute-done((bf16[384,256]{1,0:T(8,128)(2,1)S(1)}, bf16[384,256]{1,0:T(8,128)(2,1)S(1)}, u32[]{:S(2)}, u32[]{:S(2)}) %collective-permute-start.4) | collective-permute-done | bytes 196640 | tf_op jit(solution)/shard_map/ppermute | solution.py:176
  34.5 5.3 %collective-permute-done.3 = bf16[384,256]{1,0:T(8,128)(2,1)S(1)} collective-permute-done((bf16[384,256]{1,0:T(8,128)(2,1)S(1)}, bf16[384,256]{1,0:T(8,128)(2,1)S(1)}, u32[]{:S(2)}, u32[]{:S(2)}) %collective-permute-start.3) | collective-permute-done | bytes 196640 | tf_op jit(solution)/shard_map/ppermute | solution.py:176
  39.8 0.1 add_convert_fusion.refs_0_
  39.9 0.4 collective-permute-start.6
  40.3 4.0 %collective-permute-start.7 = (bf16[384,256]{1,0:T(8,128)(2,1)S(1)}, bf16[384,256]{1,0:T(8,128)(2,1)S(1)}, u32[]{:S(2)}, u32[]{:S(2)}) collective-permute-start(bf16[384,256]{1,0:T(8,128)(2,1)S(1)} %add_convert_fusion.refs_0_), channel_id=1, source_target_pairs={{0,8},{4,12},{8,0},{12,4},{1,9},{5,13},{9,1},{13,5},{2,10},{6,14},... | collective-permute-start | bytes 589832 | tf_op jit(solution)/shard_map/ppermute | solution.py:181
  44.3 0.2 collective-permute-start.8
  44.5 0.0 collective-permute-done.10
  44.6 1.4 %collective-permute-done.6.refs_1_ = bf16[384,256]{1,0:T(8,128)(2,1)S(1)} collective-permute-done((bf16[384,256]{1,0:T(8,128)(2,1)S(1)}, bf16[384,256]{1,0:T(8,128)(2,1)S(1)}, u32[]{:S(2)}, u32[]{:S(2)}) %collective-permute-start.6) | collective-permute-done | bytes 196640 | tf_op jit(solution)/shard_map/ppermute | solution.py:181
  46.0 11.3 %collective-permute-done.7.refs_2_ = bf16[384,256]{1,0:T(8,128)(2,1)S(1)} collective-permute-done((bf16[384,256]{1,0:T(8,128)(2,1)S(1)}, bf16[384,256]{1,0:T(8,128)(2,1)S(1)}, u32[]{:S(2)}, u32[]{:S(2)}) %collective-permute-start.7) | collective-permute-done | bytes 196640 | tf_op jit(solution)/shard_map/ppermute | solution.py:181
  57.3 3.4 %collective-permute-done.8.refs_3_ = bf16[384,256]{1,0:T(8,128)(2,1)S(1)} collective-permute-done((bf16[384,256]{1,0:T(8,128)(2,1)S(1)}, bf16[384,256]{1,0:T(8,128)(2,1)S(1)}, u32[]{:S(2)}, u32[]{:S(2)}) %collective-permute-start.8) | collective-permute-done | bytes 196640 | tf_op jit(solution)/shard_map/ppermute | solution.py:181
  60.6 5.2 %shard_map.84 = bf16[1024,256]{1,0:T(8,128)(2,1)S(1)} custom-call(s32[2]{0:T(128)S(1)} %pad_add_fusion.where, bf16[384,256]{1,0:T(8,128)(2,1)S(1)} %add_convert_fusion.refs_0_, bf16[384,256]{1,0:T(8,128)(2,1)S(1)} %collective-permute-done.6.refs_1_, bf16[384,256]{1,0:T(8,128)(2,1)S(1)} %collective-permute-done.7.refs_2_, ...), custom_call_target="tpu_custom_call" | custom-call | tf_op jit(solution)/shard_map/pallas_call | solution.py:114
  65.8 0.0 copy-start.9
  65.9 0.8 %collective-permute-start.12 = (bf16[512,256]{1,0:T(8,128)(2,1)S(1)}, bf16[512,256]{1,0:T(8,128)(2,1)S(1)}, u32[]{:S(2)}, u32[]{:S(2)}) collective-permute-start(bf16[512,256]{1,0:T(8,128)(2,1)S(1)} %slice.50), channel_id=1, source_target_pairs={{0,2},{2,0},{4,6},{6,4},{8,10},{10,8},{12,14},{14,12},{16,18},{18,... | collective-permute-start | bytes 786440 | tf_op jit(solution)/shard_map/ppermute | solution.py:205
  66.7 3.2 %collective-permute-start.11 = (bf16[256,256]{1,0:T(8,128)(2,1)S(1)}, bf16[256,256]{1,0:T(8,128)(2,1)S(1)}, u32[]{:S(2)}, u32[]{:S(2)}) collective-permute-start(bf16[256,256]{1,0:T(8,128)(2,1)S(1)} %slice.49), channel_id=1, source_target_pairs={{0,1},{1,0},{2,3},{3,2},{4,5},{5,4},{6,7},{7,6},{8,9},{9,8},{10,11... | collective-permute-start | bytes 393224 | tf_op jit(solution)/shard_map/ppermute | solution.py:206
  69.9 0.0 collective-permute-done.12
  69.9 5.8 %collective-permute-start.13 = (bf16[256,256]{1,0:T(8,128)(2,1)S(1)}, bf16[256,256]{1,0:T(8,128)(2,1)S(1)}, u32[]{:S(2)}, u32[]{:S(2)}) collective-permute-start(bf16[256,256]{1,0:T(8,128)(2,1)S(1)} %slice.52), channel_id=1, source_target_pairs={{0,1},{1,0},{2,3},{3,2},{4,5},{5,4},{6,7},{7,6},{8,9},{9,8},{10,11... | collective-permute-start | bytes 393224 | tf_op jit(solution)/shard_map/ppermute | solution.py:207
  75.7 0.0 collective-permute-done.11
  75.7 1.0 %collective-permute-done.13 = bf16[256,256]{1,0:T(8,128)(2,1)S(1)} collective-permute-done((bf16[256,256]{1,0:T(8,128)(2,1)S(1)}, bf16[256,256]{1,0:T(8,128)(2,1)S(1)}, u32[]{:S(2)}, u32[]{:S(2)}) %collective-permute-start.13) | collective-permute-done | bytes 131104 | tf_op jit(solution)/shard_map/ppermute | solution.py:207
  76.8 1.2 %convolution_convert_fusion = bf16[256,768]{1,0:T(8,128)(2,1)} fusion(bf16[768,768]{1,0:T(8,128)(2,1)S(1)} %copy-done.9, bf16[256,256]{1,0:T(8,128)(2,1)S(1)} %get-tuple-element.14, bf16[256,256]{1,0:T(8,128)(2,1)S(1)} %get-tuple-element.15, bf16[256,256]{1,0:T(8,128)(2,1)S(1)} %get-tuple-element.13), kind=kOutput, calls=%fused_computation | convolution fusion | flops 303366144 | bytes 1966080 | tf_op jit(solution)/shard_map/dot_general | solution.py:215
  (22 shorter events, 0.2 us)
Async XLA Ops:
  0.0 13.9 %copy-start = (bf16[512,3,3,256]{3,0,2,1:T(8,128)(2,1)S(1)}, bf16[512,3,3,256]{3,0,2,1:T(8,128)(2,1)}, u32[]{:S(2)}) copy-start(bf16[512,3,3,256]{3,0,2,1:T(8,128)(2,1)} %param.11) | copy-start | bytes 7077892
  0.0 10.2 %collective-permute-start = (bf16[256,768]{1,0:T(8,128)(2,1)}, bf16[256,768]{1,0:T(8,128)(2,1)S(1)}, u32[]{:S(2)}, u32[]{:S(2)}) collective-permute-start(bf16[256,768]{1,0:T(8,128)(2,1)} %refs_0_.1), channel_id=1, source_target_pairs={{0,2},{2,0},{1,3},{3,1},{4,6},{6,4},{5,7},{7,5},{8,10},{10,8},{9,1... | collective-permute-start | bytes 1179656 | tf_op jit(solution)/shard_map/ppermute | solution.py:147
  0.3 13.7 %collective-permute-start.2 = (bf16[256,768]{1,0:T(8,128)(2,1)}, bf16[256,768]{1,0:T(8,128)(2,1)S(1)}, u32[]{:S(2)}, u32[]{:S(2)}) collective-permute-start(bf16[256,768]{1,0:T(8,128)(2,1)} %refs_0_.1), channel_id=1, source_target_pairs={{0,1},{1,0},{2,3},{3,2},{4,5},{5,4},{6,7},{7,6},{8,9},{9,8},{10,11... | collective-permute-start | bytes 1179656 | tf_op jit(solution)/shard_map/ppermute | solution.py:148
  10.2 8.1 %collective-permute-start.1 = (bf16[256,768]{1,0:T(8,128)(2,1)S(1)}, bf16[256,768]{1,0:T(8,128)(2,1)}, u32[]{:S(2)}, u32[]{:S(2)}) collective-permute-start(bf16[256,768]{1,0:T(8,128)(2,1)S(1)} %collective-permute-done.refs_0_), channel_id=1, source_target_pairs={{0,1},{1,0},{2,3},{3,2},{4,5},{5,4},{6,7},{7,6},{8,9},{9,8},{10,11... | collective-permute-start | bytes 1179656 | tf_op jit(solution)/shard_map/ppermute | solution.py:149
  12.4 0.7 copy-start.5
  12.4 1.5 %copy-start.3 = (bf16[256,768]{1,0:T(8,128)(2,1)S(1)}, bf16[256,768]{1,0:T(8,128)(2,1)}, u32[]{:S(2)}) copy-start(bf16[256,768]{1,0:T(8,128)(2,1)} %refs_0_.1) | copy-start | bytes 1179652
  12.4 1.5 %copy-start.4 = (bf16[3,768]{1,0:T(4,128)(2,1)S(1)}, bf16[3,768]{1,0:T(4,128)(2,1)}, u32[]{:S(2)}) copy-start(bf16[3,768]{1,0:T(4,128)(2,1)} %refs_4_.3) | copy-start | bytes 13828
  13.8 14.1 %collective-permute-start.9 = (bf16[512,256]{1,0:T(8,128)(2,1)}, bf16[512,256]{1,0:T(8,128)(2,1)}, u32[]{:S(2)}, u32[]{:S(2)}) collective-permute-start(bf16[512,256]{1,0:T(8,128)(2,1)} %pad_maximum_fusion.1), channel_id=1, source_target_pairs={{0,1},{1,0},{2,3},{3,2},{4,5},{5,4},{6,7},{7,6},{8,9},{9,8},{10,11... | collective-permute-start | bytes 786440 | tf_op jit(solution)/shard_map/ppermute | solution.py:188
  14.0 1.7 %copy-start.1 = (bf16[768,1536]{1,0:T(8,128)(2,1)S(1)}, bf16[768,1536]{1,0:T(8,128)(2,1)}, u32[]{:S(2)}) copy-start(bf16[768,1536]{1,0:T(8,128)(2,1)} %refs_3_.3) | copy-start | bytes 7077892
  15.6 2.7 %copy-start.2 = (bf16[768,1536]{1,0:T(8,128)(2,1)S(1)}, bf16[768,1536]{1,0:T(8,128)(2,1)}, u32[]{:S(2)}) copy-start(bf16[768,1536]{1,0:T(8,128)(2,1)} %refs_3_.3) | copy-start | bytes 7077892
  18.3 10.5 %copy-start.6 = (bf16[256,256]{1,0:T(8,128)(2,1)S(1)}, bf16[256,256]{1,0:T(8,128)(2,1)}, u32[]{:S(2)}) copy-start(bf16[256,256]{1,0:T(8,128)(2,1)} %copy-done.5) | copy-start | bytes 393220
  22.2 22.3 %copy-start.8 = (bf16[768]{0:T(1024)(128)(2,1)S(1)}, bf16[768]{0:T(1024)(128)(2,1)}, u32[]{:S(2)}) copy-start(bf16[768]{0:T(1024)(128)(2,1)} %param.14) | copy-start | bytes 4612
  22.2 22.3 %copy-start.7 = (bf16[256,256]{1,0:T(8,128)(2,1)S(1)}, bf16[256,256]{1,0:T(8,128)(2,1)}, u32[]{:S(2)}) copy-start(bf16[256,256]{1,0:T(8,128)(2,1)} %get-tuple-element.16) | copy-start | bytes 393220
  22.2 7.3 %collective-permute-start.5 = (bf16[384,256]{1,0:T(8,128)(2,1)S(1)}, bf16[384,256]{1,0:T(8,128)(2,1)S(1)}, u32[]{:S(2)}, u32[]{:S(2)}) collective-permute-start(bf16[384,256]{1,0:T(8,128)(2,1)S(1)} %get-tuple-element.12), channel_id=1, source_target_pairs={{0,12},{4,0},{8,4},{12,8},{1,13},{5,1},{9,5},{13,9},{2,14},{6,2},{... | collective-permute-start | bytes 589832 | tf_op jit(solution)/shard_map/ppermute | solution.py:176
  22.4 12.1 %collective-permute-start.4 = (bf16[384,256]{1,0:T(8,128)(2,1)S(1)}, bf16[384,256]{1,0:T(8,128)(2,1)S(1)}, u32[]{:S(2)}, u32[]{:S(2)}) collective-permute-start(bf16[384,256]{1,0:T(8,128)(2,1)S(1)} %get-tuple-element.11), channel_id=1, source_target_pairs={{0,4},{4,8},{8,12},{12,0},{1,5},{5,9},{9,13},{13,1},{2,6},{6,10},{... | collective-permute-start | bytes 589832 | tf_op jit(solution)/shard_map/ppermute | solution.py:176
  23.7 16.1 %collective-permute-start.3 = (bf16[384,256]{1,0:T(8,128)(2,1)S(1)}, bf16[384,256]{1,0:T(8,128)(2,1)S(1)}, u32[]{:S(2)}, u32[]{:S(2)}) collective-permute-start(bf16[384,256]{1,0:T(8,128)(2,1)S(1)} %get-tuple-element.10), channel_id=1, source_target_pairs={{0,8},{4,12},{8,0},{12,4},{1,9},{5,13},{9,1},{13,5},{2,10},{6,14},... | collective-permute-start | bytes 589832 | tf_op jit(solution)/shard_map/ppermute | solution.py:176
  28.9 15.7 %collective-permute-start.10 = (bf16[512,256]{1,0:T(8,128)(2,1)S(1)}, bf16[512,256]{1,0:T(8,128)(2,1)S(1)}, u32[]{:S(2)}, u32[]{:S(2)}) collective-permute-start(bf16[512,256]{1,0:T(8,128)(2,1)S(1)} %pad_maximum_fusion.2), channel_id=1, source_target_pairs={{0,2},{2,0},{4,6},{6,4},{8,10},{10,8},{12,14},{14,12},{16,18},{18,... | collective-permute-start | bytes 786440 | tf_op jit(solution)/shard_map/ppermute | solution.py:189
  39.9 6.1 %collective-permute-start.6 = (bf16[384,256]{1,0:T(8,128)(2,1)S(1)}, bf16[384,256]{1,0:T(8,128)(2,1)S(1)}, u32[]{:S(2)}, u32[]{:S(2)}) collective-permute-start(bf16[384,256]{1,0:T(8,128)(2,1)S(1)} %add_convert_fusion.refs_0_), channel_id=1, source_target_pairs={{0,4},{4,8},{8,12},{12,0},{1,5},{5,9},{9,13},{13,1},{2,6},{6,10},{... | collective-permute-start | bytes 589832 | tf_op jit(solution)/shard_map/ppermute | solution.py:181
  40.3 17.0 %collective-permute-start.7 = (bf16[384,256]{1,0:T(8,128)(2,1)S(1)}, bf16[384,256]{1,0:T(8,128)(2,1)S(1)}, u32[]{:S(2)}, u32[]{:S(2)}) collective-permute-start(bf16[384,256]{1,0:T(8,128)(2,1)S(1)} %add_convert_fusion.refs_0_), channel_id=1, source_target_pairs={{0,8},{4,12},{8,0},{12,4},{1,9},{5,13},{9,1},{13,5},{2,10},{6,14},... | collective-permute-start | bytes 589832 | tf_op jit(solution)/shard_map/ppermute | solution.py:181
  44.3 16.3 %collective-permute-start.8 = (bf16[384,256]{1,0:T(8,128)(2,1)S(1)}, bf16[384,256]{1,0:T(8,128)(2,1)S(1)}, u32[]{:S(2)}, u32[]{:S(2)}) collective-permute-start(bf16[384,256]{1,0:T(8,128)(2,1)S(1)} %add_convert_fusion.refs_0_), channel_id=1, source_target_pairs={{0,12},{4,0},{8,4},{12,8},{1,13},{5,1},{9,5},{13,9},{2,14},{6,2},{... | collective-permute-start | bytes 589832 | tf_op jit(solution)/shard_map/ppermute | solution.py:181
  65.8 10.9 %copy-start.9 = (bf16[768,768]{1,0:T(8,128)(2,1)S(1)}, bf16[768,768]{1,0:T(8,128)(2,1)}, u32[]{:S(2)}) copy-start(bf16[768,768]{1,0:T(8,128)(2,1)} %param.15) | copy-start | bytes 3538948
  65.9 4.0 %collective-permute-start.12 = (bf16[512,256]{1,0:T(8,128)(2,1)S(1)}, bf16[512,256]{1,0:T(8,128)(2,1)S(1)}, u32[]{:S(2)}, u32[]{:S(2)}) collective-permute-start(bf16[512,256]{1,0:T(8,128)(2,1)S(1)} %slice.50), channel_id=1, source_target_pairs={{0,2},{2,0},{4,6},{6,4},{8,10},{10,8},{12,14},{14,12},{16,18},{18,... | collective-permute-start | bytes 786440 | tf_op jit(solution)/shard_map/ppermute | solution.py:205
  66.7 9.0 %collective-permute-start.11 = (bf16[256,256]{1,0:T(8,128)(2,1)S(1)}, bf16[256,256]{1,0:T(8,128)(2,1)S(1)}, u32[]{:S(2)}, u32[]{:S(2)}) collective-permute-start(bf16[256,256]{1,0:T(8,128)(2,1)S(1)} %slice.49), channel_id=1, source_target_pairs={{0,1},{1,0},{2,3},{3,2},{4,5},{5,4},{6,7},{7,6},{8,9},{9,8},{10,11... | collective-permute-start | bytes 393224 | tf_op jit(solution)/shard_map/ppermute | solution.py:206
  69.9 6.8 %collective-permute-start.13 = (bf16[256,256]{1,0:T(8,128)(2,1)S(1)}, bf16[256,256]{1,0:T(8,128)(2,1)S(1)}, u32[]{:S(2)}, u32[]{:S(2)}) collective-permute-start(bf16[256,256]{1,0:T(8,128)(2,1)S(1)} %slice.52), channel_id=1, source_target_pairs={{0,1},{1,0},{2,3},{3,2},{4,5},{5,4},{6,7},{7,6},{8,9},{9,8},{10,11... | collective-permute-start | bytes 393224 | tf_op jit(solution)/shard_map/ppermute | solution.py:207

commit v2 on v1

--- a/solution.py
+++ b/solution.py
@@ -73,7 +73,7 @@
 
 
 def decode_kernel(n_patch, where, *refs):
-    parts, (fast, gain, qry, out, grads, fresh) = refs[:n_patch], refs[n_patch:]
+    parts, (fast, gain, *queries, out, grads, fresh) = refs[:n_patch], refs[n_patch:]
     size = ROWS // n_patch
     for shift, part in enumerate(parts):
         chunk = lax.rem(where[1] + n_patch - shift, n_patch)
@@ -95,15 +95,28 @@
         old_norm = jnp.sqrt(jnp.sum(old * old, -1, keepdims=True))
         new_norm = jnp.sqrt(jnp.sum(moved * moved, -1, keepdims=True)) + eps_small
         fresh[kind] = (moved * (old_norm / new_norm)).astype(BF)
-    block = HD
-    for start in range(0, qry.shape[0], block):
-        rows = qry[start : start + block]
-        gate_pre = mm(rows, fresh[0], NT)
-        up_pre = mm(rows, fresh[1], NT)
-        hidden = (gate_pre * jax.nn.sigmoid(gate_pre) * up_pre).astype(BF)
-        read = mm(hidden, fresh[2])
-        normed = read * lax.rsqrt(jnp.mean(read * read, -1, keepdims=True) + eps_small)
-        out[start : start + block] = (normed * gain[...].astype(FP)).astype(BF)
+    start = 0
+    for qry in queries:
+        for row in range(0, qry.shape[0], HD):
+            rows = qry[row : row + HD]
+            gate_pre = mm(rows, fresh[0], NT)
+            up_pre = mm(rows, fresh[1], NT)
+            hidden = (gate_pre * jax.nn.sigmoid(gate_pre) * up_pre).astype(BF)
+            read = mm(hidden, fresh[2])
+            normed = read * lax.rsqrt(jnp.mean(read * read, -1, keepdims=True) + eps_small)
+            out[start : start + HD] = (normed * gain[...].astype(FP)).astype(BF)
+            start += HD
+
+
+def query_kernel(where, queries, w_query, own, message, other, heads):
+    rows = mm(queries[...], w_query[...])
+    for head in range(HEADS):
+        heads[head] = unit(rows[:, head * HD : (head + 1) * HD]).astype(BF)
+    n_qry = own.shape[0]
+    own[...] = heads[where[0]]
+    message[:n_qry] = heads[where[2]]
+    message[n_qry:] = heads[where[3]]
+    other[...] = heads[where[3]]
 
 
 def whole(*shape):
@@ -125,18 +138,15 @@
     )(where, *args)
 
 
-def unit_heads(raw):
-    return unit(raw.reshape(raw.shape[0], HEADS, HD))
-
-
 def local(tokens, w_kv, w_rate, fast_weights, queries, w_query, out_gain, w_out):
     n_patch, n_view, n_head = (lax.axis_size(a) for a in ("patch", "view", "head"))
     patch, view, core = (lax.axis_index(a) for a in ("patch", "view", "head"))
     n_tok, width = tokens.shape
     n_qry = queries.shape[0]
     side = view % 2
-    head = jnp.where(core == 1, 1, 2 * side).astype(jnp.int32)
-    where = jnp.stack([head, patch.astype(jnp.int32)])
+    head = jnp.where(core == 1, 1, 2 * side)
+    sibling = jnp.where(core == 1, 2 * side, 1)
+    where = jnp.stack([head, patch, sibling, 2 - 2 * side]).astype(jnp.int32)
     swap = [(0, 1), (1, 0)]
     flip = [(i, i ^ 1) for i in range(n_view)]
     first = [(v * n_head, (v ^ 1) * n_head) for v in range(n_view)]
@@ -146,13 +156,15 @@
 
     far = [lax.ppermute(tokens, "view", rotate(n_view, s)) for s in range(1, n_view)]
     near = [tokens, lax.ppermute(tokens, "head", swap)]
-    far = far + [lax.ppermute(f, "head", swap) for f in far]
     mine = lax.dynamic_index_in_dim(fast_weights, head, 2, keepdims=False).transpose(1, 0, 2)
 
-    weights = [w_kv, w_kv, w_rate, mine]
+    w_k = lax.dynamic_slice_in_dim(w_kv, head * HD, HD, 1)
+    w_v = lax.dynamic_slice_in_dim(w_kv, width + head * HD, HD, 1)
+
+    weights = [w_k, w_v, w_rate, mine]
     weight_specs = [
-        pl.BlockSpec((width, HD), lambda i, where: (0, where[0])),
-        pl.BlockSpec((width, HD), lambda i, where: (0, HEADS + where[0])),
+        whole(width, HD),
+        whole(width, HD),
         whole(HEADS, width),
         whole(3, FF, HD),
     ]
@@ -163,6 +175,8 @@
         [whole(n_tok, width)] * len(near) + weight_specs,
         jax.ShapeDtypeStruct((ROWS, HD), FP),
     )
+    begun, *far = lax.optimization_barrier((begun, *far))
+    far = far + [lax.ppermute(f, "head", swap) for f in far]
     size = ROWS // n_patch
     chunks = call(
         functools.partial(second_kernel, len(far), n_patch),
@@ -180,24 +194,30 @@
     own = own.astype(BF)
     parts = {s: lax.ppermute(own, "patch", rotate(n_patch, s)) for s in order}
 
-    qry = unit_heads(jnp.dot(queries, w_query, preferred_element_type=FP)).astype(BF)
-    pair = jnp.where(side == 0, qry[:, 0], qry[:, 2])
-    other = jnp.where(side == 0, qry[:, 2], qry[:, 0])
-    out_first = jnp.where(core == 0, qry[:, 1], pair)
-    own_qry = jnp.where(core == 0, pair, qry[:, 1])
-    swapped = lax.ppermute(jnp.concatenate([out_first, other]), "head", swap)
+    late, _ = lax.optimization_barrier((queries, chunks[0]))
+    own_qry, message, other = call(
+        query_kernel,
+        where,
+        [late, w_query],
+        [whole(n_qry, width), whole(width, width)],
+        [jax.ShapeDtypeStruct((n, HD), BF) for n in (n_qry, 2 * n_qry, n_qry)],
+        [pltpu.VMEM((HEADS, n_qry, HD), BF)],
+    )
+    swapped = lax.ppermute(message, "head", swap)
     across = lax.ppermute(jnp.concatenate([other, swapped[n_qry:]]), ("view", "head"), first)
-    all_qry = jnp.concatenate([own_qry, swapped[:n_qry], across])
 
     normed = call(
         functools.partial(decode_kernel, n_patch),
         where,
-        [own] + [parts[s] for s in range(1, n_patch)] + [mine, out_gain.reshape(1, width), all_qry],
+        [own] + [parts[s] for s in range(1, n_patch)]
+        + [mine, out_gain.reshape(1, width), own_qry, swapped, across],
         [whole(size, HD)] * n_patch
         + [
             whole(3, FF, HD),
             pl.BlockSpec((1, HD), lambda i, where: (0, where[0])),
-            whole(4 * n_qry, HD),
+            whole(n_qry, HD),
+            whole(n_qry, HD),
+            whole(2 * n_qry, HD),
         ],
         jax.ShapeDtypeStruct((4 * n_qry, HD), BF),
         [pltpu.VMEM((ROWS, HD), BF), pltpu.VMEM((3, FF, HD), BF)],

time: 78.4 us -> 77 us (0.982)
  waiting for transfers between devices: 28.5 us -> 38.5 us
  local copies, waits for them, and re-layouts: 5.76 us -> 2.01 us
  starting transfers between devices: 23.5 us -> 19.8 us
  other arithmetic: 4.18 us -> 1.13 us
  matrix products: 4.1 us -> 2.5 us
    ppermute x3, waiting for transfers between devices: 10.2 us -> 15 us  [local(): lax.ppermute(chunks[s], 'patch', rotate(n_patch, s))]
    ppermute x1, waiting for transfers between devices: 1.24 us -> 5.88 us  [local(): lax.ppermute(tokens, 'view', rotate(n_view, s))]
    dot_general x1 -> x0, matrix products: 2.87 us -> none  [local(): jnp.dot(queries, w_query, preferred_element_type=FP)]
    reshape x1 -> x0, local copies, waits for them, and re-layouts: 2.33 us -> none  [unit_heads(): return unit(raw.reshape(raw.shape[0], HEADS, HD))]
    ppermute x3, starting transfers between devices: 5.62 us -> 3.78 us  [local(): lax.ppermute(chunks[s], 'patch', rotate(n_patch, s))]
    unnamed x20 -> x12, local copies, waits for them, and re-layouts: 2.35 us -> 0.68 us
    ppermute x1, waiting for transfers between devices: 0.01 us -> 1.35 us  [local(): far = far + [lax.ppermute(f, 'head', swap) for f in far]]
    convert_element_type x1 -> x0, other arithmetic: 1.3 us -> none  [local(): unit_heads(jnp.dot(queries, w_query, preferred_element_type=FP)).astype(BF)]
  transfers between devices with their start and end apart: 14 -> 14, of which waited for: 7 -> 7; matrix products, arithmetic and copies ran while one was open for 13% -> 2% of each run, Pallas kernels for 8% -> 4%
where the time goes in v2:
time: 77 us; the launch traced here: 76 us
  waiting for transfers between devices  38.5 us (50%)
  starting transfers between devices  19.8 us (26%)
  Pallas kernels  11.9 us (15%)
  matrix products  2.5 us (3%)
  local copies, waits for them, and re-layouts  2.01 us (3%)
  other arithmetic  1.13 us (1%)
    ppermute x3, waiting for transfers between devices, local(): parts = {s: lax.ppermute(own, 'patch', rotate(n_patch, s)) for s in order}  15.2 us
    ppermute x3, waiting for transfers between devices, local(): lax.ppermute(chunks[s], 'patch', rotate(n_patch, s))  15 us
    pallas_call x4, Pallas kernels, call(): pl.pallas_call(kernel, out_shape=outs, grid_spec=pltpu.PrefetchScalarGrid...  11.9 us
    ppermute x1, waiting for transfers between devices, local(): lax.ppermute(tokens, 'view', rotate(n_view, s))  5.88 us
    ppermute x1, starting transfers between devices, local(): relayed = lax.ppermute(back[n_qry:], 'head', swap)  5.79 us
    ppermute x3, starting transfers between devices, local(): lax.ppermute(chunks[s], 'patch', rotate(n_patch, s))  3.78 us
    ppermute x3, starting transfers between devices, local(): parts = {s: lax.ppermute(own, 'patch', rotate(n_patch, s)) for s in order}  3.51 us
    ppermute x1, starting transfers between devices, local(): sib = lax.ppermute(normed[n_qry:2 * n_qry], 'head', swap)  3.13 us
  transfers between devices with their start and end apart: 14, of which 7 were waited for; matrix products, arithmetic and copies ran while one was open for 2% of the time, Pallas kernels for 4%

profile of v2, /device:TPU:11, one launch (start us, length us, event | category | flops | bytes accessed | tf_op | source)
XLA Modules:
  0.0 76.0 jit_solution(13583824993955055171)
XLA Ops:
  0.0 0.0 copy-start
  0.0 0.7 collective-permute-start
  0.7 0.3 collective-permute-start.1
  0.9 0.1 pad_add_fusion.where
  1.0 0.7 copy-done
  1.7 0.1 dynamic-slice_bitcast_fusion.refs_5_.refs_4_
  1.7 1.2 %constant_dynamic-slice_fusion = (bf16[768,256]{1,0:T(8,128)(2,1)S(1)}, bf16[768,256]{1,0:T(8,128)(2,1)S(1)}) fusion(bf16[768,1536]{1,0:T(8,128)(2,1)} %param.9, s32[]{:T(128)S(6)} %select_n.57, s32[]{:T(128)S(6)} %select_n.56), kind=kLoop, calls=%fused_computation.14 | loop fusion | bytes 1572872 | tf_op jit(solution)/shard_map/dynamic_slice | solution.py:162
  2.9 0.0 collective-permute-done.refs_1_
  3.0 0.0 copy-done.2
  3.0 0.0 copy-done.4
  3.0 2.7 %shard_map.82.refs_6_ = f32[1536,256]{1,0:T(8,128)S(1)} custom-call(s32[4]{0:T(128)S(1)} %pad_add_fusion.where, bf16[256,768]{1,0:T(8,128)(2,1)S(1)} %copy-done.2, bf16[256,768]{1,0:T(8,128)(2,1)S(1)} %collective-permute-done.refs_1_, bf16[768,256]{1,0:T(8,128)(2,1)S(1)} %get-tuple-element.26.refs_2_, bf16[768,256]{1,0:T(8,128)(2,1)S(1)} %get-tuple-element.25.refs_3_, ...), custom_call_target="tpu_custom_call" | custom-call | tf_op jit(solution)/shard_map/pallas_call | solution.py:127
  5.7 0.0 copy-start.1
  5.7 0.0 copy-start.3
  5.7 5.9 %collective-permute-done.1.refs_0_ = bf16[256,768]{1,0:T(8,128)(2,1)S(1)} collective-permute-done((bf16[256,768]{1,0:T(8,128)(2,1)}, bf16[256,768]{1,0:T(8,128)(2,1)S(1)}, u32[]{:S(2)}, u32[]{:S(2)}) %collective-permute-start.1) | collective-permute-done | bytes 393248 | tf_op jit(solution)/shard_map/ppermute | solution.py:157
  11.6 0.9 %collective-permute-start.2 = (bf16[256,768]{1,0:T(8,128)(2,1)S(1)}, bf16[256,768]{1,0:T(8,128)(2,1)S(1)}, u32[]{:S(2)}, u32[]{:S(2)}) collective-permute-start(bf16[256,768]{1,0:T(8,128)(2,1)S(1)} %collective-permute-done.1.refs_0_), channel_id=1, source_target_pairs={{0,1},{1,0},{2,3},{3,2},{4,5},{5,4},{6,7},{7,6},{8,9},{9,8},{10,11... | collective-permute-start | bytes 1179656 | tf_op jit(solution)/shard_map/ppermute | solution.py:179
  12.4 1.3 %collective-permute-done.2.refs_1_ = bf16[256,768]{1,0:T(8,128)(2,1)S(1)} collective-permute-done((bf16[256,768]{1,0:T(8,128)(2,1)S(1)}, bf16[256,768]{1,0:T(8,128)(2,1)S(1)}, u32[]{:S(2)}, u32[]{:S(2)}) %collective-permute-start.2) | collective-permute-done | bytes 393248 | tf_op jit(solution)/shard_map/ppermute | solution.py:179
  13.8 2.9 %shard_map.83 = (f32[384,256]{1,0:T(8,128)S(1)}, bf16[384,256]{1,0:T(8,128)(2,1)S(1)}, bf16[384,256]{1,0:T(8,128)(2,1)S(1)}, bf16[384,256]{1,0:T(8,128)(2,1)S(1)}) custom-call(s32[4]{0:T(128)S(1)} %pad_add_fusion.where, bf16[256,768]{1,0:T(8,128)(2,1)S(1)} %collective-permute-done.1.refs_0_, bf16[256,768]{1,0:T(8,128)(2,1)S(1)} %collective-permute-done.2.refs_1_, ...), custom_call_target="tpu_custom_call" | custom-call | tf_op jit(solution)/shard_map/pallas_call | solution.py:127
  16.6 0.0 copy-done.1
  16.7 0.0 copy-done.3
  16.7 0.0 copy-start.5
  16.7 1.1 %shard_map.84 = (bf16[256,256]{1,0:T(8,128)(2,1)S(1)}, bf16[512,256]{1,0:T(8,128)(2,1)S(1)}, bf16[256,256]{1,0:T(8,128)(2,1)S(1)}) custom-call(s32[4]{0:T(128)S(1)} %pad_add_fusion.where, bf16[256,768]{1,0:T(8,128)(2,1)S(1)} %copy-done.3, bf16[768,768]{1,0:T(8,128)(2,1)S(1)} %copy-done.1), custom_call_target="tpu_custom_call" | custom-call | tf_op jit(solution)/shard_map/pallas_call | solution.py:127
  17.8 0.4 collective-permute-start.9
  18.3 2.3 %collective-permute-start.3 = (bf16[384,256]{1,0:T(8,128)(2,1)S(1)}, bf16[384,256]{1,0:T(8,128)(2,1)S(1)}, u32[]{:S(2)}, u32[]{:S(2)}) collective-permute-start(bf16[384,256]{1,0:T(8,128)(2,1)S(1)} %get-tuple-element.18), channel_id=1, source_target_pairs={{0,8},{4,12},{8,0},{12,4},{1,9},{5,13},{9,1},{13,5},{2,10},{6,14},... | collective-permute-start | bytes 589832 | tf_op jit(solution)/shard_map/ppermute | solution.py:190
  20.6 0.0 collective-permute-start.4
  20.6 1.5 %collective-permute-start.5 = (bf16[384,256]{1,0:T(8,128)(2,1)S(1)}, bf16[384,256]{1,0:T(8,128)(2,1)S(1)}, u32[]{:S(2)}, u32[]{:S(2)}) collective-permute-start(bf16[384,256]{1,0:T(8,128)(2,1)S(1)} %get-tuple-element.20), channel_id=1, source_target_pairs={{0,12},{4,0},{8,4},{12,8},{1,13},{5,1},{9,5},{13,9},{2,14},{6,2},{... | collective-permute-start | bytes 589832 | tf_op jit(solution)/shard_map/ppermute | solution.py:190
  22.0 0.0 collective-permute-done.9.refs_7_
  22.1 0.7 collective-permute-start.10
  22.8 6.5 %collective-permute-done.3 = bf16[384,256]{1,0:T(8,128)(2,1)S(1)} collective-permute-done((bf16[384,256]{1,0:T(8,128)(2,1)S(1)}, bf16[384,256]{1,0:T(8,128)(2,1)S(1)}, u32[]{:S(2)}, u32[]{:S(2)}) %collective-permute-start.3) | collective-permute-done | bytes 196640 | tf_op jit(solution)/shard_map/ppermute | solution.py:190
  29.3 8.5 %collective-permute-done.4 = bf16[384,256]{1,0:T(8,128)(2,1)S(1)} collective-permute-done((bf16[384,256]{1,0:T(8,128)(2,1)S(1)}, bf16[384,256]{1,0:T(8,128)(2,1)S(1)}, u32[]{:S(2)}, u32[]{:S(2)}) %collective-permute-start.4) | collective-permute-done | bytes 196640 | tf_op jit(solution)/shard_map/ppermute | solution.py:190
  37.8 0.0 collective-permute-done.5
  37.8 0.1 add_convert_fusion.refs_0_
  37.9 2.3 %collective-permute-start.6 = (bf16[384,256]{1,0:T(8,128)(2,1)S(1)}, bf16[384,256]{1,0:T(8,128)(2,1)S(1)}, u32[]{:S(2)}, u32[]{:S(2)}) collective-permute-start(bf16[384,256]{1,0:T(8,128)(2,1)S(1)} %add_convert_fusion.refs_0_), channel_id=1, source_target_pairs={{0,4},{4,8},{8,12},{12,0},{1,5},{5,9},{9,13},{13,1},{2,6},{6,10},{... | collective-permute-start | bytes 589832 | tf_op jit(solution)/shard_map/ppermute | solution.py:195
  40.1 0.0 collective-permute-start.7
  40.1 1.3 %collective-permute-start.8 = (bf16[384,256]{1,0:T(8,128)(2,1)S(1)}, bf16[384,256]{1,0:T(8,128)(2,1)S(1)}, u32[]{:S(2)}, u32[]{:S(2)}) collective-permute-start(bf16[384,256]{1,0:T(8,128)(2,1)S(1)} %add_convert_fusion.refs_0_), channel_id=1, source_target_pairs={{0,12},{4,0},{8,4},{12,8},{1,13},{5,1},{9,5},{13,9},{2,14},{6,2},{... | collective-permute-start | bytes 589832 | tf_op jit(solution)/shard_map/ppermute | solution.py:195
  41.4 0.0 copy-done.5
  41.4 3.1 %collective-permute-done.6.refs_1_ = bf16[384,256]{1,0:T(8,128)(2,1)S(1)} collective-permute-done((bf16[384,256]{1,0:T(8,128)(2,1)S(1)}, bf16[384,256]{1,0:T(8,128)(2,1)S(1)}, u32[]{:S(2)}, u32[]{:S(2)}) %collective-permute-start.6) | collective-permute-done | bytes 196640 | tf_op jit(solution)/shard_map/ppermute | solution.py:195
  44.5 12.1 %collective-permute-done.7.refs_2_ = bf16[384,256]{1,0:T(8,128)(2,1)S(1)} collective-permute-done((bf16[384,256]{1,0:T(8,128)(2,1)S(1)}, bf16[384,256]{1,0:T(8,128)(2,1)S(1)}, u32[]{:S(2)}, u32[]{:S(2)}) %collective-permute-start.7) | collective-permute-done | bytes 196640 | tf_op jit(solution)/shard_map/ppermute | solution.py:195
  56.6 0.0 collective-permute-done.8.refs_3_
  56.6 0.0 collective-permute-done.10.refs_8_
  56.6 5.2 %shard_map.85 = bf16[1024,256]{1,0:T(8,128)(2,1)S(1)} custom-call(s32[4]{0:T(128)S(1)} %pad_add_fusion.where, bf16[384,256]{1,0:T(8,128)(2,1)S(1)} %add_convert_fusion.refs_0_, bf16[384,256]{1,0:T(8,128)(2,1)S(1)} %collective-permute-done.6.refs_1_, bf16[384,256]{1,0:T(8,128)(2,1)S(1)} %collective-permute-done.7.refs_2_, ...), custom_call_target="tpu_custom_call" | custom-call | tf_op jit(solution)/shard_map/pallas_call | solution.py:127
  61.8 0.7 collective-permute-start.12
  62.5 3.1 %collective-permute-start.11 = (bf16[256,256]{1,0:T(8,128)(2,1)S(1)}, bf16[256,256]{1,0:T(8,128)(2,1)S(1)}, u32[]{:S(2)}, u32[]{:S(2)}) collective-permute-start(bf16[256,256]{1,0:T(8,128)(2,1)S(1)} %slice.26), channel_id=1, source_target_pairs={{0,1},{1,0},{2,3},{3,2},{4,5},{5,4},{6,7},{7,6},{8,9},{9,8},{10,11... | collective-permute-start | bytes 393224 | tf_op jit(solution)/shard_map/ppermute | solution.py:226
  65.6 0.0 collective-permute-done.12
  65.7 5.8 %collective-permute-start.13 = (bf16[256,256]{1,0:T(8,128)(2,1)S(1)}, bf16[256,256]{1,0:T(8,128)(2,1)}, u32[]{:S(2)}, u32[]{:S(2)}) collective-permute-start(bf16[256,256]{1,0:T(8,128)(2,1)S(1)} %slice.29), channel_id=1, source_target_pairs={{0,1},{1,0},{2,3},{3,2},{4,5},{5,4},{6,7},{7,6},{8,9},{9,8},{10,11... | collective-permute-start | bytes 393224 | tf_op jit(solution)/shard_map/ppermute | solution.py:227
  71.5 0.0 collective-permute-done.11
  71.5 1.1 %collective-permute-done.13 = bf16[256,256]{1,0:T(8,128)(2,1)} collective-permute-done((bf16[256,256]{1,0:T(8,128)(2,1)S(1)}, bf16[256,256]{1,0:T(8,128)(2,1)}, u32[]{:S(2)}, u32[]{:S(2)}) %collective-permute-start.13) | collective-permute-done | bytes 131104 | tf_op jit(solution)/shard_map/ppermute | solution.py:227
  72.6 0.9 %broadcast_select_fusion.3 = (bf16[256,256]{1,0:T(8,128)(2,1)S(1)}, bf16[256,256]{1,0:T(8,128)(2,1)S(1)}, bf16[256,256]{1,0:T(8,128)(2,1)S(1)}) fusion(pred[]{:T(512)S(6)} %eq.8, bf16[256,256]{1,0:T(8,128)(2,1)S(1)} %collective-permute-done.11, bf16[1024,256]{1,0:T(8,128)(2,1)S(1)} %shard_map.85, pred[]{:T(512)S(6)} %eq.16, ...), kind=kLoop, calls=%fused_computation.13 | loop fusion | flops 327680 | bytes 917506 | tf_op jit(solution)/shard_map/jit(_where)/select_n | solution.py:232
  73.5 2.5 %convolution_convert_fusion = bf16[256,768]{1,0:T(8,128)(2,1)} fusion(bf16[768,768]{1,0:T(8,128)(2,1)} %param.15, bf16[256,256]{1,0:T(8,128)(2,1)S(1)} %get-tuple-element.28, bf16[256,256]{1,0:T(8,128)(2,1)S(1)} %get-tuple-element.29, bf16[256,256]{1,0:T(8,128)(2,1)S(1)} %get-tuple-element.27), kind=kOutput, calls=%fused_computation | convolution fusion | flops 303366144 | bytes 1966080 | tf_op jit(solution)/shard_map/dot_general | solution.py:235
  (8 shorter events, 0.1 us)
Async XLA Ops:
  0.0 1.7 %copy-start = (bf16[512,3,3,256]{3,0,2,1:T(8,128)(2,1)S(1)}, bf16[512,3,3,256]{3,0,2,1:T(8,128)(2,1)}, u32[]{:S(2)}) copy-start(bf16[512,3,3,256]{3,0,2,1:T(8,128)(2,1)} %param.11) | copy-start | bytes 7077892
  0.0 2.9 %collective-permute-start = (bf16[256,768]{1,0:T(8,128)(2,1)}, bf16[256,768]{1,0:T(8,128)(2,1)S(1)}, u32[]{:S(2)}, u32[]{:S(2)}) collective-permute-start(bf16[256,768]{1,0:T(8,128)(2,1)} %refs_0_.1), channel_id=1, source_target_pairs={{0,1},{1,0},{2,3},{3,2},{4,5},{5,4},{6,7},{7,6},{8,9},{9,8},{10,11... | collective-permute-start | bytes 1179656 | tf_op jit(solution)/shard_map/ppermute | solution.py:158
  0.7 10.9 %collective-permute-start.1 = (bf16[256,768]{1,0:T(8,128)(2,1)}, bf16[256,768]{1,0:T(8,128)(2,1)S(1)}, u32[]{:S(2)}, u32[]{:S(2)}) collective-permute-start(bf16[256,768]{1,0:T(8,128)(2,1)} %refs_0_.1), channel_id=1, source_target_pairs={{0,2},{2,0},{1,3},{3,1},{4,6},{6,4},{5,7},{7,5},{8,10},{10,8},{9,1... | collective-permute-start | bytes 1179656 | tf_op jit(solution)/shard_map/ppermute | solution.py:157
  1.7 1.3 %copy-start.2 = (bf16[256,768]{1,0:T(8,128)(2,1)S(1)}, bf16[256,768]{1,0:T(8,128)(2,1)}, u32[]{:S(2)}) copy-start(bf16[256,768]{1,0:T(8,128)(2,1)} %refs_0_.1) | copy-start | bytes 1179652
  1.7 1.3 %copy-start.4 = (bf16[3,768]{1,0:T(4,128)(2,1)S(1)}, bf16[3,768]{1,0:T(4,128)(2,1)}, u32[]{:S(2)}) copy-start(bf16[3,768]{1,0:T(4,128)(2,1)} %refs_4_.3) | copy-start | bytes 13828
  5.7 11.0 %copy-start.1 = (bf16[768,768]{1,0:T(8,128)(2,1)S(1)}, bf16[768,768]{1,0:T(8,128)(2,1)}, u32[]{:S(2)}) copy-start(bf16[768,768]{1,0:T(8,128)(2,1)} %w_query.1) | copy-start | bytes 3538948
  5.7 11.0 %copy-start.3 = (bf16[256,768]{1,0:T(8,128)(2,1)S(1)}, bf16[256,768]{1,0:T(8,128)(2,1)}, u32[]{:S(2)}) copy-start(bf16[256,768]{1,0:T(8,128)(2,1)} %queries) | copy-start | bytes 1179652
  11.6 2.2 %collective-permute-start.2 = (bf16[256,768]{1,0:T(8,128)(2,1)S(1)}, bf16[256,768]{1,0:T(8,128)(2,1)S(1)}, u32[]{:S(2)}, u32[]{:S(2)}) collective-permute-start(bf16[256,768]{1,0:T(8,128)(2,1)S(1)} %collective-permute-done.1.refs_0_), channel_id=1, source_target_pairs={{0,1},{1,0},{2,3},{3,2},{4,5},{5,4},{6,7},{7,6},{8,9},{9,8},{10,11... | collective-permute-start | bytes 1179656 | tf_op jit(solution)/shard_map/ppermute | solution.py:179
  16.7 24.7 %copy-start.5 = (bf16[768]{0:T(1024)(128)(2,1)S(1)}, bf16[768]{0:T(1024)(128)(2,1)}, u32[]{:S(2)}) copy-start(bf16[768]{0:T(1024)(128)(2,1)} %param.14) | copy-start | bytes 4612
  17.8 4.2 %collective-permute-start.9 = (bf16[512,256]{1,0:T(8,128)(2,1)S(1)}, bf16[512,256]{1,0:T(8,128)(2,1)S(1)}, u32[]{:S(2)}, u32[]{:S(2)}) collective-permute-start(bf16[512,256]{1,0:T(8,128)(2,1)S(1)} %get-tuple-element.23), channel_id=1, source_target_pairs={{0,1},{1,0},{2,3},{3,2},{4,5},{5,4},{6,7},{7,6},{8,9},{9,8},{10,11... | collective-permute-start | bytes 786440 | tf_op jit(solution)/shard_map/ppermute | solution.py:206
  18.3 11.0 %collective-permute-start.3 = (bf16[384,256]{1,0:T(8,128)(2,1)S(1)}, bf16[384,256]{1,0:T(8,128)(2,1)S(1)}, u32[]{:S(2)}, u32[]{:S(2)}) collective-permute-start(bf16[384,256]{1,0:T(8,128)(2,1)S(1)} %get-tuple-element.18), channel_id=1, source_target_pairs={{0,8},{4,12},{8,0},{12,4},{1,9},{5,13},{9,1},{13,5},{2,10},{6,14},... | collective-permute-start | bytes 589832 | tf_op jit(solution)/shard_map/ppermute | solution.py:190
  20.6 17.2 %collective-permute-start.4 = (bf16[384,256]{1,0:T(8,128)(2,1)S(1)}, bf16[384,256]{1,0:T(8,128)(2,1)S(1)}, u32[]{:S(2)}, u32[]{:S(2)}) collective-permute-start(bf16[384,256]{1,0:T(8,128)(2,1)S(1)} %get-tuple-element.19), channel_id=1, source_target_pairs={{0,4},{4,8},{8,12},{12,0},{1,5},{5,9},{9,13},{13,1},{2,6},{6,10},{... | collective-permute-start | bytes 589832 | tf_op jit(solution)/shard_map/ppermute | solution.py:190
  20.6 17.2 %collective-permute-start.5 = (bf16[384,256]{1,0:T(8,128)(2,1)S(1)}, bf16[384,256]{1,0:T(8,128)(2,1)S(1)}, u32[]{:S(2)}, u32[]{:S(2)}) collective-permute-start(bf16[384,256]{1,0:T(8,128)(2,1)S(1)} %get-tuple-element.20), channel_id=1, source_target_pairs={{0,12},{4,0},{8,4},{12,8},{1,13},{5,1},{9,5},{13,9},{2,14},{6,2},{... | collective-permute-start | bytes 589832 | tf_op jit(solution)/shard_map/ppermute | solution.py:190
  22.1 34.5 %collective-permute-start.10 = (bf16[512,256]{1,0:T(8,128)(2,1)S(1)}, bf16[512,256]{1,0:T(8,128)(2,1)S(1)}, u32[]{:S(2)}, u32[]{:S(2)}) collective-permute-start(bf16[512,256]{1,0:T(8,128)(2,1)S(1)} %pad_maximum_fusion), channel_id=1, source_target_pairs={{0,2},{2,0},{4,6},{6,4},{8,10},{10,8},{12,14},{14,12},{16,18},{18,... | collective-permute-start | bytes 786440 | tf_op jit(solution)/shard_map/ppermute | solution.py:207
  37.9 6.6 %collective-permute-start.6 = (bf16[384,256]{1,0:T(8,128)(2,1)S(1)}, bf16[384,256]{1,0:T(8,128)(2,1)S(1)}, u32[]{:S(2)}, u32[]{:S(2)}) collective-permute-start(bf16[384,256]{1,0:T(8,128)(2,1)S(1)} %add_convert_fusion.refs_0_), channel_id=1, source_target_pairs={{0,4},{4,8},{8,12},{12,0},{1,5},{5,9},{9,13},{13,1},{2,6},{6,10},{... | collective-permute-start | bytes 589832 | tf_op jit(solution)/shard_map/ppermute | solution.py:195
  40.1 16.5 %collective-permute-start.7 = (bf16[384,256]{1,0:T(8,128)(2,1)S(1)}, bf16[384,256]{1,0:T(8,128)(2,1)S(1)}, u32[]{:S(2)}, u32[]{:S(2)}) collective-permute-start(bf16[384,256]{1,0:T(8,128)(2,1)S(1)} %add_convert_fusion.refs_0_), channel_id=1, source_target_pairs={{0,8},{4,12},{8,0},{12,4},{1,9},{5,13},{9,1},{13,5},{2,10},{6,14},... | collective-permute-start | bytes 589832 | tf_op jit(solution)/shard_map/ppermute | solution.py:195
  40.1 16.5 %collective-permute-start.8 = (bf16[384,256]{1,0:T(8,128)(2,1)S(1)}, bf16[384,256]{1,0:T(8,128)(2,1)S(1)}, u32[]{:S(2)}, u32[]{:S(2)}) collective-permute-start(bf16[384,256]{1,0:T(8,128)(2,1)S(1)} %add_convert_fusion.refs_0_), channel_id=1, source_target_pairs={{0,12},{4,0},{8,4},{12,8},{1,13},{5,1},{9,5},{13,9},{2,14},{6,2},{... | collective-permute-start | bytes 589832 | tf_op jit(solution)/shard_map/ppermute | solution.py:195
  61.8 3.8 %collective-permute-start.12 = (bf16[512,256]{1,0:T(8,128)(2,1)S(1)}, bf16[512,256]{1,0:T(8,128)(2,1)S(1)}, u32[]{:S(2)}, u32[]{:S(2)}) collective-permute-start(bf16[512,256]{1,0:T(8,128)(2,1)S(1)} %slice.27), channel_id=1, source_target_pairs={{0,2},{2,0},{4,6},{6,4},{8,10},{10,8},{12,14},{14,12},{16,18},{18,... | collective-permute-start | bytes 786440 | tf_op jit(solution)/shard_map/ppermute | solution.py:225
  62.5 8.9 %collective-permute-start.11 = (bf16[256,256]{1,0:T(8,128)(2,1)S(1)}, bf16[256,256]{1,0:T(8,128)(2,1)S(1)}, u32[]{:S(2)}, u32[]{:S(2)}) collective-permute-start(bf16[256,256]{1,0:T(8,128)(2,1)S(1)} %slice.26), channel_id=1, source_target_pairs={{0,1},{1,0},{2,3},{3,2},{4,5},{5,4},{6,7},{7,6},{8,9},{9,8},{10,11... | collective-permute-start | bytes 393224 | tf_op jit(solution)/shard_map/ppermute | solution.py:226
  65.7 6.9 %collective-permute-start.13 = (bf16[256,256]{1,0:T(8,128)(2,1)S(1)}, bf16[256,256]{1,0:T(8,128)(2,1)}, u32[]{:S(2)}, u32[]{:S(2)}) collective-permute-start(bf16[256,256]{1,0:T(8,128)(2,1)S(1)} %slice.29), channel_id=1, source_target_pairs={{0,1},{1,0},{2,3},{3,2},{4,5},{5,4},{6,7},{7,6},{8,9},{9,8},{10,11... | collective-permute-start | bytes 393224 | tf_op jit(solution)/shard_map/ppermute | solution.py:227

commit v3 on v2

v3 whole, which is shorter than its diff:
```python
import functools
import jax
import jax.numpy as jnp
from jax import lax
from jax.experimental import pallas as pl
from jax.experimental.pallas import tpu as pltpu
from jax.sharding import PartitionSpec as P

HEADS = 3
HD = 256
FF = 512
STEPS = 3

coef_a = 3.4445
coef_b = -4.775
coef_c = 2.0315
eta_rate = 3.0
eps_small = 1e-06

FP = jnp.float32
BF = jnp.bfloat16
NT = (((1,), (1,)), ((), ()))
TN = (((0,), (0,)), ((), ()))
ROWS = 3 * FF


def mm(a, b, dims=(((1,), (0,)), ((), ()))):
    return lax.dot_general(a, b, dims, preferred_element_type=FP)


def unit(raw):
    return raw * lax.rsqrt(jnp.sum(raw * raw, -1, keepdims=True) + eps_small)


def peer(index, shift):
    return index ^ shift


def add_gradient(tok, head, w_k, w_v, w_rate, fast, acc):
    rows = tok[...]
    keys = unit(mm(rows, w_k[...])).astype(BF)
    rates = mm(rows, w_rate[...], NT)
    pick = lax.broadcasted_iota(jnp.int32, rates.shape, 1) == head
    rate = jnp.sum(jnp.where(pick, rates, 0.0), -1, keepdims=True)
    rate = jnp.maximum(rate, 0.0) + jnp.log1p(jnp.exp(-jnp.abs(rate)))
    scaled = (rate * mm(rows, w_v[...])).astype(BF)
    gate_pre = mm(fast[0], keys, NT)
    up_pre = mm(fast[1], keys, NT)
    back = mm(fast[2], scaled, NT)
    sig = jax.nn.sigmoid(gate_pre)
    act = gate_pre * sig
    hidden = (act * up_pre).astype(BF)
    d_gate = (back * up_pre * sig * (1.0 + gate_pre * (1.0 - sig))).astype(BF)
    d_up = (back * act).astype(BF)
    acc[0:FF] += mm(d_gate, keys)
    acc[FF : 2 * FF] += mm(d_up, keys)
    acc[2 * FF : ROWS] += mm(hidden, scaled)


def first_kernel(n_tok, where, *refs):
    toks, (w_k, w_v, w_rate, fast, acc) = refs[:n_tok], refs[n_tok:]
    acc[...] = jnp.zeros_like(acc)
    for tok in toks:
        add_gradient(tok, where[0], w_k, w_v, w_rate, fast, acc)


def second_kernel(n_tok, n_patch, where, *refs):
    toks, (w_k, w_v, w_rate, fast, begun) = refs[:n_tok], refs[n_tok : n_tok + 5]
    outs, acc = refs[n_tok + 5 : -1], refs[-1]
    acc[...] = begun[...]
    for tok in toks:
        add_gradient(tok, where[0], w_k, w_v, w_rate, fast, acc)
    size = ROWS // n_patch
    for shift, out in enumerate(outs):
        chunk = peer(where[1], shift)
        out[...] = acc[pl.ds(pl.multiple_of(chunk * size, size), size)].astype(out.dtype)


def decode(rows, fresh, gain):
    gate_pre = mm(rows, fresh[0], NT)
    up_pre = mm(rows, fresh[1], NT)
    hidden = (gate_pre * jax.nn.sigmoid(gate_pre) * up_pre).astype(BF)
    read = mm(hidden, fresh[2])
    return (read * lax.rsqrt(jnp.mean(read * read, -1, keepdims=True) + eps_small) * gain).astype(BF)


def own_gain(gains, head):
    low, middle, high = (gains[:, i * HD : (i + 1) * HD] for i in range(HEADS))
    return jnp.where(head == 0, low, jnp.where(head == 1, middle, high)).astype(FP)


def near_kernel(where, own, other, fresh, gains, w_out, for_other, begun):
    gain = own_gain(gains, where[0])
    for_other[...] = decode(other[...], fresh, gain)
    product = w_out[pl.ds(pl.multiple_of(where[0] * HD, HD), HD)]
    begun[...] = mm(decode(own[...], fresh, gain), product)


def far_kernel(n_patch, order, where, *refs):
    parts, (fast, gains, qry, out, fresh, grads) = refs[:n_patch], refs[n_patch:]
    size = ROWS // n_patch
    for shift, part in zip((0, *order), parts):
        chunk = peer(where[1], shift)
        grads[pl.ds(pl.multiple_of(chunk * size, size), size)] = part[...]
    ortho = []
    for kind in range(3):
        grad = grads[kind * FF : (kind + 1) * FF].astype(FP)
        total = jnp.sum(jnp.sum(grad * grad, -1, keepdims=True), 0, keepdims=True)
        ortho.append((grad / (jnp.sqrt(total) + eps_small)).astype(BF))
    for step in range(STEPS):
        gram = [mm(x, x, TN).astype(BF) for x in ortho]
        square = [mm(g, g) for g in gram]
        poly = [(coef_b * g.astype(FP) + coef_c * s).astype(BF) for g, s in zip(gram, square)]
        mixed = [mm(x, p) for x, p in zip(ortho, poly)]
        ortho = [(coef_a * x.astype(FP) + m).astype(BF) for x, m in zip(ortho, mixed)]
    for kind in range(3):
        old = fast[kind].astype(FP)
        moved = old + eta_rate * ortho[kind].astype(FP)
        old_norm = jnp.sqrt(jnp.sum(old * old, -1, keepdims=True))
        new_norm = jnp.sqrt(jnp.sum(moved * moved, -1, keepdims=True)) + eps_small
        fresh[kind] = (moved * (old_norm / new_norm)).astype(BF)
    gain = own_gain(gains, where[0])
    for row in range(0, qry.shape[0], HD):
        out[row : row + HD] = decode(qry[row : row + HD], fresh, gain)


def query_kernel(where, queries, w_query, own, message, other, heads):
    rows = mm(queries[...], w_query[...])
    for head in range(HEADS):
        heads[head] = unit(rows[:, head * HD : (head + 1) * HD]).astype(BF)
    n_qry = own.shape[0]
    own[...] = heads[where[0]]
    message[:n_qry] = heads[where[2]]
    message[n_qry:] = heads[where[3]]
    other[...] = heads[where[4]]


def output_kernel(where, begun, near, cross, w_out, out):
    def part(rows, head):
        return mm(rows[...], w_out[pl.ds(pl.multiple_of(head * HD, HD), HD)])

    out[...] = (begun[...] + part(near, where[2]) + part(cross, where[5])).astype(BF)


def whole(shape):
    return pl.BlockSpec(shape, lambda i, where: (0,) * len(shape))


def call(kernel, where, args, outs, scratch=()):
    return pl.pallas_call(
        kernel,
        out_shape=outs,
        grid_spec=pltpu.PrefetchScalarGridSpec(
            num_scalar_prefetch=1,
            grid=(1,),
            in_specs=[whole(a.shape) for a in args],
            out_specs=jax.tree.map(lambda o: whole(o.shape), outs),
            scratch_shapes=scratch,
        ),
        compiler_params=pltpu.CompilerParams(vmem_limit_bytes=32 << 20),
    )(where, *args)


def local(tokens, w_kv, w_rate, fast_weights, queries, w_query, out_gain, w_out):
    n_patch, n_view, n_head = (lax.axis_size(a) for a in ("patch", "view", "head"))
    patch, view, core = (lax.axis_index(a) for a in ("patch", "view", "head"))
    n_tok, width = tokens.shape
    n_qry = queries.shape[0]
    side = view % 2
    first = core == 0
    head = jnp.where(first, 2 * side, 1)
    sibling = jnp.where(first, 1, 2 * side)
    second = jnp.where(first, 1, 2 - 2 * side)
    where = jnp.stack([head, patch, sibling, second, 2 - 2 * side, 2 - 2 * side]).astype(jnp.int32)
    swap = [(0, 1), (1, 0)]

    def device(p, v, c):
        return (p * n_view + v) * n_head + c

    every = ("patch", "view", "head")
    ours = [(device(p, v, 0), device(p, v ^ 1, 0)) for p in range(n_patch) for v in range(n_view)]

    def rotate(n, shift):
        return [(i, (i + shift) % n) for i in range(n)]

    def pairs(s):
        return [(i, i ^ s) for i in range(n_patch)]

    far = [lax.ppermute(tokens, "view", rotate(n_view, s)) for s in range(1, n_view)]
    near = [tokens, lax.ppermute(tokens, "head", swap)]
    mine = lax.dynamic_index_in_dim(fast_weights, head, 2, keepdims=False).transpose(1, 0, 2)

    w_k = lax.dynamic_slice_in_dim(w_kv, head * HD, HD, 1)
    w_v = lax.dynamic_slice_in_dim(w_kv, width + head * HD, HD, 1)

    weights = [w_k, w_v, w_rate, mine]
    begun = call(
        functools.partial(first_kernel, len(near)),
        where,
        near + weights,
        jax.ShapeDtypeStruct((ROWS, HD), FP),
    )
    late, _ = lax.optimization_barrier((queries, begun))
    own_qry, message, other = call(
        query_kernel,
        where,
        [late, w_query],
        [jax.ShapeDtypeStruct((n, HD), BF) for n in (n_qry, 2 * n_qry, n_qry)],
        [pltpu.VMEM((HEADS, n_qry, HD), BF)],
    )
    begun, message, *far = lax.optimization_barrier((begun, message, *far))
    far = far + [lax.ppermute(f, "head", swap) for f in far]
    size = ROWS // n_patch
    chunks = call(
        functools.partial(second_kernel, len(far), n_patch),
        where,
        far + weights + [begun],
        [jax.ShapeDtypeStruct((size, HD), BF if s else FP) for s in range(n_patch)],
        [pltpu.VMEM((ROWS, HD), FP)],
    )
    rest = [*range(4, n_patch)]
    order = [2, 1, 3, *rest] if n_patch > 3 else [*range(1, n_patch)]
    order_back = [2, 1, 3, *rest] if n_patch > 3 else order
    got = {s: lax.ppermute(chunks[s], "patch", pairs(s)) for s in reversed(order)}
    own = chunks[0]
    for s in order:
        own = own + got[s].astype(FP)
    own = own.astype(BF)
    parts = {s: lax.ppermute(own, "patch", pairs(s)) for s in order_back}

    message, other, _ = lax.optimization_barrier((message, other, chunks[0]))
    swapped = lax.ppermute(message, "head", swap)
    across = lax.ppermute(jnp.concatenate([other, swapped[n_qry:]]), every, ours)

    gains = out_gain.reshape(1, width)
    normed, fresh = call(
        functools.partial(far_kernel, n_patch, order_back),
        where,
        [own] + [parts[s] for s in order_back] + [mine, gains, across],
        [jax.ShapeDtypeStruct((2 * n_qry, HD), BF), jax.ShapeDtypeStruct((3, FF, HD), BF)],
        [pltpu.VMEM((ROWS, HD), BF)],
    )
    back = lax.ppermute(normed, every, ours)
    for_other, begun = call(
        near_kernel,
        where,
        [own_qry, swapped[:n_qry], fresh, gains, w_out],
        [jax.ShapeDtypeStruct((n_qry, HD), BF), jax.ShapeDtypeStruct((n_qry, width), FP)],
    )
    near_out = lax.ppermute(for_other, "head", swap)
    begun, back = lax.optimization_barrier((begun, back))
    relayed = lax.ppermute(back[n_qry:], "head", swap)
    cross = jnp.where(first, back[:n_qry], relayed)
    return call(
        output_kernel,
        where,
        [begun, near_out, cross, w_out],
        jax.ShapeDtypeStruct((n_qry, width), BF),
    )


def solution(mesh):
    split = P(("groups", "patch", "view", "head"), None)
    in_specs = (split, P(), P(), P(), split, P(), P(), P())
    return jax.shard_map(local, mesh=mesh, in_specs=in_specs, out_specs=split, check_vma=False)
```

time: 77 us -> 73.1 us (0.949); the launches traced: 76 us -> 72.9 us
  matrix products: 2.5 us -> 0 us
  Pallas kernels: 11.9 us -> 14.4 us
  starting transfers between devices: 19.8 us -> 17.3 us
  other arithmetic: 1.13 us -> 0.13 us
    ppermute x9, starting transfers between devices: 11.8 us -> 8.46 us  [the longest x3 3.53 us: local(): parts = {s: lax.ppermute(own, 'patch', pairs(s)) for s in order_back}]
    pallas_call x4 -> x6, Pallas kernels: 11.9 us -> 14.4 us  [call(): pl.pallas_call(kernel, out_shape=outs, grid_spec=pltpu.PrefetchScalarGrid...]
    dot_general x1 -> x0, matrix products: 2.5 us -> none  [local(): return jnp.dot(joined, w_out, preferred_element_type=FP).astype(BF)]
    ppermute x9, waiting for transfers between devices: 30.2 us -> 31.9 us  [the longest x3 17.7 us: local(): parts = {s: lax.ppermute(own, 'patch', pairs(s)) for s in order_back}]
    ppermute x1, waiting for transfers between devices: 5.88 us -> 4.86 us  [local(): lax.ppermute(tokens, 'view', rotate(n_view, s))]
    select_n x1, other arithmetic: 0.94 us -> 0.02 us  [local(): cross = jnp.where(first, back[:n_qry], relayed)]
  transfers between devices with their start and end apart: 14 -> 14, of which waited for: 7 -> 9; matrix products, arithmetic and copies ran while one was open for 2% -> 2% of each run, Pallas kernels for 4% -> 7%
where the time goes in v3:
time: 73.1 us; the launch traced here: 72.9 us
  waiting for transfers between devices  39 us (53%)
  starting transfers between devices  17.3 us (24%)
  Pallas kernels  14.4 us (20%)
  local copies, waits for them, and re-layouts  1.94 us (3%)
    ppermute x3, waiting for transfers between devices, local(): parts = {s: lax.ppermute(own, 'patch', pairs(s)) for s in order_back}  17.7 us
    pallas_call x6, Pallas kernels, call(): pl.pallas_call(kernel, out_shape=outs, grid_spec=pltpu.PrefetchScalarGrid...  14.4 us
    ppermute x3, waiting for transfers between devices, local(): lax.ppermute(chunks[s], 'patch', pairs(s))  13.9 us
    ppermute x1, starting transfers between devices, local(): relayed = lax.ppermute(back[n_qry:], 'head', swap)  6.5 us
    ppermute x1, waiting for transfers between devices, local(): lax.ppermute(tokens, 'view', rotate(n_view, s))  4.86 us
    ppermute x3, starting transfers between devices, local(): parts = {s: lax.ppermute(own, 'patch', pairs(s)) for s in order_back}  3.53 us
    ppermute x3, starting transfers between devices, local(): lax.ppermute(chunks[s], 'patch', pairs(s))  3.5 us
  transfers between devices with their start and end apart: 14, of which 9 were waited for; matrix products, arithmetic and copies ran while one was open for 2% of the time, Pallas kernels for 7%

profile of v3, /device:TPU:11, one launch (start us, length us, event | category | flops | bytes accessed | tf_op | source)
XLA Modules:
  0.0 72.9 jit_solution(187346410407874814)
XLA Ops:
  0.0 0.0 copy-start
  0.0 0.7 %collective-permute-start = (bf16[256,768]{1,0:T(8,128)(2,1)}, bf16[256,768]{1,0:T(8,128)(2,1)S(1)}, u32[]{:S(2)}, u32[]{:S(2)}) collective-permute-start(bf16[256,768]{1,0:T(8,128)(2,1)} %refs_0_.1), channel_id=1, source_target_pairs={{0,1},{1,0},{2,3},{3,2},{4,5},{5,4},{6,7},{7,6},{8,9},{9,8},{10,11... | collective-permute-start | bytes 1179656 | tf_op jit(solution)/shard_map/ppermute | solution.py:190
  0.8 0.3 collective-permute-start.1
  1.0 0.1 stack.24.where
  1.1 0.6 copy-done
  1.7 0.1 dynamic-slice_bitcast_fusion.refs_5_.refs_4_
  1.7 1.2 %constant_dynamic-slice_fusion = (bf16[768,256]{1,0:T(8,128)(2,1)S(1)}, bf16[768,256]{1,0:T(8,128)(2,1)S(1)}) fusion(bf16[768,1536]{1,0:T(8,128)(2,1)} %param.9, s32[]{:T(128)S(6)} %select_n.41, s32[]{:T(128)S(6)} %select_n.40), kind=kLoop, calls=%fused_computation.4 | loop fusion | bytes 1572872 | tf_op jit(solution)/shard_map/dynamic_slice | solution.py:194
  2.9 0.0 copy-start.2
  2.9 0.0 copy-start.4
  2.9 0.0 collective-permute-done.refs_1_
  2.9 0.0 copy-done.3
  3.0 0.0 copy-done.5
  3.0 2.7 %shard_map.82.refs_6_ = f32[1536,256]{1,0:T(8,128)S(1)} custom-call(s32[6]{0:T(128)S(1)} %stack.24.where, bf16[256,768]{1,0:T(8,128)(2,1)S(1)} %copy-done.3, bf16[256,768]{1,0:T(8,128)(2,1)S(1)} %collective-permute-done.refs_1_, bf16[768,256]{1,0:T(8,128)(2,1)S(1)} %get-tuple-element.44.refs_2_, bf16[768,256]{1,0:T(8,128)(2,1)S(1)} %get-tuple-element.43.refs_3_, ...), custom_call_target="tpu_custom_call" | custom-call | tf_op jit(solution)/shard_map/pallas_call | solution.py:150
  5.6 0.0 copy-done.2
  5.6 0.0 copy-done.4
  5.6 1.1 %shard_map.83 = (bf16[256,256]{1,0:T(8,128)(2,1)S(1)}, bf16[512,256]{1,0:T(8,128)(2,1)S(1)}, bf16[256,256]{1,0:T(8,128)(2,1)S(1)}) custom-call(s32[6]{0:T(128)S(1)} %stack.24.where, bf16[256,768]{1,0:T(8,128)(2,1)S(1)} %copy-done.4, bf16[768,768]{1,0:T(8,128)(2,1)S(1)} %copy-done.2), custom_call_target="tpu_custom_call" | custom-call | tf_op jit(solution)/shard_map/pallas_call | solution.py:150
  6.8 4.9 %collective-permute-done.1.refs_0_ = bf16[256,768]{1,0:T(8,128)(2,1)S(1)} collective-permute-done((bf16[256,768]{1,0:T(8,128)(2,1)}, bf16[256,768]{1,0:T(8,128)(2,1)S(1)}, u32[]{:S(2)}, u32[]{:S(2)}) %collective-permute-start.1) | collective-permute-done | bytes 393248 | tf_op jit(solution)/shard_map/ppermute | solution.py:189
  11.7 0.8 %collective-permute-start.2 = (bf16[256,768]{1,0:T(8,128)(2,1)S(1)}, bf16[256,768]{1,0:T(8,128)(2,1)S(1)}, u32[]{:S(2)}, u32[]{:S(2)}) collective-permute-start(bf16[256,768]{1,0:T(8,128)(2,1)S(1)} %collective-permute-done.1.refs_0_), channel_id=1, source_target_pairs={{0,1},{1,0},{2,3},{3,2},{4,5},{5,4},{6,7},{7,6},{8,9},{9,8},{10,11... | collective-permute-start | bytes 1179656 | tf_op jit(solution)/shard_map/ppermute | solution.py:212
  12.5 1.3 %collective-permute-done.2.refs_1_ = bf16[256,768]{1,0:T(8,128)(2,1)S(1)} collective-permute-done((bf16[256,768]{1,0:T(8,128)(2,1)S(1)}, bf16[256,768]{1,0:T(8,128)(2,1)S(1)}, u32[]{:S(2)}, u32[]{:S(2)}) %collective-permute-start.2) | collective-permute-done | bytes 393248 | tf_op jit(solution)/shard_map/ppermute | solution.py:212
  13.9 2.7 %shard_map.84 = (f32[384,256]{1,0:T(8,128)S(1)}, bf16[384,256]{1,0:T(8,128)(2,1)S(1)}, bf16[384,256]{1,0:T(8,128)(2,1)S(1)}, bf16[384,256]{1,0:T(8,128)(2,1)S(1)}) custom-call(s32[6]{0:T(128)S(1)} %stack.24.where, bf16[256,768]{1,0:T(8,128)(2,1)S(1)} %collective-permute-done.1.refs_0_, bf16[256,768]{1,0:T(8,128)(2,1)S(1)} %collective-permute-done.2.refs_1_, ...), custom_call_target="tpu_custom_call" | custom-call | tf_op jit(solution)/shard_map/pallas_call | solution.py:150
  16.6 0.0 copy-start.1
  16.6 0.4 collective-permute-start.3
  17.1 1.3 %collective-permute-start.6 = (bf16[384,256]{1,0:T(8,128)(2,1)S(1)}, bf16[384,256]{1,0:T(8,128)(2,1)S(1)}, u32[]{:S(2)}, u32[]{:S(2)}) collective-permute-start(bf16[384,256]{1,0:T(8,128)(2,1)S(1)} %get-tuple-element.35), channel_id=1, source_target_pairs={{0,12},{4,8},{8,4},{12,0},{1,13},{5,9},{9,5},{13,1},{2,14},{6,10},... | collective-permute-start | bytes 589832 | tf_op jit(solution)/shard_map/ppermute | solution.py:224
  18.4 2.2 %collective-permute-start.5 = (bf16[384,256]{1,0:T(8,128)(2,1)S(1)}, bf16[384,256]{1,0:T(8,128)(2,1)S(1)}, u32[]{:S(2)}, u32[]{:S(2)}) collective-permute-start(bf16[384,256]{1,0:T(8,128)(2,1)S(1)} %get-tuple-element.34), channel_id=1, source_target_pairs={{0,4},{4,0},{8,12},{12,8},{1,5},{5,1},{9,13},{13,9},{2,6},{6,2},{1... | collective-permute-start | bytes 589832 | tf_op jit(solution)/shard_map/ppermute | solution.py:224
  20.5 0.0 collective-permute-start.4
  20.6 0.0 collective-permute-done.3
  20.6 0.7 collective-permute-start.10
  21.3 6.3 %collective-permute-done.6 = bf16[384,256]{1,0:T(8,128)(2,1)S(1)} collective-permute-done((bf16[384,256]{1,0:T(8,128)(2,1)S(1)}, bf16[384,256]{1,0:T(8,128)(2,1)S(1)}, u32[]{:S(2)}, u32[]{:S(2)}) %collective-permute-start.6) | collective-permute-done | bytes 196640 | tf_op jit(solution)/shard_map/ppermute | solution.py:224
  27.6 2.1 %collective-permute-done.5 = bf16[384,256]{1,0:T(8,128)(2,1)S(1)} collective-permute-done((bf16[384,256]{1,0:T(8,128)(2,1)S(1)}, bf16[384,256]{1,0:T(8,128)(2,1)S(1)}, u32[]{:S(2)}, u32[]{:S(2)}) %collective-permute-start.5) | collective-permute-done | bytes 196640 | tf_op jit(solution)/shard_map/ppermute | solution.py:224
  29.7 5.5 %collective-permute-done.4 = bf16[384,256]{1,0:T(8,128)(2,1)S(1)} collective-permute-done((bf16[384,256]{1,0:T(8,128)(2,1)S(1)}, bf16[384,256]{1,0:T(8,128)(2,1)S(1)}, u32[]{:S(2)}, u32[]{:S(2)}) %collective-permute-start.4) | collective-permute-done | bytes 196640 | tf_op jit(solution)/shard_map/ppermute | solution.py:224
  35.2 0.1 add_convert_fusion.refs_0_
  35.3 3.2 %collective-permute-start.7 = (bf16[384,256]{1,0:T(8,128)(2,1)S(1)}, bf16[384,256]{1,0:T(8,128)(2,1)S(1)}, u32[]{:S(2)}, u32[]{:S(2)}) collective-permute-start(bf16[384,256]{1,0:T(8,128)(2,1)S(1)} %add_convert_fusion.refs_0_), channel_id=1, source_target_pairs={{0,8},{4,12},{8,0},{12,4},{1,9},{5,13},{9,1},{13,5},{2,10},{6,14},... | collective-permute-start | bytes 589832 | tf_op jit(solution)/shard_map/ppermute | solution.py:229
  38.4 0.0 collective-permute-start.8
  38.4 0.4 collective-permute-start.9
  38.8 0.0 copy-done.6
  38.8 7.8 %collective-permute-done.7.refs_1_ = bf16[384,256]{1,0:T(8,128)(2,1)S(1)} collective-permute-done((bf16[384,256]{1,0:T(8,128)(2,1)S(1)}, bf16[384,256]{1,0:T(8,128)(2,1)S(1)}, u32[]{:S(2)}, u32[]{:S(2)}) %collective-permute-start.7) | collective-permute-done | bytes 196640 | tf_op jit(solution)/shard_map/ppermute | solution.py:229
  46.6 0.0 collective-permute-done.8.refs_2_
  46.6 9.9 %collective-permute-done.9.refs_3_ = bf16[384,256]{1,0:T(8,128)(2,1)S(1)} collective-permute-done((bf16[384,256]{1,0:T(8,128)(2,1)S(1)}, bf16[384,256]{1,0:T(8,128)(2,1)S(1)}, u32[]{:S(2)}, u32[]{:S(2)}) %collective-permute-start.9) | collective-permute-done | bytes 196640 | tf_op jit(solution)/shard_map/ppermute | solution.py:229
  56.5 0.0 collective-permute-done.10.refs_6_
  56.5 4.6 %shard_map.85 = (bf16[512,256]{1,0:T(8,128)(2,1)S(1)}, bf16[3,512,256]{2,1,0:T(8,128)(2,1)S(1)}) custom-call(s32[6]{0:T(128)S(1)} %stack.24.where, bf16[384,256]{1,0:T(8,128)(2,1)S(1)} %add_convert_fusion.refs_0_, bf16[384,256]{1,0:T(8,128)(2,1)S(1)} %collective-permute-done.7.refs_1_, bf16[384,256]{1,0:T(8,128)(2,1)S(1)} %collective-permute-done.8.refs_2_, ...), custom_call_target="tpu_custom_call" | custom-call | tf_op jit(solution)/shard_map/pallas_call | solution.py:150
  61.1 0.7 collective-permute-start.11
  61.8 1.6 %shard_map.86 = (bf16[256,256]{1,0:T(8,128)(2,1)S(1)}, f32[256,768]{1,0:T(8,128)S(1)}) custom-call(s32[6]{0:T(128)S(1)} %stack.24.where, bf16[256,256]{1,0:T(8,128)(2,1)S(1)} %get-tuple-element.25.own, bf16[256,256]{1,0:T(8,128)(2,1)S(1)} %get-tuple-element.46.other, bf16[3,512,256]{2,1,0:T(8,128)(2,1)S(1)} %get-tuple-element.37.fresh, ...), custom_call_target="tpu_custom_call" | custom-call | tf_op jit(solution)/shard_map/pallas_call | solution.py:150
  63.4 0.0 collective-permute-done.11
  63.4 6.5 %collective-permute-start.13 = (bf16[256,256]{1,0:T(8,128)(2,1)S(1)}, bf16[256,256]{1,0:T(8,128)(2,1)S(1)}, u32[]{:S(2)}, u32[]{:S(2)}) collective-permute-start(bf16[256,256]{1,0:T(8,128)(2,1)S(1)} %slice.15), channel_id=1, source_target_pairs={{0,1},{1,0},{2,3},{3,2},{4,5},{5,4},{6,7},{7,6},{8,9},{9,8},{10,11... | collective-permute-start | bytes 393224 | tf_op jit(solution)/shard_map/ppermute | solution.py:252
  69.9 0.1 collective-permute-start.12
  70.0 0.9 %collective-permute-done.13 = bf16[256,256]{1,0:T(8,128)(2,1)S(1)} collective-permute-done((bf16[256,256]{1,0:T(8,128)(2,1)S(1)}, bf16[256,256]{1,0:T(8,128)(2,1)S(1)}, u32[]{:S(2)}, u32[]{:S(2)}) %collective-permute-start.13) | collective-permute-done | bytes 131104 | tf_op jit(solution)/shard_map/ppermute | solution.py:252
  70.9 0.3 collective-permute-done.12.near
  71.2 1.7 %shard_map.87 = bf16[256,768]{1,0:T(8,128)(2,1)} custom-call(s32[6]{0:T(128)S(1)} %stack.24.where, f32[256,768]{1,0:T(8,128)S(1)} %get-tuple-element.40.begun, bf16[256,256]{1,0:T(8,128)(2,1)S(1)} %collective-permute-done.12.near, bf16[256,256]{1,0:T(8,128)(2,1)S(1)} %slice_select_fusion.cross, bf16[768,768]{1,0:T(8,128)(2,1)S(1)} %copy-done.1), custom_call_target="tpu_custom_call" | custom-call | tf_op jit(solution)/shard_map/pallas_call | solution.py:150
  (9 shorter events, 0.1 us)
Async XLA Ops:
  0.0 1.7 %copy-start = (bf16[512,3,3,256]{3,0,2,1:T(8,128)(2,1)S(1)}, bf16[512,3,3,256]{3,0,2,1:T(8,128)(2,1)}, u32[]{:S(2)}) copy-start(bf16[512,3,3,256]{3,0,2,1:T(8,128)(2,1)} %param.11) | copy-start | bytes 7077892
  0.0 2.9 %copy-start.3 = (bf16[256,768]{1,0:T(8,128)(2,1)S(1)}, bf16[256,768]{1,0:T(8,128)(2,1)}, u32[]{:S(2)}) copy-start(bf16[256,768]{1,0:T(8,128)(2,1)} %refs_0_.1) | copy-start | bytes 1179652
  0.0 2.9 %copy-start.5 = (bf16[3,768]{1,0:T(4,128)(2,1)S(1)}, bf16[3,768]{1,0:T(4,128)(2,1)}, u32[]{:S(2)}) copy-start(bf16[3,768]{1,0:T(4,128)(2,1)} %refs_4_.3) | copy-start | bytes 13828
  0.0 2.9 %collective-permute-start = (bf16[256,768]{1,0:T(8,128)(2,1)}, bf16[256,768]{1,0:T(8,128)(2,1)S(1)}, u32[]{:S(2)}, u32[]{:S(2)}) collective-permute-start(bf16[256,768]{1,0:T(8,128)(2,1)} %refs_0_.1), channel_id=1, source_target_pairs={{0,1},{1,0},{2,3},{3,2},{4,5},{5,4},{6,7},{7,6},{8,9},{9,8},{10,11... | collective-permute-start | bytes 1179656 | tf_op jit(solution)/shard_map/ppermute | solution.py:190
  0.8 10.9 %collective-permute-start.1 = (bf16[256,768]{1,0:T(8,128)(2,1)}, bf16[256,768]{1,0:T(8,128)(2,1)S(1)}, u32[]{:S(2)}, u32[]{:S(2)}) collective-permute-start(bf16[256,768]{1,0:T(8,128)(2,1)} %refs_0_.1), channel_id=1, source_target_pairs={{0,2},{2,0},{1,3},{3,1},{4,6},{6,4},{5,7},{7,5},{8,10},{10,8},{9,1... | collective-permute-start | bytes 1179656 | tf_op jit(solution)/shard_map/ppermute | solution.py:189
  2.9 2.7 %copy-start.2 = (bf16[768,768]{1,0:T(8,128)(2,1)S(1)}, bf16[768,768]{1,0:T(8,128)(2,1)}, u32[]{:S(2)}) copy-start(bf16[768,768]{1,0:T(8,128)(2,1)} %w_query.1) | copy-start | bytes 3538948
  2.9 2.7 %copy-start.4 = (bf16[256,768]{1,0:T(8,128)(2,1)S(1)}, bf16[256,768]{1,0:T(8,128)(2,1)}, u32[]{:S(2)}) copy-start(bf16[256,768]{1,0:T(8,128)(2,1)} %queries) | copy-start | bytes 1179652
  11.7 27.1 %copy-start.6 = (bf16[768]{0:T(1024)(128)(2,1)S(1)}, bf16[768]{0:T(1024)(128)(2,1)}, u32[]{:S(2)}) copy-start(bf16[768]{0:T(1024)(128)(2,1)} %param.14) | copy-start | bytes 4612
  11.7 2.2 %collective-permute-start.2 = (bf16[256,768]{1,0:T(8,128)(2,1)S(1)}, bf16[256,768]{1,0:T(8,128)(2,1)S(1)}, u32[]{:S(2)}, u32[]{:S(2)}) collective-permute-start(bf16[256,768]{1,0:T(8,128)(2,1)S(1)} %collective-permute-done.1.refs_0_), channel_id=1, source_target_pairs={{0,1},{1,0},{2,3},{3,2},{4,5},{5,4},{6,7},{7,6},{8,9},{9,8},{10,11... | collective-permute-start | bytes 1179656 | tf_op jit(solution)/shard_map/ppermute | solution.py:212
  16.6 45.1 %copy-start.1 = (bf16[768,768]{1,0:T(8,128)(2,1)S(1)}, bf16[768,768]{1,0:T(8,128)(2,1)}, u32[]{:S(2)}) copy-start(bf16[768,768]{1,0:T(8,128)(2,1)} %w_out.3) | copy-start | bytes 3538948
  16.6 3.9 %collective-permute-start.3 = (bf16[512,256]{1,0:T(8,128)(2,1)S(1)}, bf16[512,256]{1,0:T(8,128)(2,1)S(1)}, u32[]{:S(2)}, u32[]{:S(2)}) collective-permute-start(bf16[512,256]{1,0:T(8,128)(2,1)S(1)} %get-tuple-element.32), channel_id=1, source_target_pairs={{0,1},{1,0},{2,3},{3,2},{4,5},{5,4},{6,7},{7,6},{8,9},{9,8},{10,11... | collective-permute-start | bytes 786440 | tf_op jit(solution)/shard_map/ppermute | solution.py:232
  17.1 10.6 %collective-permute-start.6 = (bf16[384,256]{1,0:T(8,128)(2,1)S(1)}, bf16[384,256]{1,0:T(8,128)(2,1)S(1)}, u32[]{:S(2)}, u32[]{:S(2)}) collective-permute-start(bf16[384,256]{1,0:T(8,128)(2,1)S(1)} %get-tuple-element.35), channel_id=1, source_target_pairs={{0,12},{4,8},{8,4},{12,0},{1,13},{5,9},{9,5},{13,1},{2,14},{6,10},... | collective-permute-start | bytes 589832 | tf_op jit(solution)/shard_map/ppermute | solution.py:224
  18.4 11.4 %collective-permute-start.5 = (bf16[384,256]{1,0:T(8,128)(2,1)S(1)}, bf16[384,256]{1,0:T(8,128)(2,1)S(1)}, u32[]{:S(2)}, u32[]{:S(2)}) collective-permute-start(bf16[384,256]{1,0:T(8,128)(2,1)S(1)} %get-tuple-element.34), channel_id=1, source_target_pairs={{0,4},{4,0},{8,12},{12,8},{1,5},{5,1},{9,13},{13,9},{2,6},{6,2},{1... | collective-permute-start | bytes 589832 | tf_op jit(solution)/shard_map/ppermute | solution.py:224
  20.5 14.6 %collective-permute-start.4 = (bf16[384,256]{1,0:T(8,128)(2,1)S(1)}, bf16[384,256]{1,0:T(8,128)(2,1)S(1)}, u32[]{:S(2)}, u32[]{:S(2)}) collective-permute-start(bf16[384,256]{1,0:T(8,128)(2,1)S(1)} %get-tuple-element.33), channel_id=1, source_target_pairs={{0,8},{4,12},{8,0},{12,4},{1,9},{5,13},{9,1},{13,5},{2,10},{6,14},... | collective-permute-start | bytes 589832 | tf_op jit(solution)/shard_map/ppermute | solution.py:224
  20.6 35.9 %collective-permute-start.10 = (bf16[512,256]{1,0:T(8,128)(2,1)S(1)}, bf16[512,256]{1,0:T(8,128)(2,1)S(1)}, u32[]{:S(2)}, u32[]{:S(2)}) collective-permute-start(bf16[512,256]{1,0:T(8,128)(2,1)S(1)} %pad_maximum_fusion), channel_id=1, source_target_pairs={{0,2},{2,0},{4,6},{6,4},{8,10},{10,8},{12,14},{14,12},{16,18},{18,... | collective-permute-start | bytes 786440 | tf_op jit(solution)/shard_map/ppermute | solution.py:233
  35.3 11.3 %collective-permute-start.7 = (bf16[384,256]{1,0:T(8,128)(2,1)S(1)}, bf16[384,256]{1,0:T(8,128)(2,1)S(1)}, u32[]{:S(2)}, u32[]{:S(2)}) collective-permute-start(bf16[384,256]{1,0:T(8,128)(2,1)S(1)} %add_convert_fusion.refs_0_), channel_id=1, source_target_pairs={{0,8},{4,12},{8,0},{12,4},{1,9},{5,13},{9,1},{13,5},{2,10},{6,14},... | collective-permute-start | bytes 589832 | tf_op jit(solution)/shard_map/ppermute | solution.py:229
  38.4 8.2 %collective-permute-start.8 = (bf16[384,256]{1,0:T(8,128)(2,1)S(1)}, bf16[384,256]{1,0:T(8,128)(2,1)S(1)}, u32[]{:S(2)}, u32[]{:S(2)}) collective-permute-start(bf16[384,256]{1,0:T(8,128)(2,1)S(1)} %add_convert_fusion.refs_0_), channel_id=1, source_target_pairs={{0,4},{4,0},{8,12},{12,8},{1,5},{5,1},{9,13},{13,9},{2,6},{6,2},{1... | collective-permute-start | bytes 589832 | tf_op jit(solution)/shard_map/ppermute | solution.py:229
  38.4 18.0 %collective-permute-start.9 = (bf16[384,256]{1,0:T(8,128)(2,1)S(1)}, bf16[384,256]{1,0:T(8,128)(2,1)S(1)}, u32[]{:S(2)}, u32[]{:S(2)}) collective-permute-start(bf16[384,256]{1,0:T(8,128)(2,1)S(1)} %add_convert_fusion.refs_0_), channel_id=1, source_target_pairs={{0,12},{4,8},{8,4},{12,0},{1,13},{5,9},{9,5},{13,1},{2,14},{6,10},... | collective-permute-start | bytes 589832 | tf_op jit(solution)/shard_map/ppermute | solution.py:229
  61.1 2.3 %collective-permute-start.11 = (bf16[512,256]{1,0:T(8,128)(2,1)S(1)}, bf16[512,256]{1,0:T(8,128)(2,1)S(1)}, u32[]{:S(2)}, u32[]{:S(2)}) collective-permute-start(bf16[512,256]{1,0:T(8,128)(2,1)S(1)} %get-tuple-element.39), channel_id=1, source_target_pairs={{0,2},{2,0},{4,6},{6,4},{8,10},{10,8},{12,14},{14,12},{16,18},{18,... | collective-permute-start | bytes 786440 | tf_op jit(solution)/shard_map/ppermute | solution.py:243
  63.4 7.5 %collective-permute-start.13 = (bf16[256,256]{1,0:T(8,128)(2,1)S(1)}, bf16[256,256]{1,0:T(8,128)(2,1)S(1)}, u32[]{:S(2)}, u32[]{:S(2)}) collective-permute-start(bf16[256,256]{1,0:T(8,128)(2,1)S(1)} %slice.15), channel_id=1, source_target_pairs={{0,1},{1,0},{2,3},{3,2},{4,5},{5,4},{6,7},{7,6},{8,9},{9,8},{10,11... | collective-permute-start | bytes 393224 | tf_op jit(solution)/shard_map/ppermute | solution.py:252
  69.9 1.3 %collective-permute-start.12 = (bf16[256,256]{1,0:T(8,128)(2,1)S(1)}, bf16[256,256]{1,0:T(8,128)(2,1)S(1)}, u32[]{:S(2)}, u32[]{:S(2)}) collective-permute-start(bf16[256,256]{1,0:T(8,128)(2,1)S(1)} %get-tuple-element.41), channel_id=1, source_target_pairs={{0,1},{1,0},{2,3},{3,2},{4,5},{5,4},{6,7},{7,6},{8,9},{9,8},{10,11... | collective-permute-start | bytes 393224 | tf_op jit(solution)/shard_map/ppermute | solution.py:250

commit v4 on v3

--- a/solution.py
+++ b/solution.py
@@ -89,15 +89,14 @@
     return jnp.where(head == 0, low, jnp.where(head == 1, middle, high)).astype(FP)
 
 
-def near_kernel(where, own, other, fresh, gains, w_out, for_other, begun):
+def near_kernel(where, own, fresh, gains, w_out, begun):
     gain = own_gain(gains, where[0])
-    for_other[...] = decode(other[...], fresh, gain)
     product = w_out[pl.ds(pl.multiple_of(where[0] * HD, HD), HD)]
     begun[...] = mm(decode(own[...], fresh, gain), product)
 
 
 def far_kernel(n_patch, order, where, *refs):
-    parts, (fast, gains, qry, out, fresh, grads) = refs[:n_patch], refs[n_patch:]
+    parts, (fast, gains, qry, other, *outs, fresh, grads) = refs[:n_patch], refs[n_patch:]
     size = ROWS // n_patch
     for shift, part in zip((0, *order), parts):
         chunk = peer(where[1], shift)
@@ -120,8 +119,9 @@
         new_norm = jnp.sqrt(jnp.sum(moved * moved, -1, keepdims=True)) + eps_small
         fresh[kind] = (moved * (old_norm / new_norm)).astype(BF)
     gain = own_gain(gains, where[0])
-    for row in range(0, qry.shape[0], HD):
-        out[row : row + HD] = decode(qry[row : row + HD], fresh, gain)
+    n_qry = other.shape[0]
+    for i, out in enumerate(outs):
+        out[...] = decode(qry[i * n_qry : (i + 1) * n_qry] if i < 2 else other[...], fresh, gain)
 
 
 def query_kernel(where, queries, w_query, own, message, other, heads):
@@ -135,11 +135,12 @@
     other[...] = heads[where[4]]
 
 
-def output_kernel(where, begun, near, cross, w_out, out):
+def output_kernel(where, begun, near, to_first, to_second, w_out, out):
     def part(rows, head):
-        return mm(rows[...], w_out[pl.ds(pl.multiple_of(head * HD, HD), HD)])
-
-    out[...] = (begun[...] + part(near, where[2]) + part(cross, where[5])).astype(BF)
+        return mm(rows, w_out[pl.ds(pl.multiple_of(head * HD, HD), HD)])
+
+    cross = to_first[...] + to_second[...]
+    out[...] = (begun[...] + part(near[...], where[2]) + part(cross, where[5])).astype(BF)
 
 
 def whole(shape):
@@ -233,28 +234,26 @@
     across = lax.ppermute(jnp.concatenate([other, swapped[n_qry:]]), every, ours)
 
     gains = out_gain.reshape(1, width)
-    normed, fresh = call(
+    for_first, for_second, for_other, fresh = call(
         functools.partial(far_kernel, n_patch, order_back),
         where,
-        [own] + [parts[s] for s in order_back] + [mine, gains, across],
-        [jax.ShapeDtypeStruct((2 * n_qry, HD), BF), jax.ShapeDtypeStruct((3, FF, HD), BF)],
+        [own] + [parts[s] for s in order_back] + [mine, gains, across, swapped[:n_qry]],
+        [jax.ShapeDtypeStruct((n_qry, HD), BF)] * 3 + [jax.ShapeDtypeStruct((3, FF, HD), BF)],
         [pltpu.VMEM((ROWS, HD), BF)],
     )
-    back = lax.ppermute(normed, every, ours)
-    for_other, begun = call(
+    to_first = lax.ppermute(for_first, every, ours)
+    to_second = lax.ppermute(for_second, every, [(a, b + 1) for a, b in ours])
+    near_out = lax.ppermute(for_other, "head", swap)
+    begun = call(
         near_kernel,
         where,
-        [own_qry, swapped[:n_qry], fresh, gains, w_out],
-        [jax.ShapeDtypeStruct((n_qry, HD), BF), jax.ShapeDtypeStruct((n_qry, width), FP)],
-    )
-    near_out = lax.ppermute(for_other, "head", swap)
-    begun, back = lax.optimization_barrier((begun, back))
-    relayed = lax.ppermute(back[n_qry:], "head", swap)
-    cross = jnp.where(first, back[:n_qry], relayed)
+        [own_qry, fresh, gains, w_out],
+        jax.ShapeDtypeStruct((n_qry, width), FP),
+    )
     return call(
         output_kernel,
         where,
-        [begun, near_out, cross, w_out],
+        [begun, near_out, to_first, to_second, w_out],
         jax.ShapeDtypeStruct((n_qry, width), BF),
     )
 

time: 73.1 us -> 71.9 us (0.984)
  starting transfers between devices: 17.3 us -> 11.7 us
  waiting for transfers between devices: 39 us -> 43.3 us
    ppermute x2, starting transfers between devices: 7.18 us -> 1.95 us  [the longest x1 1.29 us: local(): to_second = lax.ppermute(for_second, every, [(a, b + 1) for a, b in ours])]
    ppermute x2, waiting for transfers between devices: 0.91 us -> 4.26 us  [the longest x1 4.26 us: local(): to_second = lax.ppermute(for_second, every, [(a, b + 1) for a, b in ours])]
    ppermute x3, waiting for transfers between devices: 13.9 us -> 16.1 us  [local(): lax.ppermute(chunks[s], 'patch', pairs(s))]
    ppermute x3, waiting for transfers between devices: 17.7 us -> 16.7 us  [local(): parts = {s: lax.ppermute(own, 'patch', pairs(s)) for s in order_back}]
    ppermute x3, starting transfers between devices: 3.5 us -> 2.65 us  [local(): lax.ppermute(chunks[s], 'patch', pairs(s))]
where the time goes in v4:
time: 71.9 us; the launch traced here: 71.7 us
  waiting for transfers between devices  43.3 us (60%)
  Pallas kernels  14.4 us (20%)
  starting transfers between devices  11.7 us (16%)
  local copies, waits for them, and re-layouts  1.93 us (3%)
    ppermute x3, waiting for transfers between devices, local(): parts = {s: lax.ppermute(own, 'patch', pairs(s)) for s in order_back}  16.7 us
    ppermute x3, waiting for transfers between devices, local(): lax.ppermute(chunks[s], 'patch', pairs(s))  16.1 us
    pallas_call x6, Pallas kernels, call(): pl.pallas_call(kernel, out_shape=outs, grid_spec=pltpu.PrefetchScalarGrid...  14.4 us
    ppermute x1, waiting for transfers between devices, local(): lax.ppermute(tokens, 'view', rotate(n_view, s))  4.86 us
    ppermute x1, waiting for transfers between devices, local(): to_second = lax.ppermute(for_second, every, [(a, b + 1) for a, b in ours])  4.26 us
    ppermute x3, starting transfers between devices, local(): parts = {s: lax.ppermute(own, 'patch', pairs(s)) for s in order_back}  3.44 us
    ppermute x3, starting transfers between devices, local(): lax.ppermute(chunks[s], 'patch', pairs(s))  2.65 us
  transfers between devices with their start and end apart: 14, of which 9 were waited for; matrix products, arithmetic and copies ran while one was open for 2% of the time, Pallas kernels for 7%

profile of v4, /device:TPU:11, one launch (start us, length us, event | category | flops | bytes accessed | tf_op | source)
XLA Modules:
  0.0 71.7 jit_solution(9130987609558843459)
XLA Ops:
  0.0 0.0 copy-start
  0.0 0.7 %collective-permute-start = (bf16[256,768]{1,0:T(8,128)(2,1)}, bf16[256,768]{1,0:T(8,128)(2,1)S(1)}, u32[]{:S(2)}, u32[]{:S(2)}) collective-permute-start(bf16[256,768]{1,0:T(8,128)(2,1)} %refs_0_.1), channel_id=1, source_target_pairs={{0,1},{1,0},{2,3},{3,2},{4,5},{5,4},{6,7},{7,6},{8,9},{9,8},{10,11... | collective-permute-start | bytes 1179656 | tf_op jit(solution)/shard_map/ppermute | solution.py:191
  0.8 0.3 collective-permute-start.1
  1.0 0.1 stack.24.where
  1.1 0.6 copy-done
  1.7 0.1 dynamic-slice_bitcast_fusion.refs_5_.refs_4_
  1.7 1.2 %constant_dynamic-slice_fusion = (bf16[768,256]{1,0:T(8,128)(2,1)S(1)}, bf16[768,256]{1,0:T(8,128)(2,1)S(1)}) fusion(bf16[768,1536]{1,0:T(8,128)(2,1)} %param.9, s32[]{:T(128)S(6)} %select_n.33, s32[]{:T(128)S(6)} %select_n.32), kind=kLoop, calls=%fused_computation.3 | loop fusion | bytes 1572872 | tf_op jit(solution)/shard_map/dynamic_slice | solution.py:195
  2.9 0.0 copy-start.2
  2.9 0.0 copy-start.4
  2.9 0.0 collective-permute-done.refs_1_
  2.9 0.0 copy-done.3
  3.0 0.0 copy-done.5
  3.0 2.7 %shard_map.82.refs_6_ = f32[1536,256]{1,0:T(8,128)S(1)} custom-call(s32[6]{0:T(128)S(1)} %stack.24.where, bf16[256,768]{1,0:T(8,128)(2,1)S(1)} %copy-done.3, bf16[256,768]{1,0:T(8,128)(2,1)S(1)} %collective-permute-done.refs_1_, bf16[768,256]{1,0:T(8,128)(2,1)S(1)} %get-tuple-element.40.refs_2_, bf16[768,256]{1,0:T(8,128)(2,1)S(1)} %get-tuple-element.39.refs_3_, ...), custom_call_target="tpu_custom_call" | custom-call | tf_op jit(solution)/shard_map/pallas_call | solution.py:151
  5.6 0.0 copy-done.2
  5.6 0.0 copy-done.4
  5.6 1.1 %shard_map.83 = (bf16[256,256]{1,0:T(8,128)(2,1)S(1)}, bf16[512,256]{1,0:T(8,128)(2,1)S(1)}, bf16[256,256]{1,0:T(8,128)(2,1)S(1)}) custom-call(s32[6]{0:T(128)S(1)} %stack.24.where, bf16[256,768]{1,0:T(8,128)(2,1)S(1)} %copy-done.4, bf16[768,768]{1,0:T(8,128)(2,1)S(1)} %copy-done.2), custom_call_target="tpu_custom_call" | custom-call | tf_op jit(solution)/shard_map/pallas_call | solution.py:151
  6.8 4.9 %collective-permute-done.1.refs_0_ = bf16[256,768]{1,0:T(8,128)(2,1)S(1)} collective-permute-done((bf16[256,768]{1,0:T(8,128)(2,1)}, bf16[256,768]{1,0:T(8,128)(2,1)S(1)}, u32[]{:S(2)}, u32[]{:S(2)}) %collective-permute-start.1) | collective-permute-done | bytes 393248 | tf_op jit(solution)/shard_map/ppermute | solution.py:190
  11.7 0.8 %collective-permute-start.2 = (bf16[256,768]{1,0:T(8,128)(2,1)S(1)}, bf16[256,768]{1,0:T(8,128)(2,1)S(1)}, u32[]{:S(2)}, u32[]{:S(2)}) collective-permute-start(bf16[256,768]{1,0:T(8,128)(2,1)S(1)} %collective-permute-done.1.refs_0_), channel_id=1, source_target_pairs={{0,1},{1,0},{2,3},{3,2},{4,5},{5,4},{6,7},{7,6},{8,9},{9,8},{10,11... | collective-permute-start | bytes 1179656 | tf_op jit(solution)/shard_map/ppermute | solution.py:213
  12.5 1.3 %collective-permute-done.2.refs_1_ = bf16[256,768]{1,0:T(8,128)(2,1)S(1)} collective-permute-done((bf16[256,768]{1,0:T(8,128)(2,1)S(1)}, bf16[256,768]{1,0:T(8,128)(2,1)S(1)}, u32[]{:S(2)}, u32[]{:S(2)}) %collective-permute-start.2) | collective-permute-done | bytes 393248 | tf_op jit(solution)/shard_map/ppermute | solution.py:213
  13.9 2.7 %shard_map.84 = (f32[384,256]{1,0:T(8,128)S(1)}, bf16[384,256]{1,0:T(8,128)(2,1)S(1)}, bf16[384,256]{1,0:T(8,128)(2,1)S(1)}, bf16[384,256]{1,0:T(8,128)(2,1)S(1)}) custom-call(s32[6]{0:T(128)S(1)} %stack.24.where, bf16[256,768]{1,0:T(8,128)(2,1)S(1)} %collective-permute-done.1.refs_0_, bf16[256,768]{1,0:T(8,128)(2,1)S(1)} %collective-permute-done.2.refs_1_, ...), custom_call_target="tpu_custom_call" | custom-call | tf_op jit(solution)/shard_map/pallas_call | solution.py:151
  16.6 0.0 copy-start.1
  16.6 0.4 collective-permute-start.9
  17.1 2.3 %collective-permute-start.3 = (bf16[384,256]{1,0:T(8,128)(2,1)S(1)}, bf16[384,256]{1,0:T(8,128)(2,1)S(1)}, u32[]{:S(2)}, u32[]{:S(2)}) collective-permute-start(bf16[384,256]{1,0:T(8,128)(2,1)S(1)} %get-tuple-element.28), channel_id=1, source_target_pairs={{0,8},{4,12},{8,0},{12,4},{1,9},{5,13},{9,1},{13,5},{2,10},{6,14},... | collective-permute-start | bytes 589832 | tf_op jit(solution)/shard_map/ppermute | solution.py:225
  19.4 0.2 collective-permute-start.4
  19.5 0.2 collective-permute-start.5
  19.7 0.0 collective-permute-done.9
  19.8 0.7 collective-permute-start.10
  20.4 7.6 %collective-permute-done.3 = bf16[384,256]{1,0:T(8,128)(2,1)S(1)} collective-permute-done((bf16[384,256]{1,0:T(8,128)(2,1)S(1)}, bf16[384,256]{1,0:T(8,128)(2,1)S(1)}, u32[]{:S(2)}, u32[]{:S(2)}) %collective-permute-start.3) | collective-permute-done | bytes 196640 | tf_op jit(solution)/shard_map/ppermute | solution.py:225
  28.1 0.6 collective-permute-done.4
  28.7 7.9 %collective-permute-done.5 = bf16[384,256]{1,0:T(8,128)(2,1)S(1)} collective-permute-done((bf16[384,256]{1,0:T(8,128)(2,1)S(1)}, bf16[384,256]{1,0:T(8,128)(2,1)S(1)}, u32[]{:S(2)}, u32[]{:S(2)}) %collective-permute-start.5) | collective-permute-done | bytes 196640 | tf_op jit(solution)/shard_map/ppermute | solution.py:225
  36.6 0.1 add_convert_fusion.refs_0_
  36.7 0.1 collective-permute-start.6
  36.7 3.4 %collective-permute-start.7 = (bf16[384,256]{1,0:T(8,128)(2,1)S(1)}, bf16[384,256]{1,0:T(8,128)(2,1)S(1)}, u32[]{:S(2)}, u32[]{:S(2)}) collective-permute-start(bf16[384,256]{1,0:T(8,128)(2,1)S(1)} %add_convert_fusion.refs_0_), channel_id=1, source_target_pairs={{0,4},{4,0},{8,12},{12,8},{1,5},{5,1},{9,13},{13,9},{2,6},{6,2},{1... | collective-permute-start | bytes 589832 | tf_op jit(solution)/shard_map/ppermute | solution.py:230
  40.1 0.0 collective-permute-start.8
  40.1 0.0 copy-done.6
  40.1 4.0 %collective-permute-done.6.refs_1_ = bf16[384,256]{1,0:T(8,128)(2,1)S(1)} collective-permute-done((bf16[384,256]{1,0:T(8,128)(2,1)S(1)}, bf16[384,256]{1,0:T(8,128)(2,1)S(1)}, u32[]{:S(2)}, u32[]{:S(2)}) %collective-permute-start.6) | collective-permute-done | bytes 196640 | tf_op jit(solution)/shard_map/ppermute | solution.py:230
  44.2 4.8 %collective-permute-done.7.refs_2_ = bf16[384,256]{1,0:T(8,128)(2,1)S(1)} collective-permute-done((bf16[384,256]{1,0:T(8,128)(2,1)S(1)}, bf16[384,256]{1,0:T(8,128)(2,1)S(1)}, u32[]{:S(2)}, u32[]{:S(2)}) %collective-permute-start.7) | collective-permute-done | bytes 196640 | tf_op jit(solution)/shard_map/ppermute | solution.py:230
  48.9 7.9 %collective-permute-done.8.refs_3_ = bf16[384,256]{1,0:T(8,128)(2,1)S(1)} collective-permute-done((bf16[384,256]{1,0:T(8,128)(2,1)S(1)}, bf16[384,256]{1,0:T(8,128)(2,1)S(1)}, u32[]{:S(2)}, u32[]{:S(2)}) %collective-permute-start.8) | collective-permute-done | bytes 196640 | tf_op jit(solution)/shard_map/ppermute | solution.py:230
  56.8 0.0 collective-permute-done.10.refs_6_
  56.8 4.9 %shard_map.85 = (bf16[256,256]{1,0:T(8,128)(2,1)S(1)}, bf16[256,256]{1,0:T(8,128)(2,1)S(1)}, bf16[256,256]{1,0:T(8,128)(2,1)S(1)}, bf16[3,512,256]{2,1,0:T(8,128)(2,1)S(1)}) custom-call(s32[6]{0:T(128)S(1)} %stack.24.where, bf16[384,256]{1,0:T(8,128)(2,1)S(1)} %add_convert_fusion.refs_0_, bf16[384,256]{1,0:T(8,128)(2,1)S(1)} %collective-permute-done.6.refs_1_, ...), custom_call_target="tpu_custom_call" | custom-call | tf_op jit(solution)/shard_map/pallas_call | solution.py:151
  61.7 0.7 collective-permute-start.11
  62.4 0.7 collective-permute-start.12
  63.1 1.3 %collective-permute-start.13 = (bf16[256,256]{1,0:T(8,128)(2,1)S(1)}, bf16[256,256]{1,0:T(8,128)(2,1)S(1)}, u32[]{:S(2)}, u32[]{:S(2)}) collective-permute-start(bf16[256,256]{1,0:T(8,128)(2,1)S(1)} %get-tuple-element.38), channel_id=1, source_target_pairs={{0,3},{2,1},{4,7},{6,5},{8,11},{10,9},{12,15},{14,13},{16,19},{18,... | collective-permute-start | bytes 393224 | tf_op jit(solution)/shard_map/ppermute | solution.py:245
  64.4 1.3 %shard_map.86.begun = f32[256,768]{1,0:T(8,128)S(1)} custom-call(s32[6]{0:T(128)S(1)} %stack.24.where, bf16[256,256]{1,0:T(8,128)(2,1)S(1)} %get-tuple-element.23.own, bf16[3,512,256]{2,1,0:T(8,128)(2,1)S(1)} %get-tuple-element.35.fresh, bf16[1,768]{1,0:T(2,128)(2,1)S(1)} %reshape.3.refs_5_.gains, bf16[768,768]{1,0:T(8,128)(2,1)S(1)} %copy-done.1), custom_call_target="tpu_custom_call" | custom-call | tf_op jit(solution)/shard_map/pallas_call | solution.py:151
  65.7 0.0 collective-permute-done.11.near
  65.7 0.0 collective-permute-done.12.to_first
  65.7 4.3 %collective-permute-done.13.to_second = bf16[256,256]{1,0:T(8,128)(2,1)S(1)} collective-permute-done((bf16[256,256]{1,0:T(8,128)(2,1)S(1)}, bf16[256,256]{1,0:T(8,128)(2,1)S(1)}, u32[]{:S(2)}, u32[]{:S(2)}) %collective-permute-start.13) | collective-permute-done | bytes 131104 | tf_op jit(solution)/shard_map/ppermute | solution.py:245
  70.0 1.7 %shard_map.87 = bf16[256,768]{1,0:T(8,128)(2,1)} custom-call(s32[6]{0:T(128)S(1)} %stack.24.where, f32[256,768]{1,0:T(8,128)S(1)} %shard_map.86.begun, bf16[256,256]{1,0:T(8,128)(2,1)S(1)} %collective-permute-done.11.near, bf16[256,256]{1,0:T(8,128)(2,1)S(1)} %collective-permute-done.12.to_first, bf16[256,256]{1,0:T(8,128)(2,1)S(1)} %collective-permute-done.13.to_second, ...), custom_call_target="tpu_custom_call" | custom-call | tf_op jit(solution)/shard_map/pallas_call | solution.py:151
  (7 shorter events, 0.0 us)
Async XLA Ops:
  0.0 1.7 %copy-start = (bf16[512,3,3,256]{3,0,2,1:T(8,128)(2,1)S(1)}, bf16[512,3,3,256]{3,0,2,1:T(8,128)(2,1)}, u32[]{:S(2)}) copy-start(bf16[512,3,3,256]{3,0,2,1:T(8,128)(2,1)} %param.11) | copy-start | bytes 7077892
  0.0 2.9 %copy-start.3 = (bf16[256,768]{1,0:T(8,128)(2,1)S(1)}, bf16[256,768]{1,0:T(8,128)(2,1)}, u32[]{:S(2)}) copy-start(bf16[256,768]{1,0:T(8,128)(2,1)} %refs_0_.1) | copy-start | bytes 1179652
  0.0 2.9 %copy-start.5 = (bf16[3,768]{1,0:T(4,128)(2,1)S(1)}, bf16[3,768]{1,0:T(4,128)(2,1)}, u32[]{:S(2)}) copy-start(bf16[3,768]{1,0:T(4,128)(2,1)} %refs_4_.3) | copy-start | bytes 13828
  0.0 2.9 %collective-permute-start = (bf16[256,768]{1,0:T(8,128)(2,1)}, bf16[256,768]{1,0:T(8,128)(2,1)S(1)}, u32[]{:S(2)}, u32[]{:S(2)}) collective-permute-start(bf16[256,768]{1,0:T(8,128)(2,1)} %refs_0_.1), channel_id=1, source_target_pairs={{0,1},{1,0},{2,3},{3,2},{4,5},{5,4},{6,7},{7,6},{8,9},{9,8},{10,11... | collective-permute-start | bytes 1179656 | tf_op jit(solution)/shard_map/ppermute | solution.py:191
  0.8 10.9 %collective-permute-start.1 = (bf16[256,768]{1,0:T(8,128)(2,1)}, bf16[256,768]{1,0:T(8,128)(2,1)S(1)}, u32[]{:S(2)}, u32[]{:S(2)}) collective-permute-start(bf16[256,768]{1,0:T(8,128)(2,1)} %refs_0_.1), channel_id=1, source_target_pairs={{0,2},{2,0},{1,3},{3,1},{4,6},{6,4},{5,7},{7,5},{8,10},{10,8},{9,1... | collective-permute-start | bytes 1179656 | tf_op jit(solution)/shard_map/ppermute | solution.py:190
  2.9 2.7 %copy-start.2 = (bf16[768,768]{1,0:T(8,128)(2,1)S(1)}, bf16[768,768]{1,0:T(8,128)(2,1)}, u32[]{:S(2)}) copy-start(bf16[768,768]{1,0:T(8,128)(2,1)} %w_query.1) | copy-start | bytes 3538948
  2.9 2.7 %copy-start.4 = (bf16[256,768]{1,0:T(8,128)(2,1)S(1)}, bf16[256,768]{1,0:T(8,128)(2,1)}, u32[]{:S(2)}) copy-start(bf16[256,768]{1,0:T(8,128)(2,1)} %queries) | copy-start | bytes 1179652
  11.7 28.5 %copy-start.6 = (bf16[768]{0:T(1024)(128)(2,1)S(1)}, bf16[768]{0:T(1024)(128)(2,1)}, u32[]{:S(2)}) copy-start(bf16[768]{0:T(1024)(128)(2,1)} %param.14) | copy-start | bytes 4612
  11.7 2.2 %collective-permute-start.2 = (bf16[256,768]{1,0:T(8,128)(2,1)S(1)}, bf16[256,768]{1,0:T(8,128)(2,1)S(1)}, u32[]{:S(2)}, u32[]{:S(2)}) collective-permute-start(bf16[256,768]{1,0:T(8,128)(2,1)S(1)} %collective-permute-done.1.refs_0_), channel_id=1, source_target_pairs={{0,1},{1,0},{2,3},{3,2},{4,5},{5,4},{6,7},{7,6},{8,9},{9,8},{10,11... | collective-permute-start | bytes 1179656 | tf_op jit(solution)/shard_map/ppermute | solution.py:213
  16.6 47.8 %copy-start.1 = (bf16[768,768]{1,0:T(8,128)(2,1)S(1)}, bf16[768,768]{1,0:T(8,128)(2,1)}, u32[]{:S(2)}) copy-start(bf16[768,768]{1,0:T(8,128)(2,1)} %w_out.3) | copy-start | bytes 3538948
  16.6 3.1 %collective-permute-start.9 = (bf16[512,256]{1,0:T(8,128)(2,1)S(1)}, bf16[512,256]{1,0:T(8,128)(2,1)S(1)}, u32[]{:S(2)}, u32[]{:S(2)}) collective-permute-start(bf16[512,256]{1,0:T(8,128)(2,1)S(1)} %get-tuple-element.34), channel_id=1, source_target_pairs={{0,1},{1,0},{2,3},{3,2},{4,5},{5,4},{6,7},{7,6},{8,9},{9,8},{10,11... | collective-permute-start | bytes 786440 | tf_op jit(solution)/shard_map/ppermute | solution.py:233
  17.1 11.0 %collective-permute-start.3 = (bf16[384,256]{1,0:T(8,128)(2,1)S(1)}, bf16[384,256]{1,0:T(8,128)(2,1)S(1)}, u32[]{:S(2)}, u32[]{:S(2)}) collective-permute-start(bf16[384,256]{1,0:T(8,128)(2,1)S(1)} %get-tuple-element.28), channel_id=1, source_target_pairs={{0,8},{4,12},{8,0},{12,4},{1,9},{5,13},{9,1},{13,5},{2,10},{6,14},... | collective-permute-start | bytes 589832 | tf_op jit(solution)/shard_map/ppermute | solution.py:225
  19.4 9.3 %collective-permute-start.4 = (bf16[384,256]{1,0:T(8,128)(2,1)S(1)}, bf16[384,256]{1,0:T(8,128)(2,1)S(1)}, u32[]{:S(2)}, u32[]{:S(2)}) collective-permute-start(bf16[384,256]{1,0:T(8,128)(2,1)S(1)} %get-tuple-element.29), channel_id=1, source_target_pairs={{0,4},{4,0},{8,12},{12,8},{1,5},{5,1},{9,13},{13,9},{2,6},{6,2},{1... | collective-permute-start | bytes 589832 | tf_op jit(solution)/shard_map/ppermute | solution.py:225
  19.5 17.0 %collective-permute-start.5 = (bf16[384,256]{1,0:T(8,128)(2,1)S(1)}, bf16[384,256]{1,0:T(8,128)(2,1)S(1)}, u32[]{:S(2)}, u32[]{:S(2)}) collective-permute-start(bf16[384,256]{1,0:T(8,128)(2,1)S(1)} %get-tuple-element.30), channel_id=1, source_target_pairs={{0,12},{4,8},{8,4},{12,0},{1,13},{5,9},{9,5},{13,1},{2,14},{6,10},... | collective-permute-start | bytes 589832 | tf_op jit(solution)/shard_map/ppermute | solution.py:225
  19.8 37.1 %collective-permute-start.10 = (bf16[512,256]{1,0:T(8,128)(2,1)S(1)}, bf16[512,256]{1,0:T(8,128)(2,1)S(1)}, u32[]{:S(2)}, u32[]{:S(2)}) collective-permute-start(bf16[512,256]{1,0:T(8,128)(2,1)S(1)} %pad_maximum_fusion), channel_id=1, source_target_pairs={{0,2},{2,0},{4,6},{6,4},{8,10},{10,8},{12,14},{14,12},{16,18},{18,... | collective-permute-start | bytes 786440 | tf_op jit(solution)/shard_map/ppermute | solution.py:234
  36.7 7.5 %collective-permute-start.6 = (bf16[384,256]{1,0:T(8,128)(2,1)S(1)}, bf16[384,256]{1,0:T(8,128)(2,1)S(1)}, u32[]{:S(2)}, u32[]{:S(2)}) collective-permute-start(bf16[384,256]{1,0:T(8,128)(2,1)S(1)} %add_convert_fusion.refs_0_), channel_id=1, source_target_pairs={{0,8},{4,12},{8,0},{12,4},{1,9},{5,13},{9,1},{13,5},{2,10},{6,14},... | collective-permute-start | bytes 589832 | tf_op jit(solution)/shard_map/ppermute | solution.py:230
  36.7 12.2 %collective-permute-start.7 = (bf16[384,256]{1,0:T(8,128)(2,1)S(1)}, bf16[384,256]{1,0:T(8,128)(2,1)S(1)}, u32[]{:S(2)}, u32[]{:S(2)}) collective-permute-start(bf16[384,256]{1,0:T(8,128)(2,1)S(1)} %add_convert_fusion.refs_0_), channel_id=1, source_target_pairs={{0,4},{4,0},{8,12},{12,8},{1,5},{5,1},{9,13},{13,9},{2,6},{6,2},{1... | collective-permute-start | bytes 589832 | tf_op jit(solution)/shard_map/ppermute | solution.py:230
  40.1 16.7 %collective-permute-start.8 = (bf16[384,256]{1,0:T(8,128)(2,1)S(1)}, bf16[384,256]{1,0:T(8,128)(2,1)S(1)}, u32[]{:S(2)}, u32[]{:S(2)}) collective-permute-start(bf16[384,256]{1,0:T(8,128)(2,1)S(1)} %add_convert_fusion.refs_0_), channel_id=1, source_target_pairs={{0,12},{4,8},{8,4},{12,0},{1,13},{5,9},{9,5},{13,1},{2,14},{6,10},... | collective-permute-start | bytes 589832 | tf_op jit(solution)/shard_map/ppermute | solution.py:230
  61.7 4.0 %collective-permute-start.11 = (bf16[256,256]{1,0:T(8,128)(2,1)S(1)}, bf16[256,256]{1,0:T(8,128)(2,1)S(1)}, u32[]{:S(2)}, u32[]{:S(2)}) collective-permute-start(bf16[256,256]{1,0:T(8,128)(2,1)S(1)} %get-tuple-element.36), channel_id=1, source_target_pairs={{0,1},{1,0},{2,3},{3,2},{4,5},{5,4},{6,7},{7,6},{8,9},{9,8},{10,11... | collective-permute-start | bytes 393224 | tf_op jit(solution)/shard_map/ppermute | solution.py:246
  62.4 3.3 %collective-permute-start.12 = (bf16[256,256]{1,0:T(8,128)(2,1)S(1)}, bf16[256,256]{1,0:T(8,128)(2,1)S(1)}, u32[]{:S(2)}, u32[]{:S(2)}) collective-permute-start(bf16[256,256]{1,0:T(8,128)(2,1)S(1)} %get-tuple-element.37), channel_id=1, source_target_pairs={{0,2},{2,0},{4,6},{6,4},{8,10},{10,8},{12,14},{14,12},{16,18},{18,... | collective-permute-start | bytes 393224 | tf_op jit(solution)/shard_map/ppermute | solution.py:244
  63.1 6.9 %collective-permute-start.13 = (bf16[256,256]{1,0:T(8,128)(2,1)S(1)}, bf16[256,256]{1,0:T(8,128)(2,1)S(1)}, u32[]{:S(2)}, u32[]{:S(2)}) collective-permute-start(bf16[256,256]{1,0:T(8,128)(2,1)S(1)} %get-tuple-element.38), channel_id=1, source_target_pairs={{0,3},{2,1},{4,7},{6,5},{8,11},{10,9},{12,15},{14,13},{16,19},{18,... | collective-permute-start | bytes 393224 | tf_op jit(solution)/shard_map/ppermute | solution.py:245

commit v5 on v3

--- a/solution.py
+++ b/solution.py
@@ -21,7 +21,12 @@
 BF = jnp.bfloat16
 NT = (((1,), (1,)), ((), ()))
 TN = (((0,), (0,)), ((), ()))
-ROWS = 3 * FF
+LARGE = FF // 2
+SMALL = FF // 4
+
+
+def exchange_order(n_patch):
+    return [0, 2, 1, 3, *range(4, n_patch)] if n_patch > 3 else [*range(n_patch)]
 
 
 def mm(a, b, dims=(((1,), (0,)), ((), ()))):
@@ -32,12 +37,8 @@
     return raw * lax.rsqrt(jnp.sum(raw * raw, -1, keepdims=True) + eps_small)
 
 
-def peer(index, shift):
-    return index ^ shift
-
-
-def add_gradient(tok, head, w_k, w_v, w_rate, fast, acc):
-    rows = tok[...]
+def add_gradient(rows, segment, acc):
+    head, w_k, w_v, w_rate, fast = segment
     keys = unit(mm(rows, w_k[...])).astype(BF)
     rates = mm(rows, w_rate[...], NT)
     pick = lax.broadcasted_iota(jnp.int32, rates.shape, 1) == head
@@ -52,28 +53,51 @@
     hidden = (act * up_pre).astype(BF)
     d_gate = (back * up_pre * sig * (1.0 + gate_pre * (1.0 - sig))).astype(BF)
     d_up = (back * act).astype(BF)
-    acc[0:FF] += mm(d_gate, keys)
-    acc[FF : 2 * FF] += mm(d_up, keys)
-    acc[2 * FF : ROWS] += mm(hidden, scaled)
+    acc[0] += mm(d_gate, keys)
+    acc[1] += mm(d_up, keys)
+    acc[2] += mm(hidden, scaled)
+
+
+def add_segments(where, toks, weights, accs):
+    w_rate, *weights = weights
+    for i, acc in enumerate(accs):
+        w_k, w_v, fast = weights[3 * i : 3 * i + 3]
+        for tok in toks:
+            for at in range(0, tok.shape[0], HD):
+                add_gradient(tok[at : at + HD], (where[6 + i], w_k, w_v, w_rate, fast), acc)
 
 
 def first_kernel(n_tok, where, *refs):
-    toks, (w_k, w_v, w_rate, fast, acc) = refs[:n_tok], refs[n_tok:]
-    acc[...] = jnp.zeros_like(acc)
-    for tok in toks:
-        add_gradient(tok, where[0], w_k, w_v, w_rate, fast, acc)
+    toks, weights, accs = refs[:n_tok], refs[n_tok:-2], refs[-2:]
+    for acc in accs:
+        acc[...] = jnp.zeros_like(acc)
+    add_segments(where, toks, weights, accs)
 
 
 def second_kernel(n_tok, n_patch, where, *refs):
-    toks, (w_k, w_v, w_rate, fast, begun) = refs[:n_tok], refs[n_tok : n_tok + 5]
-    outs, acc = refs[n_tok + 5 : -1], refs[-1]
-    acc[...] = begun[...]
-    for tok in toks:
-        add_gradient(tok, where[0], w_k, w_v, w_rate, fast, acc)
-    size = ROWS // n_patch
-    for shift, out in enumerate(outs):
-        chunk = peer(where[1], shift)
-        out[...] = acc[pl.ds(pl.multiple_of(chunk * size, size), size)].astype(out.dtype)
+    toks, weights, begun = refs[:n_tok], refs[n_tok : n_tok + 7], refs[n_tok + 7 : n_tok + 9]
+    outs, accs = refs[n_tok + 9 : -2], refs[-2:]
+    for acc, part in zip(accs, begun):
+        acc[...] = part[...]
+    add_segments(where, toks, weights, accs)
+    for out, shift in zip(outs, exchange_order(n_patch)):
+        chunk = where[1] ^ shift
+        at = 0
+        for acc in accs:
+            size = acc.shape[1] // n_patch
+            out[:, at : at + size] = acc[:, pl.ds(pl.multiple_of(chunk * size, size), size)].astype(out.dtype)
+            at += size
+
+
+def collect_kernel(n_patch, where, *refs):
+    parts, segments = refs[:n_patch], refs[n_patch:]
+    for part, shift in zip(parts, exchange_order(n_patch)):
+        chunk = where[1] ^ shift
+        at = 0
+        for segment in segments:
+            size = segment.shape[1] // n_patch
+            segment[:, pl.ds(pl.multiple_of(chunk * size, size), size)] = part[:, at : at + size]
+            at += size
 
 
 def decode(rows, fresh, gain):
@@ -96,15 +120,22 @@
     begun[...] = mm(decode(own[...], fresh, gain), product)
 
 
-def far_kernel(n_patch, order, where, *refs):
-    parts, (fast, gains, qry, out, fresh, grads) = refs[:n_patch], refs[n_patch:]
-    size = ROWS // n_patch
-    for shift, part in zip((0, *order), parts):
-        chunk = peer(where[1], shift)
-        grads[pl.ds(pl.multiple_of(chunk * size, size), size)] = part[...]
+def far_kernel(where, large, small, rest, half, fast, gains, qry, out, fresh, grads):
+    @pl.when(where[8] == 0)
+    def _():
+        grads[:, :LARGE] = large[...]
+        grads[:, LARGE : LARGE + SMALL] = small[...]
+        grads[:, LARGE + SMALL :] = rest[...]
+
+    @pl.when(where[8] == 1)
+    def _():
+        at = pl.multiple_of(where[9] * LARGE, LARGE)
+        grads[:, pl.ds(at, LARGE)] = large[...]
+        grads[:, pl.ds(pl.multiple_of(LARGE - at, LARGE), LARGE)] = half[...]
+
     ortho = []
     for kind in range(3):
-        grad = grads[kind * FF : (kind + 1) * FF].astype(FP)
+        grad = grads[kind].astype(FP)
         total = jnp.sum(jnp.sum(grad * grad, -1, keepdims=True), 0, keepdims=True)
         ortho.append((grad / (jnp.sqrt(total) + eps_small)).astype(BF))
     for step in range(STEPS):
@@ -120,8 +151,11 @@
         new_norm = jnp.sqrt(jnp.sum(moved * moved, -1, keepdims=True)) + eps_small
         fresh[kind] = (moved * (old_norm / new_norm)).astype(BF)
     gain = own_gain(gains, where[0])
-    for row in range(0, qry.shape[0], HD):
-        out[row : row + HD] = decode(qry[row : row + HD], fresh, gain)
+
+    @pl.when(where[8] == 0)
+    def _():
+        for row in range(0, qry.shape[0], HD):
+            out[row : row + HD] = decode(qry[row : row + HD], fresh, gain)
 
 
 def query_kernel(where, queries, w_query, own, message, other, heads):
@@ -135,11 +169,12 @@
     other[...] = heads[where[4]]
 
 
-def output_kernel(where, begun, near, cross, w_out, out):
+def output_kernel(where, begun, near, back, relayed, w_out, out):
     def part(rows, head):
-        return mm(rows[...], w_out[pl.ds(pl.multiple_of(head * HD, HD), HD)])
-
-    out[...] = (begun[...] + part(near, where[2]) + part(cross, where[5])).astype(BF)
+        return mm(rows, w_out[pl.ds(pl.multiple_of(head * HD, HD), HD)])
+
+    cross = jnp.where(where[8] == 0, back[: relayed.shape[0]], relayed[...])
+    out[...] = (begun[...] + part(near[...], where[2]) + part(cross, where[5])).astype(BF)
 
 
 def whole(shape):
@@ -171,7 +206,9 @@
     head = jnp.where(first, 2 * side, 1)
     sibling = jnp.where(first, 1, 2 * side)
     second = jnp.where(first, 1, 2 - 2 * side)
-    where = jnp.stack([head, patch, sibling, second, 2 - 2 * side, 2 - 2 * side]).astype(jnp.int32)
+    units = jnp.where(first, 0, side * LARGE), jnp.where(first, LARGE, LARGE + SMALL)
+    where = [head, patch, sibling, second, 2 - 2 * side, 2 - 2 * side, head, 2 * side, core, side]
+    where = jnp.stack(where).astype(jnp.int32)
     swap = [(0, 1), (1, 0)]
 
     def device(p, v, c):
@@ -182,6 +219,8 @@
 
     def rotate(n, shift):
         return [(i, (i + shift) % n) for i in range(n)]
+
+    seconds = [(a + 1, b + 1) for a, b in ours]
 
     def pairs(s):
         return [(i, i ^ s) for i in range(n_patch)]
@@ -190,17 +229,15 @@
     near = [tokens, lax.ppermute(tokens, "head", swap)]
     mine = lax.dynamic_index_in_dim(fast_weights, head, 2, keepdims=False).transpose(1, 0, 2)
 
-    w_k = lax.dynamic_slice_in_dim(w_kv, head * HD, HD, 1)
-    w_v = lax.dynamic_slice_in_dim(w_kv, width + head * HD, HD, 1)
-
-    weights = [w_k, w_v, w_rate, mine]
-    begun = call(
-        functools.partial(first_kernel, len(near)),
-        where,
-        near + weights,
-        jax.ShapeDtypeStruct((ROWS, HD), FP),
-    )
-    late, _ = lax.optimization_barrier((queries, begun))
+    weights = [w_rate]
+    for owner, unit_at, size in ((head, units[0], LARGE), (2 * side, units[1], SMALL)):
+        weights.append(lax.dynamic_slice_in_dim(w_kv, owner * HD, HD, 1))
+        weights.append(lax.dynamic_slice_in_dim(w_kv, width + owner * HD, HD, 1))
+        piece = lax.dynamic_slice(fast_weights, (unit_at, 0, owner, 0), (size, 3, 1, HD))
+        weights.append(piece.reshape(size, 3, HD).transpose(1, 0, 2))
+    sums = [jax.ShapeDtypeStruct((3, size, HD), FP) for size in (LARGE, SMALL)]
+    begun = list(call(functools.partial(first_kernel, len(near)), where, near + weights, sums))
+    late, _ = lax.optimization_barrier((queries, begun[0]))
     own_qry, message, other = call(
         query_kernel,
         where,
@@ -208,37 +245,43 @@
         [jax.ShapeDtypeStruct((n, HD), BF) for n in (n_qry, 2 * n_qry, n_qry)],
         [pltpu.VMEM((HEADS, n_qry, HD), BF)],
     )
-    begun, message, *far = lax.optimization_barrier((begun, message, *far))
+    begun[0], message, *far = lax.optimization_barrier((begun[0], message, *far))
     far = far + [lax.ppermute(f, "head", swap) for f in far]
-    size = ROWS // n_patch
+    size = (LARGE + SMALL) // n_patch
     chunks = call(
         functools.partial(second_kernel, len(far), n_patch),
         where,
-        far + weights + [begun],
-        [jax.ShapeDtypeStruct((size, HD), BF if s else FP) for s in range(n_patch)],
-        [pltpu.VMEM((ROWS, HD), FP)],
-    )
-    rest = [*range(4, n_patch)]
-    order = [2, 1, 3, *rest] if n_patch > 3 else [*range(1, n_patch)]
-    order_back = [2, 1, 3, *rest] if n_patch > 3 else order
-    got = {s: lax.ppermute(chunks[s], "patch", pairs(s)) for s in reversed(order)}
+        far + weights + begun,
+        [jax.ShapeDtypeStruct((3, size, HD), BF if k else FP) for k in range(n_patch)],
+        [pltpu.VMEM(s.shape, FP) for s in sums],
+    )
+    order = exchange_order(n_patch)
+    got = [lax.ppermute(chunks[k], "patch", pairs(order[k])) for k in range(n_patch - 1, 0, -1)]
     own = chunks[0]
-    for s in order:
-        own = own + got[s].astype(FP)
+    for part in got:
+        own = own + part.astype(FP)
     own = own.astype(BF)
-    parts = {s: lax.ppermute(own, "patch", pairs(s)) for s in order_back}
+    parts = [lax.ppermute(own, "patch", pairs(s)) for s in exchange_order(n_patch)[1:]]
 
     message, other, _ = lax.optimization_barrier((message, other, chunks[0]))
     swapped = lax.ppermute(message, "head", swap)
     across = lax.ppermute(jnp.concatenate([other, swapped[n_qry:]]), every, ours)
 
+    large, small = call(
+        functools.partial(collect_kernel, n_patch),
+        where,
+        [own, *parts],
+        [jax.ShapeDtypeStruct(s.shape, BF) for s in sums],
+    )
+    rest = lax.ppermute(small, "head", swap)
+    half = lax.ppermute(large, every, seconds)
     gains = out_gain.reshape(1, width)
     normed, fresh = call(
-        functools.partial(far_kernel, n_patch, order_back),
-        where,
-        [own] + [parts[s] for s in order_back] + [mine, gains, across],
+        far_kernel,
+        where,
+        [large, small, rest, half, mine, gains, across],
         [jax.ShapeDtypeStruct((2 * n_qry, HD), BF), jax.ShapeDtypeStruct((3, FF, HD), BF)],
-        [pltpu.VMEM((ROWS, HD), BF)],
+        [pltpu.VMEM((3, FF, HD), BF)],
     )
     back = lax.ppermute(normed, every, ours)
     for_other, begun = call(
@@ -250,11 +293,10 @@
     near_out = lax.ppermute(for_other, "head", swap)
     begun, back = lax.optimization_barrier((begun, back))
     relayed = lax.ppermute(back[n_qry:], "head", swap)
-    cross = jnp.where(first, back[:n_qry], relayed)
     return call(
         output_kernel,
         where,
-        [begun, near_out, cross, w_out],
+        [begun, near_out, back, relayed, w_out],
         jax.ShapeDtypeStruct((n_qry, width), BF),
     )
 

time: 73.1 us -> 77.7 us (1.063)
  starting transfers between devices: 17.3 us -> 21.7 us
  waiting for transfers between devices: 39 us -> 36.7 us
  Pallas kernels: 14.4 us -> 16.3 us
    ppermute x1, starting transfers between devices: 0.08 us -> 3.65 us  [local(): near_out = lax.ppermute(for_other, 'head', swap)]
    ppermute x6 -> x8, starting transfers between devices: 7.02 us -> 9.48 us  [the longest x3 3.44 us: local(): lax.ppermute(own, 'patch', pairs(s))]
    ppermute x1, starting transfers between devices: 6.5 us -> 4.18 us  [local(): relayed = lax.ppermute(back[n_qry:], 'head', swap)]
    pallas_call x6 -> x7, Pallas kernels: 14.4 us -> 16.3 us  [call(): pl.pallas_call(kernel, out_shape=outs, grid_spec=pltpu.PrefetchScalarGrid...]
    ppermute x1, waiting for transfers between devices: 4.86 us -> 3.39 us  [local(): lax.ppermute(tokens, 'view', rotate(n_view, s))]
    ppermute x6 -> x8, waiting for transfers between devices: 31.5 us -> 31 us  [the longest x3 12.5 us: local(): lax.ppermute(own, 'patch', pairs(s))]
  transfers between devices with their start and end apart: 14 -> 16, of which waited for: 9 -> 11; matrix products, arithmetic and copies ran while one was open for 2% -> 2% of each run, Pallas kernels for 7% -> 9%
where the time goes in v5:
time: 77.7 us; the launch traced here: 77.5 us
  waiting for transfers between devices  36.7 us (47%)
  starting transfers between devices  21.7 us (28%)
  Pallas kernels  16.3 us (21%)
  local copies, waits for them, and re-layouts  2.41 us (3%)
    pallas_call x7, Pallas kernels, call(): pl.pallas_call(kernel, out_shape=outs, grid_spec=pltpu.PrefetchScalarGrid...  16.3 us
    ppermute x3, waiting for transfers between devices, local(): lax.ppermute(own, 'patch', pairs(s))  12.5 us
    ppermute x3, waiting for transfers between devices, local(): lax.ppermute(chunks[k], 'patch', pairs(order[k]))  11.4 us
    ppermute x1, waiting for transfers between devices, local(): half = lax.ppermute(large, every, seconds)  6.09 us
    ppermute x1, starting transfers between devices, local(): relayed = lax.ppermute(back[n_qry:], 'head', swap)  4.18 us
    ppermute x1, starting transfers between devices, local(): near_out = lax.ppermute(for_other, 'head', swap)  3.65 us
    ppermute x3, starting transfers between devices, local(): lax.ppermute(own, 'patch', pairs(s))  3.44 us
    ppermute x1, waiting for transfers between devices, local(): lax.ppermute(tokens, 'view', rotate(n_view, s))  3.39 us
  transfers between devices with their start and end apart: 16, of which 11 were waited for; matrix products, arithmetic and copies ran while one was open for 2% of the time, Pallas kernels for 9%

profile of v5, /device:TPU:11, one launch (start us, length us, event | category | flops | bytes accessed | tf_op | source)
XLA Modules:
  0.0 77.5 jit_solution(9742534469147458761)
XLA Ops:
  0.0 0.7 collective-permute-start
  0.8 0.3 collective-permute-start.1
  1.0 0.1 stack.37.where
  1.1 0.6 copy-done
  1.7 0.0 copy-start.2
  1.7 0.0 copy-start.3
  1.8 1.6 %constant_dynamic-slice_fusion = (bf16[768,256]{1,0:T(8,128)(2,1)S(1)}, bf16[768,256]{1,0:T(8,128)(2,1)S(1)}, bf16[768,256]{1,0:T(8,128)(2,1)S(1)}, bf16[768,256]{1,0:T(8,128)(2,1)S(1)}) fusion(bf16[768,1536]{1,0:T(8,128)(2,1)} %param.9, s32[]{:T(128)S(6)} %select_n.59, s32[]{:T(128)S(6)} %select_n.54, s32[]{:T(128)S(6)} %select_n.53, s32[]{:T(128)S(6)} %select_n.58), kind=kLoop, calls=%fused_computation.5 | loop fusion | bytes 3145744 | tf_op jit(solution)/shard_map/dynamic_slice | solution.py:235
  3.4 0.0 collective-permute-done.refs_1_
  3.4 0.0 copy-done.4
  3.4 3.7 %shard_map.82 = (f32[3,256,256]{2,1,0:T(8,128)S(1)}, f32[3,128,256]{2,1,0:T(8,128)S(1)}) custom-call(s32[10]{0:T(128)S(1)} %stack.37.where, bf16[256,768]{1,0:T(8,128)(2,1)S(1)} %copy-done.4, bf16[256,768]{1,0:T(8,128)(2,1)S(1)} %collective-permute-done.refs_1_, bf16[3,768]{1,0:T(4,128)(2,1)S(1)} %copy-done.5, ...), custom_call_target="tpu_custom_call" | custom-call | tf_op jit(solution)/shard_map/pallas_call | solution.py:185
  7.1 1.1 %shard_map.83 = (bf16[256,256]{1,0:T(8,128)(2,1)S(1)}, bf16[512,256]{1,0:T(8,128)(2,1)S(1)}, bf16[256,256]{1,0:T(8,128)(2,1)S(1)}) custom-call(s32[10]{0:T(128)S(1)} %stack.37.where, bf16[256,768]{1,0:T(8,128)(2,1)S(1)} %copy-done.3, bf16[768,768]{1,0:T(8,128)(2,1)S(1)} %copy-done.2), custom_call_target="tpu_custom_call" | custom-call | tf_op jit(solution)/shard_map/pallas_call | solution.py:185
  8.3 3.4 %collective-permute-done.1.refs_0_ = bf16[256,768]{1,0:T(8,128)(2,1)S(1)} collective-permute-done((bf16[256,768]{1,0:T(8,128)(2,1)}, bf16[256,768]{1,0:T(8,128)(2,1)S(1)}, u32[]{:S(2)}, u32[]{:S(2)}) %collective-permute-start.1) | collective-permute-done | bytes 393248 | tf_op jit(solution)/shard_map/ppermute | solution.py:228
  11.7 0.8 %collective-permute-start.2 = (bf16[256,768]{1,0:T(8,128)(2,1)S(1)}, bf16[256,768]{1,0:T(8,128)(2,1)S(1)}, u32[]{:S(2)}, u32[]{:S(2)}) collective-permute-start(bf16[256,768]{1,0:T(8,128)(2,1)S(1)} %collective-permute-done.1.refs_0_), channel_id=1, source_target_pairs={{0,1},{1,0},{2,3},{3,2},{4,5},{5,4},{6,7},{7,6},{8,9},{9,8},{10,11... | collective-permute-start | bytes 1179656 | tf_op jit(solution)/shard_map/ppermute | solution.py:249
  12.5 1.3 %collective-permute-done.2.refs_1_ = bf16[256,768]{1,0:T(8,128)(2,1)S(1)} collective-permute-done((bf16[256,768]{1,0:T(8,128)(2,1)S(1)}, bf16[256,768]{1,0:T(8,128)(2,1)S(1)}, u32[]{:S(2)}, u32[]{:S(2)}) %collective-permute-start.2) | collective-permute-done | bytes 393248 | tf_op jit(solution)/shard_map/ppermute | solution.py:249
  13.9 3.7 %shard_map.84 = (f32[3,96,256]{2,1,0:T(8,128)S(1)}, bf16[3,96,256]{2,1,0:T(8,128)(2,1)S(1)}, bf16[3,96,256]{2,1,0:T(8,128)(2,1)S(1)}, bf16[3,96,256]{2,1,0:T(8,128)(2,1)S(1)}) custom-call(s32[10]{0:T(128)S(1)} %stack.37.where, bf16[256,768]{1,0:T(8,128)(2,1)S(1)} %collective-permute-done.1.refs_0_, bf16[256,768]{1,0:T(8,128)(2,1)S(1)} %collective-permute-done.2.refs_1_, ...), custom_call_target="tpu_custom_call" | custom-call | tf_op jit(solution)/shard_map/pallas_call | solution.py:185
  17.6 2.4 %collective-permute-start.6 = (bf16[3,96,256]{2,1,0:T(8,128)(2,1)S(1)}, bf16[3,96,256]{2,1,0:T(8,128)(2,1)S(1)}, u32[]{:S(2)}, u32[]{:S(2)}) collective-permute-start(bf16[3,96,256]{2,1,0:T(8,128)(2,1)S(1)} %get-tuple-element.41), channel_id=1, source_target_pairs={{0,8},{4,12},{8,0},{12,4},{1,9},{5,13},{9,1},{13,5},{2,10},{6,14},... | collective-permute-start | bytes 442376 | tf_op jit(solution)/shard_map/ppermute | solution.py:259
  20.0 0.2 collective-permute-start.5
  20.2 0.2 collective-permute-start.4
  20.4 1.2 %collective-permute-start.3 = (bf16[512,256]{1,0:T(8,128)(2,1)S(1)}, bf16[512,256]{1,0:T(8,128)(2,1)S(1)}, u32[]{:S(2)}, u32[]{:S(2)}) collective-permute-start(bf16[512,256]{1,0:T(8,128)(2,1)S(1)} %get-tuple-element.38), channel_id=1, source_target_pairs={{0,1},{1,0},{2,3},{3,2},{4,5},{5,4},{6,7},{7,6},{8,9},{9,8},{10,11... | collective-permute-start | bytes 786440 | tf_op jit(solution)/shard_map/ppermute | solution.py:267
  21.5 5.3 %collective-permute-done.6 = bf16[3,96,256]{2,1,0:T(8,128)(2,1)S(1)} collective-permute-done((bf16[3,96,256]{2,1,0:T(8,128)(2,1)S(1)}, bf16[3,96,256]{2,1,0:T(8,128)(2,1)S(1)}, u32[]{:S(2)}, u32[]{:S(2)}) %collective-permute-start.6) | collective-permute-done | bytes 147488 | tf_op jit(solution)/shard_map/ppermute | solution.py:259
  26.8 0.2 collective-permute-done.5
  27.0 6.0 %collective-permute-done.4 = bf16[3,96,256]{2,1,0:T(8,128)(2,1)S(1)} collective-permute-done((bf16[3,96,256]{2,1,0:T(8,128)(2,1)S(1)}, bf16[3,96,256]{2,1,0:T(8,128)(2,1)S(1)}, u32[]{:S(2)}, u32[]{:S(2)}) %collective-permute-start.4) | collective-permute-done | bytes 147488 | tf_op jit(solution)/shard_map/ppermute | solution.py:259
  32.9 0.1 add_convert_fusion.refs_0_
  33.0 0.1 collective-permute-start.7
  33.1 3.4 %collective-permute-start.8 = (bf16[3,96,256]{2,1,0:T(8,128)(2,1)S(1)}, bf16[3,96,256]{2,1,0:T(8,128)(2,1)S(1)}, u32[]{:S(2)}, u32[]{:S(2)}) collective-permute-start(bf16[3,96,256]{2,1,0:T(8,128)(2,1)S(1)} %add_convert_fusion.refs_0_), channel_id=1, source_target_pairs={{0,4},{4,0},{8,12},{12,8},{1,5},{5,1},{9,13},{13,9},{2,6},{6,2},{1... | collective-permute-start | bytes 442376 | tf_op jit(solution)/shard_map/ppermute | solution.py:264
  36.5 0.0 collective-permute-start.9
  36.5 2.5 %collective-permute-done.7.refs_1_ = bf16[3,96,256]{2,1,0:T(8,128)(2,1)S(1)} collective-permute-done((bf16[3,96,256]{2,1,0:T(8,128)(2,1)S(1)}, bf16[3,96,256]{2,1,0:T(8,128)(2,1)S(1)}, u32[]{:S(2)}, u32[]{:S(2)}) %collective-permute-start.7) | collective-permute-done | bytes 147488 | tf_op jit(solution)/shard_map/ppermute | solution.py:264
  39.0 4.2 %collective-permute-done.8.refs_2_ = bf16[3,96,256]{2,1,0:T(8,128)(2,1)S(1)} collective-permute-done((bf16[3,96,256]{2,1,0:T(8,128)(2,1)S(1)}, bf16[3,96,256]{2,1,0:T(8,128)(2,1)S(1)}, u32[]{:S(2)}, u32[]{:S(2)}) %collective-permute-start.8) | collective-permute-done | bytes 147488 | tf_op jit(solution)/shard_map/ppermute | solution.py:264
  43.2 5.8 %collective-permute-done.9.refs_3_ = bf16[3,96,256]{2,1,0:T(8,128)(2,1)S(1)} collective-permute-done((bf16[3,96,256]{2,1,0:T(8,128)(2,1)S(1)}, bf16[3,96,256]{2,1,0:T(8,128)(2,1)S(1)}, u32[]{:S(2)}, u32[]{:S(2)}) %collective-permute-start.9) | collective-permute-done | bytes 147488 | tf_op jit(solution)/shard_map/ppermute | solution.py:264
  49.0 0.6 shard_map.85
  49.6 0.0 copy-start.1
  49.6 2.3 %collective-permute-start.11 = (bf16[3,256,256]{2,1,0:T(8,128)(2,1)S(1)}, bf16[3,256,256]{2,1,0:T(8,128)(2,1)S(1)}, u32[]{:S(2)}, u32[]{:S(2)}) collective-permute-start(bf16[3,256,256]{2,1,0:T(8,128)(2,1)S(1)} %get-tuple-element.42.large), channel_id=1, source_target_pairs={{1,3},{3,1},{5,7},{7,5},{9,11},{11,9},{13,15},{15,13},{17,19},{19,... | collective-permute-start | bytes 1179656 | tf_op jit(solution)/shard_map/ppermute | solution.py:277
  51.9 0.0 collective-permute-done.3
  51.9 0.7 collective-permute-start.12
  52.6 1.0 %collective-permute-start.10 = (bf16[3,128,256]{2,1,0:T(8,128)(2,1)S(1)}, bf16[3,128,256]{2,1,0:T(8,128)(2,1)S(1)}, u32[]{:S(2)}, u32[]{:S(2)}) collective-permute-start(bf16[3,128,256]{2,1,0:T(8,128)(2,1)S(1)} %get-tuple-element.43.small), channel_id=1, source_target_pairs={{0,1},{1,0},{2,3},{3,2},{4,5},{5,4},{6,7},{7,6},{8,9},{9,8},{10,11... | collective-permute-start | bytes 589832 | tf_op jit(solution)/shard_map/ppermute | solution.py:276
  53.6 0.1 dynamic-slice_bitcast_fusion.fast
  53.7 1.0 %collective-permute-done.10.rest = bf16[3,128,256]{2,1,0:T(8,128)(2,1)S(1)} collective-permute-done((bf16[3,128,256]{2,1,0:T(8,128)(2,1)S(1)}, bf16[3,128,256]{2,1,0:T(8,128)(2,1)S(1)}, u32[]{:S(2)}, u32[]{:S(2)}) %collective-permute-start.10) | collective-permute-done | bytes 196640 | tf_op jit(solution)/shard_map/ppermute | solution.py:276
  54.7 0.0 collective-permute-done.12.qry
  54.7 6.1 %collective-permute-done.11.half = bf16[3,256,256]{2,1,0:T(8,128)(2,1)S(1)} collective-permute-done((bf16[3,256,256]{2,1,0:T(8,128)(2,1)S(1)}, bf16[3,256,256]{2,1,0:T(8,128)(2,1)S(1)}, u32[]{:S(2)}, u32[]{:S(2)}) %collective-permute-start.11) | collective-permute-done | bytes 393248 | tf_op jit(solution)/shard_map/ppermute | solution.py:277
  60.8 3.9 %shard_map.86 = (bf16[512,256]{1,0:T(8,128)(2,1)S(1)}, bf16[3,512,256]{2,1,0:T(8,128)(2,1)S(1)}) custom-call(s32[10]{0:T(128)S(1)} %stack.37.where, bf16[3,256,256]{2,1,0:T(8,128)(2,1)S(1)} %get-tuple-element.42.large, bf16[3,128,256]{2,1,0:T(8,128)(2,1)S(1)} %get-tuple-element.43.small, bf16[3,128,256]{2,1,0:T(8,128)(2,1)S(1)} %collective-permute-done.10.rest, ...), custom_call_target="tpu_custom_call" | custom-call | tf_op jit(solution)/shard_map/pallas_call | solution.py:185
  64.7 0.7 collective-permute-start.13
  65.4 1.6 %shard_map.87 = (bf16[256,256]{1,0:T(8,128)(2,1)S(1)}, f32[256,768]{1,0:T(8,128)S(1)}) custom-call(s32[10]{0:T(128)S(1)} %stack.37.where, bf16[256,256]{1,0:T(8,128)(2,1)S(1)} %get-tuple-element.30.own, bf16[256,256]{1,0:T(8,128)(2,1)S(1)} %get-tuple-element.56.other, bf16[3,512,256]{2,1,0:T(8,128)(2,1)S(1)} %get-tuple-element.45.fresh, ...), custom_call_target="tpu_custom_call" | custom-call | tf_op jit(solution)/shard_map/pallas_call | solution.py:185
  67.0 3.7 %collective-permute-start.14 = (bf16[256,256]{1,0:T(8,128)(2,1)S(1)}, bf16[256,256]{1,0:T(8,128)(2,1)S(1)}, u32[]{:S(2)}, u32[]{:S(2)}) collective-permute-start(bf16[256,256]{1,0:T(8,128)(2,1)S(1)} %get-tuple-element.49), channel_id=1, source_target_pairs={{0,1},{1,0},{2,3},{3,2},{4,5},{5,4},{6,7},{7,6},{8,9},{9,8},{10,11... | collective-permute-start | bytes 393224 | tf_op jit(solution)/shard_map/ppermute | solution.py:293
  70.6 0.0 collective-permute-done.13.back
  70.7 4.2 %collective-permute-start.15 = (bf16[256,256]{1,0:T(8,128)(2,1)S(1)}, bf16[256,256]{1,0:T(8,128)(2,1)S(1)}, u32[]{:S(2)}, u32[]{:S(2)}) collective-permute-start(bf16[256,256]{1,0:T(8,128)(2,1)S(1)} %slice.11), channel_id=1, source_target_pairs={{0,1},{1,0},{2,3},{3,2},{4,5},{5,4},{6,7},{7,6},{8,9},{9,8},{10,11... | collective-permute-start | bytes 393224 | tf_op jit(solution)/shard_map/ppermute | solution.py:295
  74.8 0.0 collective-permute-done.14.near
  74.8 1.0 %collective-permute-done.15.relayed = bf16[256,256]{1,0:T(8,128)(2,1)S(1)} collective-permute-done((bf16[256,256]{1,0:T(8,128)(2,1)S(1)}, bf16[256,256]{1,0:T(8,128)(2,1)S(1)}, u32[]{:S(2)}, u32[]{:S(2)}) %collective-permute-start.15) | collective-permute-done | bytes 131104 | tf_op jit(solution)/shard_map/ppermute | solution.py:295
  75.8 1.7 %shard_map.88 = bf16[256,768]{1,0:T(8,128)(2,1)} custom-call(s32[10]{0:T(128)S(1)} %stack.37.where, f32[256,768]{1,0:T(8,128)S(1)} %get-tuple-element.48.begun, bf16[256,256]{1,0:T(8,128)(2,1)S(1)} %collective-permute-done.14.near, bf16[512,256]{1,0:T(8,128)(2,1)S(1)} %collective-permute-done.13.back, bf16[256,256]{1,0:T(8,128)(2,1)S(1)} %collective-permute-done.15.relayed, ...), custom_call_target="tpu_custom_call" | custom-call | tf_op jit(solution)/shard_map/pallas_call | solution.py:185
  (15 shorter events, 0.1 us)
Async XLA Ops:
  0.0 1.7 %copy-start = (bf16[512,3,3,256]{3,0,2,1:T(8,128)(2,1)S(1)}, bf16[512,3,3,256]{3,0,2,1:T(8,128)(2,1)}, u32[]{:S(2)}) copy-start(bf16[512,3,3,256]{3,0,2,1:T(8,128)(2,1)} %param.11) | copy-start | bytes 7077892
  0.0 3.4 %copy-start.4 = (bf16[256,768]{1,0:T(8,128)(2,1)S(1)}, bf16[256,768]{1,0:T(8,128)(2,1)}, u32[]{:S(2)}) copy-start(bf16[256,768]{1,0:T(8,128)(2,1)} %refs_0_.1) | copy-start | bytes 1179652
  0.0 3.4 %copy-start.5 = (bf16[3,768]{1,0:T(4,128)(2,1)S(1)}, bf16[3,768]{1,0:T(4,128)(2,1)}, u32[]{:S(2)}) copy-start(bf16[3,768]{1,0:T(4,128)(2,1)} %refs_2_.3) | copy-start | bytes 13828
  0.0 3.3 %collective-permute-start = (bf16[256,768]{1,0:T(8,128)(2,1)}, bf16[256,768]{1,0:T(8,128)(2,1)S(1)}, u32[]{:S(2)}, u32[]{:S(2)}) collective-permute-start(bf16[256,768]{1,0:T(8,128)(2,1)} %refs_0_.1), channel_id=1, source_target_pairs={{0,1},{1,0},{2,3},{3,2},{4,5},{5,4},{6,7},{7,6},{8,9},{9,8},{10,11... | collective-permute-start | bytes 1179656 | tf_op jit(solution)/shard_map/ppermute | solution.py:229
  0.8 10.9 %collective-permute-start.1 = (bf16[256,768]{1,0:T(8,128)(2,1)}, bf16[256,768]{1,0:T(8,128)(2,1)S(1)}, u32[]{:S(2)}, u32[]{:S(2)}) collective-permute-start(bf16[256,768]{1,0:T(8,128)(2,1)} %refs_0_.1), channel_id=1, source_target_pairs={{0,2},{2,0},{1,3},{3,1},{4,6},{6,4},{5,7},{7,5},{8,10},{10,8},{9,1... | collective-permute-start | bytes 1179656 | tf_op jit(solution)/shard_map/ppermute | solution.py:228
  1.7 5.4 %copy-start.2 = (bf16[768,768]{1,0:T(8,128)(2,1)S(1)}, bf16[768,768]{1,0:T(8,128)(2,1)}, u32[]{:S(2)}) copy-start(bf16[768,768]{1,0:T(8,128)(2,1)} %w_query.1) | copy-start | bytes 3538948
  1.7 5.4 %copy-start.3 = (bf16[256,768]{1,0:T(8,128)(2,1)S(1)}, bf16[256,768]{1,0:T(8,128)(2,1)}, u32[]{:S(2)}) copy-start(bf16[256,768]{1,0:T(8,128)(2,1)} %queries) | copy-start | bytes 1179652
  11.7 2.2 %collective-permute-start.2 = (bf16[256,768]{1,0:T(8,128)(2,1)S(1)}, bf16[256,768]{1,0:T(8,128)(2,1)S(1)}, u32[]{:S(2)}, u32[]{:S(2)}) collective-permute-start(bf16[256,768]{1,0:T(8,128)(2,1)S(1)} %collective-permute-done.1.refs_0_), channel_id=1, source_target_pairs={{0,1},{1,0},{2,3},{3,2},{4,5},{5,4},{6,7},{7,6},{8,9},{9,8},{10,11... | collective-permute-start | bytes 1179656 | tf_op jit(solution)/shard_map/ppermute | solution.py:249
  13.9 39.8 %copy-start.6 = (bf16[768]{0:T(1024)(128)(2,1)S(1)}, bf16[768]{0:T(1024)(128)(2,1)}, u32[]{:S(2)}) copy-start(bf16[768]{0:T(1024)(128)(2,1)} %param.14) | copy-start | bytes 4612
  17.6 9.2 %collective-permute-start.6 = (bf16[3,96,256]{2,1,0:T(8,128)(2,1)S(1)}, bf16[3,96,256]{2,1,0:T(8,128)(2,1)S(1)}, u32[]{:S(2)}, u32[]{:S(2)}) collective-permute-start(bf16[3,96,256]{2,1,0:T(8,128)(2,1)S(1)} %get-tuple-element.41), channel_id=1, source_target_pairs={{0,8},{4,12},{8,0},{12,4},{1,9},{5,13},{9,1},{13,5},{2,10},{6,14},... | collective-permute-start | bytes 442376 | tf_op jit(solution)/shard_map/ppermute | solution.py:259
  20.0 7.0 %collective-permute-start.5 = (bf16[3,96,256]{2,1,0:T(8,128)(2,1)S(1)}, bf16[3,96,256]{2,1,0:T(8,128)(2,1)S(1)}, u32[]{:S(2)}, u32[]{:S(2)}) collective-permute-start(bf16[3,96,256]{2,1,0:T(8,128)(2,1)S(1)} %get-tuple-element.40), channel_id=1, source_target_pairs={{0,4},{4,0},{8,12},{12,8},{1,5},{5,1},{9,13},{13,9},{2,6},{6,2},{1... | collective-permute-start | bytes 442376 | tf_op jit(solution)/shard_map/ppermute | solution.py:259
  20.2 12.8 %collective-permute-start.4 = (bf16[3,96,256]{2,1,0:T(8,128)(2,1)S(1)}, bf16[3,96,256]{2,1,0:T(8,128)(2,1)S(1)}, u32[]{:S(2)}, u32[]{:S(2)}) collective-permute-start(bf16[3,96,256]{2,1,0:T(8,128)(2,1)S(1)} %get-tuple-element.39), channel_id=1, source_target_pairs={{0,12},{4,8},{8,4},{12,0},{1,13},{5,9},{9,5},{13,1},{2,14},{6,10},... | collective-permute-start | bytes 442376 | tf_op jit(solution)/shard_map/ppermute | solution.py:259
  20.4 31.5 %collective-permute-start.3 = (bf16[512,256]{1,0:T(8,128)(2,1)S(1)}, bf16[512,256]{1,0:T(8,128)(2,1)S(1)}, u32[]{:S(2)}, u32[]{:S(2)}) collective-permute-start(bf16[512,256]{1,0:T(8,128)(2,1)S(1)} %get-tuple-element.38), channel_id=1, source_target_pairs={{0,1},{1,0},{2,3},{3,2},{4,5},{5,4},{6,7},{7,6},{8,9},{9,8},{10,11... | collective-permute-start | bytes 786440 | tf_op jit(solution)/shard_map/ppermute | solution.py:267
  33.0 5.9 %collective-permute-start.7 = (bf16[3,96,256]{2,1,0:T(8,128)(2,1)S(1)}, bf16[3,96,256]{2,1,0:T(8,128)(2,1)S(1)}, u32[]{:S(2)}, u32[]{:S(2)}) collective-permute-start(bf16[3,96,256]{2,1,0:T(8,128)(2,1)S(1)} %add_convert_fusion.refs_0_), channel_id=1, source_target_pairs={{0,8},{4,12},{8,0},{12,4},{1,9},{5,13},{9,1},{13,5},{2,10},{6,14},... | collective-permute-start | bytes 442376 | tf_op jit(solution)/shard_map/ppermute | solution.py:264
  33.1 10.1 %collective-permute-start.8 = (bf16[3,96,256]{2,1,0:T(8,128)(2,1)S(1)}, bf16[3,96,256]{2,1,0:T(8,128)(2,1)S(1)}, u32[]{:S(2)}, u32[]{:S(2)}) collective-permute-start(bf16[3,96,256]{2,1,0:T(8,128)(2,1)S(1)} %add_convert_fusion.refs_0_), channel_id=1, source_target_pairs={{0,4},{4,0},{8,12},{12,8},{1,5},{5,1},{9,13},{13,9},{2,6},{6,2},{1... | collective-permute-start | bytes 442376 | tf_op jit(solution)/shard_map/ppermute | solution.py:264
  36.5 12.5 %collective-permute-start.9 = (bf16[3,96,256]{2,1,0:T(8,128)(2,1)S(1)}, bf16[3,96,256]{2,1,0:T(8,128)(2,1)S(1)}, u32[]{:S(2)}, u32[]{:S(2)}) collective-permute-start(bf16[3,96,256]{2,1,0:T(8,128)(2,1)S(1)} %add_convert_fusion.refs_0_), channel_id=1, source_target_pairs={{0,12},{4,8},{8,4},{12,0},{1,13},{5,9},{9,5},{13,1},{2,14},{6,10},... | collective-permute-start | bytes 442376 | tf_op jit(solution)/shard_map/ppermute | solution.py:264
  49.6 15.8 %copy-start.1 = (bf16[768,768]{1,0:T(8,128)(2,1)S(1)}, bf16[768,768]{1,0:T(8,128)(2,1)}, u32[]{:S(2)}) copy-start(bf16[768,768]{1,0:T(8,128)(2,1)} %w_out.3) | copy-start | bytes 3538948
  49.6 11.2 %collective-permute-start.11 = (bf16[3,256,256]{2,1,0:T(8,128)(2,1)S(1)}, bf16[3,256,256]{2,1,0:T(8,128)(2,1)S(1)}, u32[]{:S(2)}, u32[]{:S(2)}) collective-permute-start(bf16[3,256,256]{2,1,0:T(8,128)(2,1)S(1)} %get-tuple-element.42.large), channel_id=1, source_target_pairs={{1,3},{3,1},{5,7},{7,5},{9,11},{11,9},{13,15},{15,13},{17,19},{19,... | collective-permute-start | bytes 1179656 | tf_op jit(solution)/shard_map/ppermute | solution.py:277
  51.9 2.8 %collective-permute-start.12 = (bf16[512,256]{1,0:T(8,128)(2,1)S(1)}, bf16[512,256]{1,0:T(8,128)(2,1)S(1)}, u32[]{:S(2)}, u32[]{:S(2)}) collective-permute-start(bf16[512,256]{1,0:T(8,128)(2,1)S(1)} %pad_maximum_fusion), channel_id=1, source_target_pairs={{0,2},{2,0},{4,6},{6,4},{8,10},{10,8},{12,14},{14,12},{16,18},{18,... | collective-permute-start | bytes 786440 | tf_op jit(solution)/shard_map/ppermute | solution.py:268
  52.6 2.1 %collective-permute-start.10 = (bf16[3,128,256]{2,1,0:T(8,128)(2,1)S(1)}, bf16[3,128,256]{2,1,0:T(8,128)(2,1)S(1)}, u32[]{:S(2)}, u32[]{:S(2)}) collective-permute-start(bf16[3,128,256]{2,1,0:T(8,128)(2,1)S(1)} %get-tuple-element.43.small), channel_id=1, source_target_pairs={{0,1},{1,0},{2,3},{3,2},{4,5},{5,4},{6,7},{7,6},{8,9},{9,8},{10,11... | collective-permute-start | bytes 589832 | tf_op jit(solution)/shard_map/ppermute | solution.py:276
  64.7 6.0 %collective-permute-start.13 = (bf16[512,256]{1,0:T(8,128)(2,1)S(1)}, bf16[512,256]{1,0:T(8,128)(2,1)S(1)}, u32[]{:S(2)}, u32[]{:S(2)}) collective-permute-start(bf16[512,256]{1,0:T(8,128)(2,1)S(1)} %get-tuple-element.47), channel_id=1, source_target_pairs={{0,2},{2,0},{4,6},{6,4},{8,10},{10,8},{12,14},{14,12},{16,18},{18,... | collective-permute-start | bytes 786440 | tf_op jit(solution)/shard_map/ppermute | solution.py:286
  67.0 7.9 %collective-permute-start.14 = (bf16[256,256]{1,0:T(8,128)(2,1)S(1)}, bf16[256,256]{1,0:T(8,128)(2,1)S(1)}, u32[]{:S(2)}, u32[]{:S(2)}) collective-permute-start(bf16[256,256]{1,0:T(8,128)(2,1)S(1)} %get-tuple-element.49), channel_id=1, source_target_pairs={{0,1},{1,0},{2,3},{3,2},{4,5},{5,4},{6,7},{7,6},{8,9},{9,8},{10,11... | collective-permute-start | bytes 393224 | tf_op jit(solution)/shard_map/ppermute | solution.py:293
  70.7 5.2 %collective-permute-start.15 = (bf16[256,256]{1,0:T(8,128)(2,1)S(1)}, bf16[256,256]{1,0:T(8,128)(2,1)S(1)}, u32[]{:S(2)}, u32[]{:S(2)}) collective-permute-start(bf16[256,256]{1,0:T(8,128)(2,1)S(1)} %slice.11), channel_id=1, source_target_pairs={{0,1},{1,0},{2,3},{3,2},{4,5},{5,4},{6,7},{7,6},{8,9},{9,8},{10,11... | collective-permute-start | bytes 393224 | tf_op jit(solution)/shard_map/ppermute | solution.py:295

commit v6 on v5

--- a/solution.py
+++ b/solution.py
@@ -25,8 +25,10 @@
 SMALL = FF // 4
 
 
-def exchange_order(n_patch):
-    return [0, 2, 1, 3, *range(4, n_patch)] if n_patch > 3 else [*range(n_patch)]
+def exchange_order(n_patch, back=False):
+    if n_patch < 4:
+        return [*range(n_patch)]
+    return [0, *((2, 1, 3) if back else (3, 1, 2)), *range(4, n_patch)]
 
 
 def mm(a, b, dims=(((1,), (0,)), ((), ()))):
@@ -37,14 +39,16 @@
     return raw * lax.rsqrt(jnp.sum(raw * raw, -1, keepdims=True) + eps_small)
 
 
-def add_gradient(rows, segment, acc):
-    head, w_k, w_v, w_rate, fast = segment
-    keys = unit(mm(rows, w_k[...])).astype(BF)
+def project(rows, head, w_k, w_v, w_rate, keys, scaled):
+    keys[...] = unit(mm(rows, w_k[...])).astype(BF)
     rates = mm(rows, w_rate[...], NT)
     pick = lax.broadcasted_iota(jnp.int32, rates.shape, 1) == head
     rate = jnp.sum(jnp.where(pick, rates, 0.0), -1, keepdims=True)
     rate = jnp.maximum(rate, 0.0) + jnp.log1p(jnp.exp(-jnp.abs(rate)))
-    scaled = (rate * mm(rows, w_v[...])).astype(BF)
+    scaled[...] = (rate * mm(rows, w_v[...])).astype(BF)
+
+
+def add_gradient(keys, scaled, fast, acc):
     gate_pre = mm(fast[0], keys, NT)
     up_pre = mm(fast[1], keys, NT)
     back = mm(fast[2], scaled, NT)
@@ -58,28 +62,37 @@
     acc[2] += mm(hidden, scaled)
 
 
-def add_segments(where, toks, weights, accs):
+def add_segments(where, toks, weights, accs, keys, scaled):
     w_rate, *weights = weights
-    for i, acc in enumerate(accs):
-        w_k, w_v, fast = weights[3 * i : 3 * i + 3]
-        for tok in toks:
-            for at in range(0, tok.shape[0], HD):
-                add_gradient(tok[at : at + HD], (where[6 + i], w_k, w_v, w_rate, fast), acc)
+    large, small = weights[:3], weights[3:]
+    both = [(tok, at) for tok in toks for at in range(0, tok.shape[0], HD)]
+    for i, (tok, at) in enumerate(both):
+        rows = tok[at : at + HD]
+        project(rows, where[6], *large[:2], w_rate, keys.at[i], scaled.at[i])
+        add_gradient(keys[i], scaled[i], large[2], accs[0])
+
+    @pl.when(where[8] != 0)
+    def _():
+        for i, (tok, at) in enumerate(both):
+            project(tok[at : at + HD], where[7], *small[:2], w_rate, keys.at[i], scaled.at[i])
+
+    for i in range(len(both)):
+        add_gradient(keys[i], scaled[i], small[2], accs[1])
 
 
 def first_kernel(n_tok, where, *refs):
-    toks, weights, accs = refs[:n_tok], refs[n_tok:-2], refs[-2:]
+    toks, weights, accs, rows = refs[:n_tok], refs[n_tok:-4], refs[-4:-2], refs[-2:]
     for acc in accs:
         acc[...] = jnp.zeros_like(acc)
-    add_segments(where, toks, weights, accs)
+    add_segments(where, toks, weights, accs, *rows)
 
 
 def second_kernel(n_tok, n_patch, where, *refs):
     toks, weights, begun = refs[:n_tok], refs[n_tok : n_tok + 7], refs[n_tok + 7 : n_tok + 9]
-    outs, accs = refs[n_tok + 9 : -2], refs[-2:]
+    outs, accs, rows = refs[n_tok + 9 : -4], refs[-4:-2], refs[-2:]
     for acc, part in zip(accs, begun):
         acc[...] = part[...]
-    add_segments(where, toks, weights, accs)
+    add_segments(where, toks, weights, accs, *rows)
     for out, shift in zip(outs, exchange_order(n_patch)):
         chunk = where[1] ^ shift
         at = 0
@@ -91,7 +104,7 @@
 
 def collect_kernel(n_patch, where, *refs):
     parts, segments = refs[:n_patch], refs[n_patch:]
-    for part, shift in zip(parts, exchange_order(n_patch)):
+    for part, shift in zip(parts, exchange_order(n_patch, True)):
         chunk = where[1] ^ shift
         at = 0
         for segment in segments:
@@ -236,7 +249,11 @@
         piece = lax.dynamic_slice(fast_weights, (unit_at, 0, owner, 0), (size, 3, 1, HD))
         weights.append(piece.reshape(size, 3, HD).transpose(1, 0, 2))
     sums = [jax.ShapeDtypeStruct((3, size, HD), FP) for size in (LARGE, SMALL)]
-    begun = list(call(functools.partial(first_kernel, len(near)), where, near + weights, sums))
+
+    def held(toks):
+        return [pltpu.VMEM((len(toks) * n_tok // HD, HD, HD), BF)] * 2
+
+    begun = list(call(functools.partial(first_kernel, len(near)), where, near + weights, sums, held(near)))
     late, _ = lax.optimization_barrier((queries, begun[0]))
     own_qry, message, other = call(
         query_kernel,
@@ -247,26 +264,26 @@
     )
     begun[0], message, *far = lax.optimization_barrier((begun[0], message, *far))
     far = far + [lax.ppermute(f, "head", swap) for f in far]
+    message, far[-1] = lax.optimization_barrier((message, far[-1]))
+    swapped = lax.ppermute(message, "head", swap)
     size = (LARGE + SMALL) // n_patch
     chunks = call(
         functools.partial(second_kernel, len(far), n_patch),
         where,
         far + weights + begun,
         [jax.ShapeDtypeStruct((3, size, HD), BF if k else FP) for k in range(n_patch)],
-        [pltpu.VMEM(s.shape, FP) for s in sums],
+        [pltpu.VMEM(s.shape, FP) for s in sums] + held(far),
     )
     order = exchange_order(n_patch)
     got = [lax.ppermute(chunks[k], "patch", pairs(order[k])) for k in range(n_patch - 1, 0, -1)]
     own = chunks[0]
     for part in got:
         own = own + part.astype(FP)
+    other, swapped, _ = lax.optimization_barrier((other, swapped, chunks[0]))
+    across = lax.ppermute(jnp.concatenate([other, swapped[n_qry:]]), every, ours)
     own = own.astype(BF)
-    parts = [lax.ppermute(own, "patch", pairs(s)) for s in exchange_order(n_patch)[1:]]
-
-    message, other, _ = lax.optimization_barrier((message, other, chunks[0]))
-    swapped = lax.ppermute(message, "head", swap)
-    across = lax.ppermute(jnp.concatenate([other, swapped[n_qry:]]), every, ours)
-
+    parts = [lax.ppermute(own, "patch", pairs(s)) for s in exchange_order(n_patch, True)[1:]]
+    parts[0], across = lax.optimization_barrier((parts[0], across))
     large, small = call(
         functools.partial(collect_kernel, n_patch),
         where,
@@ -274,6 +291,7 @@
         [jax.ShapeDtypeStruct(s.shape, BF) for s in sums],
     )
     rest = lax.ppermute(small, "head", swap)
+    large, rest = lax.optimization_barrier((large, rest))
     half = lax.ppermute(large, every, seconds)
     gains = out_gain.reshape(1, width)
     normed, fresh = call(

time: 77.7 us -> 69.8 us (0.90)
  starting transfers between devices: 21.7 us -> 13.7 us
    ppermute x1, starting transfers between devices: 4.18 us -> 0.55 us  [local(): relayed = lax.ppermute(back[n_qry:], 'head', swap)]
    ppermute x1, starting transfers between devices: 3.65 us -> 0.07 us  [local(): near_out = lax.ppermute(for_other, 'head', swap)]
    ppermute x3, waiting for transfers between devices: 11.4 us -> 9.99 us  [local(): lax.ppermute(chunks[k], 'patch', pairs(order[k]))]
    ppermute x3, waiting for transfers between devices: 12.5 us -> 13.5 us  [local(): lax.ppermute(own, 'patch', pairs(s))]
    ppermute x3, starting transfers between devices: 2.74 us -> 3.56 us  [local(): lax.ppermute(chunks[k], 'patch', pairs(order[k]))]
    ppermute x1, starting transfers between devices: 1.19 us -> 0.37 us  [local(): swapped = lax.ppermute(message, 'head', swap)]
  transfers between devices with their start and end apart: 16 -> 16, of which waited for: 11 -> 12; matrix products, arithmetic and copies ran while one was open for 2% -> 3% of each run, Pallas kernels for 9% -> 15%
where the time goes in v6:
time: 69.8 us; the launch traced here: 69.6 us
  waiting for transfers between devices  36.3 us (52%)
  Pallas kernels  16.8 us (24%)
  starting transfers between devices  13.7 us (20%)
  local copies, waits for them, and re-layouts  2.42 us (3%)
    pallas_call x7, Pallas kernels, call(): pl.pallas_call(kernel, out_shape=outs, grid_spec=pltpu.PrefetchScalarGrid...  16.8 us
    ppermute x3, waiting for transfers between devices, local(): lax.ppermute(own, 'patch', pairs(s))  13.5 us
    ppermute x3, waiting for transfers between devices, local(): lax.ppermute(chunks[k], 'patch', pairs(order[k]))  9.99 us
    ppermute x1, waiting for transfers between devices, local(): half = lax.ppermute(large, every, seconds)  6.27 us
    ppermute x3, starting transfers between devices, local(): lax.ppermute(chunks[k], 'patch', pairs(order[k]))  3.56 us
    ppermute x3, starting transfers between devices, local(): lax.ppermute(own, 'patch', pairs(s))  3.26 us
    ppermute x1, waiting for transfers between devices, local(): lax.ppermute(tokens, 'view', rotate(n_view, s))  3.15 us
    ppermute x1, starting transfers between devices, local(): half = lax.ppermute(large, every, seconds)  2.14 us
  transfers between devices with their start and end apart: 16, of which 12 were waited for; matrix products, arithmetic and copies ran while one was open for 3% of the time, Pallas kernels for 15%

profile of v6, /device:TPU:11, one launch (start us, length us, event | category | flops | bytes accessed | tf_op | source)
XLA Modules:
  0.0 69.6 jit_solution(12606765025871058819)
XLA Ops:
  0.0 0.0 copy-start
  0.0 0.7 %collective-permute-start = (bf16[256,768]{1,0:T(8,128)(2,1)}, bf16[256,768]{1,0:T(8,128)(2,1)S(1)}, u32[]{:S(2)}, u32[]{:S(2)}) collective-permute-start(bf16[256,768]{1,0:T(8,128)(2,1)} %refs_0_.1), channel_id=1, source_target_pairs={{0,1},{1,0},{2,3},{3,2},{4,5},{5,4},{6,7},{7,6},{8,9},{9,8},{10,11... | collective-permute-start | bytes 1179656 | tf_op jit(solution)/shard_map/ppermute | solution.py:242
  0.8 0.3 collective-permute-start.1
  1.0 0.1 stack.37.where
  1.1 0.6 copy-done
  1.7 0.0 copy-start.2
  1.7 0.0 copy-start.3
  1.8 1.6 %constant_dynamic-slice_fusion = (bf16[768,256]{1,0:T(8,128)(2,1)S(1)}, bf16[768,256]{1,0:T(8,128)(2,1)S(1)}, bf16[768,256]{1,0:T(8,128)(2,1)S(1)}, bf16[768,256]{1,0:T(8,128)(2,1)S(1)}) fusion(bf16[768,1536]{1,0:T(8,128)(2,1)} %param.9, s32[]{:T(128)S(6)} %select_n.59, s32[]{:T(128)S(6)} %select_n.54, s32[]{:T(128)S(6)} %select_n.53, s32[]{:T(128)S(6)} %select_n.58), kind=kLoop, calls=%fused_computation.5 | loop fusion | bytes 3145744 | tf_op jit(solution)/shard_map/dynamic_slice | solution.py:248
  3.4 0.0 collective-permute-done.refs_1_
  3.4 4.0 %shard_map.82 = (f32[3,256,256]{2,1,0:T(8,128)S(1)}, f32[3,128,256]{2,1,0:T(8,128)S(1)}) custom-call(s32[10]{0:T(128)S(1)} %stack.37.where, bf16[256,768]{1,0:T(8,128)(2,1)S(1)} %copy-done.4, bf16[256,768]{1,0:T(8,128)(2,1)S(1)} %collective-permute-done.refs_1_, bf16[3,768]{1,0:T(4,128)(2,1)S(1)} %copy-done.5, ...), custom_call_target="tpu_custom_call" | custom-call | tf_op jit(solution)/shard_map/pallas_call | solution.py:198
  7.4 1.1 %shard_map.83 = (bf16[256,256]{1,0:T(8,128)(2,1)S(1)}, bf16[512,256]{1,0:T(8,128)(2,1)S(1)}, bf16[256,256]{1,0:T(8,128)(2,1)S(1)}) custom-call(s32[10]{0:T(128)S(1)} %stack.37.where, bf16[256,768]{1,0:T(8,128)(2,1)S(1)} %copy-done.3, bf16[768,768]{1,0:T(8,128)(2,1)S(1)} %copy-done.2), custom_call_target="tpu_custom_call" | custom-call | tf_op jit(solution)/shard_map/pallas_call | solution.py:198
  8.5 3.1 %collective-permute-done.1.refs_0_ = bf16[256,768]{1,0:T(8,128)(2,1)S(1)} collective-permute-done((bf16[256,768]{1,0:T(8,128)(2,1)}, bf16[256,768]{1,0:T(8,128)(2,1)S(1)}, u32[]{:S(2)}, u32[]{:S(2)}) %collective-permute-start.1) | collective-permute-done | bytes 393248 | tf_op jit(solution)/shard_map/ppermute | solution.py:241
  11.7 0.8 %collective-permute-start.2 = (bf16[256,768]{1,0:T(8,128)(2,1)S(1)}, bf16[256,768]{1,0:T(8,128)(2,1)S(1)}, u32[]{:S(2)}, u32[]{:S(2)}) collective-permute-start(bf16[256,768]{1,0:T(8,128)(2,1)S(1)} %collective-permute-done.1.refs_0_), channel_id=1, source_target_pairs={{0,1},{1,0},{2,3},{3,2},{4,5},{5,4},{6,7},{7,6},{8,9},{9,8},{10,11... | collective-permute-start | bytes 1179656 | tf_op jit(solution)/shard_map/ppermute | solution.py:266
  12.5 1.3 %collective-permute-done.2.refs_1_ = bf16[256,768]{1,0:T(8,128)(2,1)S(1)} collective-permute-done((bf16[256,768]{1,0:T(8,128)(2,1)S(1)}, bf16[256,768]{1,0:T(8,128)(2,1)S(1)}, u32[]{:S(2)}, u32[]{:S(2)}) %collective-permute-start.2) | collective-permute-done | bytes 393248 | tf_op jit(solution)/shard_map/ppermute | solution.py:266
  13.9 0.4 collective-permute-start.3
  14.2 4.0 %shard_map.84 = (f32[3,96,256]{2,1,0:T(8,128)S(1)}, bf16[3,96,256]{2,1,0:T(8,128)(2,1)S(1)}, bf16[3,96,256]{2,1,0:T(8,128)(2,1)S(1)}, bf16[3,96,256]{2,1,0:T(8,128)(2,1)S(1)}) custom-call(s32[10]{0:T(128)S(1)} %stack.37.where, bf16[256,768]{1,0:T(8,128)(2,1)S(1)} %collective-permute-done.1.refs_0_, bf16[256,768]{1,0:T(8,128)(2,1)S(1)} %collective-permute-done.2.refs_1_, ...), custom_call_target="tpu_custom_call" | custom-call | tf_op jit(solution)/shard_map/pallas_call | solution.py:198
  18.2 1.4 %collective-permute-start.6 = (bf16[3,96,256]{2,1,0:T(8,128)(2,1)S(1)}, bf16[3,96,256]{2,1,0:T(8,128)(2,1)S(1)}, u32[]{:S(2)}, u32[]{:S(2)}) collective-permute-start(bf16[3,96,256]{2,1,0:T(8,128)(2,1)S(1)} %get-tuple-element.49), channel_id=1, source_target_pairs={{0,12},{4,8},{8,4},{12,0},{1,13},{5,9},{9,5},{13,1},{2,14},{6,10},... | collective-permute-start | bytes 442376 | tf_op jit(solution)/shard_map/ppermute | solution.py:278
  19.6 2.2 %collective-permute-start.5 = (bf16[3,96,256]{2,1,0:T(8,128)(2,1)S(1)}, bf16[3,96,256]{2,1,0:T(8,128)(2,1)S(1)}, u32[]{:S(2)}, u32[]{:S(2)}) collective-permute-start(bf16[3,96,256]{2,1,0:T(8,128)(2,1)S(1)} %get-tuple-element.48), channel_id=1, source_target_pairs={{0,4},{4,0},{8,12},{12,8},{1,5},{5,1},{9,13},{13,9},{2,6},{6,2},{1... | collective-permute-start | bytes 442376 | tf_op jit(solution)/shard_map/ppermute | solution.py:278
  21.8 0.0 collective-permute-start.4
  21.8 0.0 collective-permute-done.3
  21.9 0.7 collective-permute-start.8
  22.5 4.8 %collective-permute-done.6 = bf16[3,96,256]{2,1,0:T(8,128)(2,1)S(1)} collective-permute-done((bf16[3,96,256]{2,1,0:T(8,128)(2,1)S(1)}, bf16[3,96,256]{2,1,0:T(8,128)(2,1)S(1)}, u32[]{:S(2)}, u32[]{:S(2)}) %collective-permute-start.6) | collective-permute-done | bytes 147488 | tf_op jit(solution)/shard_map/ppermute | solution.py:278
  27.3 2.1 %collective-permute-done.5 = bf16[3,96,256]{2,1,0:T(8,128)(2,1)S(1)} collective-permute-done((bf16[3,96,256]{2,1,0:T(8,128)(2,1)S(1)}, bf16[3,96,256]{2,1,0:T(8,128)(2,1)S(1)}, u32[]{:S(2)}, u32[]{:S(2)}) %collective-permute-start.5) | collective-permute-done | bytes 147488 | tf_op jit(solution)/shard_map/ppermute | solution.py:278
  29.4 3.1 %collective-permute-done.4 = bf16[3,96,256]{2,1,0:T(8,128)(2,1)S(1)} collective-permute-done((bf16[3,96,256]{2,1,0:T(8,128)(2,1)S(1)}, bf16[3,96,256]{2,1,0:T(8,128)(2,1)S(1)}, u32[]{:S(2)}, u32[]{:S(2)}) %collective-permute-start.4) | collective-permute-done | bytes 147488 | tf_op jit(solution)/shard_map/ppermute | solution.py:278
  32.5 0.1 add_convert_fusion.refs_0_
  32.6 0.0 copy-start.1
  32.6 2.9 %collective-permute-start.7 = (bf16[3,96,256]{2,1,0:T(8,128)(2,1)S(1)}, bf16[3,96,256]{2,1,0:T(8,128)(2,1)S(1)}, u32[]{:S(2)}, u32[]{:S(2)}) collective-permute-start(bf16[3,96,256]{2,1,0:T(8,128)(2,1)S(1)} %add_convert_fusion.refs_0_), channel_id=1, source_target_pairs={{0,8},{4,12},{8,0},{12,4},{1,9},{5,13},{9,1},{13,5},{2,10},{6,14},... | collective-permute-start | bytes 442376 | tf_op jit(solution)/shard_map/ppermute | solution.py:285
  35.5 0.0 collective-permute-start.9
  35.5 0.4 collective-permute-start.10
  35.9 5.4 %collective-permute-done.7.refs_1_ = bf16[3,96,256]{2,1,0:T(8,128)(2,1)S(1)} collective-permute-done((bf16[3,96,256]{2,1,0:T(8,128)(2,1)S(1)}, bf16[3,96,256]{2,1,0:T(8,128)(2,1)S(1)}, u32[]{:S(2)}, u32[]{:S(2)}) %collective-permute-start.7) | collective-permute-done | bytes 147488 | tf_op jit(solution)/shard_map/ppermute | solution.py:285
  41.3 0.0 collective-permute-done.8.qry
  41.3 0.1 collective-permute-done.9.refs_2_
  41.4 7.9 %collective-permute-done.10.refs_3_ = bf16[3,96,256]{2,1,0:T(8,128)(2,1)S(1)} collective-permute-done((bf16[3,96,256]{2,1,0:T(8,128)(2,1)S(1)}, bf16[3,96,256]{2,1,0:T(8,128)(2,1)S(1)}, u32[]{:S(2)}, u32[]{:S(2)}) %collective-permute-start.10) | collective-permute-done | bytes 147488 | tf_op jit(solution)/shard_map/ppermute | solution.py:285
  49.4 0.6 shard_map.85
  49.9 0.5 collective-permute-start.11
  50.5 1.1 %collective-permute-done.11.rest = bf16[3,128,256]{2,1,0:T(8,128)(2,1)S(1)} collective-permute-done((bf16[3,128,256]{2,1,0:T(8,128)(2,1)S(1)}, bf16[3,128,256]{2,1,0:T(8,128)(2,1)S(1)}, u32[]{:S(2)}, u32[]{:S(2)}) %collective-permute-start.11) | collective-permute-done | bytes 196640 | tf_op jit(solution)/shard_map/ppermute | solution.py:293
  51.6 2.1 %collective-permute-start.12 = (bf16[3,256,256]{2,1,0:T(8,128)(2,1)S(1)}, bf16[3,256,256]{2,1,0:T(8,128)(2,1)S(1)}, u32[]{:S(2)}, u32[]{:S(2)}) collective-permute-start(bf16[3,256,256]{2,1,0:T(8,128)(2,1)S(1)} %get-tuple-element.54.large), channel_id=1, source_target_pairs={{1,3},{3,1},{5,7},{7,5},{9,11},{11,9},{13,15},{15,13},{17,19},{19,... | collective-permute-start | bytes 1179656 | tf_op jit(solution)/shard_map/ppermute | solution.py:295
  53.7 0.1 dynamic-slice_bitcast_fusion.fast
  53.8 6.3 %collective-permute-done.12.half = bf16[3,256,256]{2,1,0:T(8,128)(2,1)S(1)} collective-permute-done((bf16[3,256,256]{2,1,0:T(8,128)(2,1)S(1)}, bf16[3,256,256]{2,1,0:T(8,128)(2,1)S(1)}, u32[]{:S(2)}, u32[]{:S(2)}) %collective-permute-start.12) | collective-permute-done | bytes 393248 | tf_op jit(solution)/shard_map/ppermute | solution.py:295
  60.1 3.9 %shard_map.86 = (bf16[512,256]{1,0:T(8,128)(2,1)S(1)}, bf16[3,512,256]{2,1,0:T(8,128)(2,1)S(1)}) custom-call(s32[10]{0:T(128)S(1)} %stack.37.where, bf16[3,256,256]{2,1,0:T(8,128)(2,1)S(1)} %get-tuple-element.54.large, bf16[3,128,256]{2,1,0:T(8,128)(2,1)S(1)} %get-tuple-element.53.small, bf16[3,128,256]{2,1,0:T(8,128)(2,1)S(1)} %collective-permute-done.11.rest, ...), custom_call_target="tpu_custom_call" | custom-call | tf_op jit(solution)/shard_map/pallas_call | solution.py:198
  64.0 0.7 collective-permute-start.13
  64.7 1.6 %shard_map.87 = (bf16[256,256]{1,0:T(8,128)(2,1)S(1)}, f32[256,768]{1,0:T(8,128)S(1)}) custom-call(s32[10]{0:T(128)S(1)} %stack.37.where, bf16[256,256]{1,0:T(8,128)(2,1)S(1)} %get-tuple-element.36.own, bf16[256,256]{1,0:T(8,128)(2,1)S(1)} %get-tuple-element.68.other, bf16[3,512,256]{2,1,0:T(8,128)(2,1)S(1)} %get-tuple-element.57.fresh, ...), custom_call_target="tpu_custom_call" | custom-call | tf_op jit(solution)/shard_map/pallas_call | solution.py:198
  66.3 0.1 collective-permute-start.14
  66.4 0.0 collective-permute-done.13.back
  66.4 0.6 collective-permute-start.15
  66.9 0.8 %collective-permute-done.14.near = bf16[256,256]{1,0:T(8,128)(2,1)S(1)} collective-permute-done((bf16[256,256]{1,0:T(8,128)(2,1)S(1)}, bf16[256,256]{1,0:T(8,128)(2,1)S(1)}, u32[]{:S(2)}, u32[]{:S(2)}) %collective-permute-start.14) | collective-permute-done | bytes 131104 | tf_op jit(solution)/shard_map/ppermute | solution.py:311
  67.7 0.2 collective-permute-done.15.relayed
  67.9 1.7 %shard_map.88 = bf16[256,768]{1,0:T(8,128)(2,1)} custom-call(s32[10]{0:T(128)S(1)} %stack.37.where, f32[256,768]{1,0:T(8,128)S(1)} %get-tuple-element.60.begun, bf16[256,256]{1,0:T(8,128)(2,1)S(1)} %collective-permute-done.14.near, bf16[512,256]{1,0:T(8,128)(2,1)S(1)} %collective-permute-done.13.back, bf16[256,256]{1,0:T(8,128)(2,1)S(1)} %collective-permute-done.15.relayed, ...), custom_call_target="tpu_custom_call" | custom-call | tf_op jit(solution)/shard_map/pallas_call | solution.py:198
  (15 shorter events, 0.1 us)
Async XLA Ops:
  0.0 1.7 %copy-start = (bf16[512,3,3,256]{3,0,2,1:T(8,128)(2,1)S(1)}, bf16[512,3,3,256]{3,0,2,1:T(8,128)(2,1)}, u32[]{:S(2)}) copy-start(bf16[512,3,3,256]{3,0,2,1:T(8,128)(2,1)} %param.11) | copy-start | bytes 7077892
  0.0 3.4 %copy-start.4 = (bf16[256,768]{1,0:T(8,128)(2,1)S(1)}, bf16[256,768]{1,0:T(8,128)(2,1)}, u32[]{:S(2)}) copy-start(bf16[256,768]{1,0:T(8,128)(2,1)} %refs_0_.1) | copy-start | bytes 1179652
  0.0 3.4 %copy-start.5 = (bf16[3,768]{1,0:T(4,128)(2,1)S(1)}, bf16[3,768]{1,0:T(4,128)(2,1)}, u32[]{:S(2)}) copy-start(bf16[3,768]{1,0:T(4,128)(2,1)} %refs_2_.3) | copy-start | bytes 13828
  0.0 3.3 %collective-permute-start = (bf16[256,768]{1,0:T(8,128)(2,1)}, bf16[256,768]{1,0:T(8,128)(2,1)S(1)}, u32[]{:S(2)}, u32[]{:S(2)}) collective-permute-start(bf16[256,768]{1,0:T(8,128)(2,1)} %refs_0_.1), channel_id=1, source_target_pairs={{0,1},{1,0},{2,3},{3,2},{4,5},{5,4},{6,7},{7,6},{8,9},{9,8},{10,11... | collective-permute-start | bytes 1179656 | tf_op jit(solution)/shard_map/ppermute | solution.py:242
  0.8 10.9 %collective-permute-start.1 = (bf16[256,768]{1,0:T(8,128)(2,1)}, bf16[256,768]{1,0:T(8,128)(2,1)S(1)}, u32[]{:S(2)}, u32[]{:S(2)}) collective-permute-start(bf16[256,768]{1,0:T(8,128)(2,1)} %refs_0_.1), channel_id=1, source_target_pairs={{0,2},{2,0},{1,3},{3,1},{4,6},{6,4},{5,7},{7,5},{8,10},{10,8},{9,1... | collective-permute-start | bytes 1179656 | tf_op jit(solution)/shard_map/ppermute | solution.py:241
  1.7 5.6 %copy-start.2 = (bf16[768,768]{1,0:T(8,128)(2,1)S(1)}, bf16[768,768]{1,0:T(8,128)(2,1)}, u32[]{:S(2)}) copy-start(bf16[768,768]{1,0:T(8,128)(2,1)} %w_query.1) | copy-start | bytes 3538948
  1.7 5.6 %copy-start.3 = (bf16[256,768]{1,0:T(8,128)(2,1)S(1)}, bf16[256,768]{1,0:T(8,128)(2,1)}, u32[]{:S(2)}) copy-start(bf16[256,768]{1,0:T(8,128)(2,1)} %queries) | copy-start | bytes 1179652
  11.7 2.2 %collective-permute-start.2 = (bf16[256,768]{1,0:T(8,128)(2,1)S(1)}, bf16[256,768]{1,0:T(8,128)(2,1)S(1)}, u32[]{:S(2)}, u32[]{:S(2)}) collective-permute-start(bf16[256,768]{1,0:T(8,128)(2,1)S(1)} %collective-permute-done.1.refs_0_), channel_id=1, source_target_pairs={{0,1},{1,0},{2,3},{3,2},{4,5},{5,4},{6,7},{7,6},{8,9},{9,8},{10,11... | collective-permute-start | bytes 1179656 | tf_op jit(solution)/shard_map/ppermute | solution.py:266
  13.9 7.9 %collective-permute-start.3 = (bf16[512,256]{1,0:T(8,128)(2,1)S(1)}, bf16[512,256]{1,0:T(8,128)(2,1)S(1)}, u32[]{:S(2)}, u32[]{:S(2)}) collective-permute-start(bf16[512,256]{1,0:T(8,128)(2,1)S(1)} %get-tuple-element.41), channel_id=1, source_target_pairs={{0,1},{1,0},{2,3},{3,2},{4,5},{5,4},{6,7},{7,6},{8,9},{9,8},{10,11... | collective-permute-start | bytes 786440 | tf_op jit(solution)/shard_map/ppermute | solution.py:268
  14.2 39.5 %copy-start.6 = (bf16[768]{0:T(1024)(128)(2,1)S(1)}, bf16[768]{0:T(1024)(128)(2,1)}, u32[]{:S(2)}) copy-start(bf16[768]{0:T(1024)(128)(2,1)} %param.14) | copy-start | bytes 4612
  18.2 9.1 %collective-permute-start.6 = (bf16[3,96,256]{2,1,0:T(8,128)(2,1)S(1)}, bf16[3,96,256]{2,1,0:T(8,128)(2,1)S(1)}, u32[]{:S(2)}, u32[]{:S(2)}) collective-permute-start(bf16[3,96,256]{2,1,0:T(8,128)(2,1)S(1)} %get-tuple-element.49), channel_id=1, source_target_pairs={{0,12},{4,8},{8,4},{12,0},{1,13},{5,9},{9,5},{13,1},{2,14},{6,10},... | collective-permute-start | bytes 442376 | tf_op jit(solution)/shard_map/ppermute | solution.py:278
  19.6 9.8 %collective-permute-start.5 = (bf16[3,96,256]{2,1,0:T(8,128)(2,1)S(1)}, bf16[3,96,256]{2,1,0:T(8,128)(2,1)S(1)}, u32[]{:S(2)}, u32[]{:S(2)}) collective-permute-start(bf16[3,96,256]{2,1,0:T(8,128)(2,1)S(1)} %get-tuple-element.48), channel_id=1, source_target_pairs={{0,4},{4,0},{8,12},{12,8},{1,5},{5,1},{9,13},{13,9},{2,6},{6,2},{1... | collective-permute-start | bytes 442376 | tf_op jit(solution)/shard_map/ppermute | solution.py:278
  21.8 10.7 %collective-permute-start.4 = (bf16[3,96,256]{2,1,0:T(8,128)(2,1)S(1)}, bf16[3,96,256]{2,1,0:T(8,128)(2,1)S(1)}, u32[]{:S(2)}, u32[]{:S(2)}) collective-permute-start(bf16[3,96,256]{2,1,0:T(8,128)(2,1)S(1)} %get-tuple-element.47), channel_id=1, source_target_pairs={{0,8},{4,12},{8,0},{12,4},{1,9},{5,13},{9,1},{13,5},{2,10},{6,14},... | collective-permute-start | bytes 442376 | tf_op jit(solution)/shard_map/ppermute | solution.py:278
  21.9 19.5 %collective-permute-start.8 = (bf16[512,256]{1,0:T(8,128)(2,1)S(1)}, bf16[512,256]{1,0:T(8,128)(2,1)S(1)}, u32[]{:S(2)}, u32[]{:S(2)}) collective-permute-start(bf16[512,256]{1,0:T(8,128)(2,1)S(1)} %pad_maximum_fusion), channel_id=1, source_target_pairs={{0,2},{2,0},{4,6},{6,4},{8,10},{10,8},{12,14},{14,12},{16,18},{18,... | collective-permute-start | bytes 786440 | tf_op jit(solution)/shard_map/ppermute | solution.py:283
  32.6 32.1 %copy-start.1 = (bf16[768,768]{1,0:T(8,128)(2,1)S(1)}, bf16[768,768]{1,0:T(8,128)(2,1)}, u32[]{:S(2)}) copy-start(bf16[768,768]{1,0:T(8,128)(2,1)} %w_out.3) | copy-start | bytes 3538948
  32.6 8.7 %collective-permute-start.7 = (bf16[3,96,256]{2,1,0:T(8,128)(2,1)S(1)}, bf16[3,96,256]{2,1,0:T(8,128)(2,1)S(1)}, u32[]{:S(2)}, u32[]{:S(2)}) collective-permute-start(bf16[3,96,256]{2,1,0:T(8,128)(2,1)S(1)} %add_convert_fusion.refs_0_), channel_id=1, source_target_pairs={{0,8},{4,12},{8,0},{12,4},{1,9},{5,13},{9,1},{13,5},{2,10},{6,14},... | collective-permute-start | bytes 442376 | tf_op jit(solution)/shard_map/ppermute | solution.py:285
  35.5 5.9 %collective-permute-start.9 = (bf16[3,96,256]{2,1,0:T(8,128)(2,1)S(1)}, bf16[3,96,256]{2,1,0:T(8,128)(2,1)S(1)}, u32[]{:S(2)}, u32[]{:S(2)}) collective-permute-start(bf16[3,96,256]{2,1,0:T(8,128)(2,1)S(1)} %add_convert_fusion.refs_0_), channel_id=1, source_target_pairs={{0,4},{4,0},{8,12},{12,8},{1,5},{5,1},{9,13},{13,9},{2,6},{6,2},{1... | collective-permute-start | bytes 442376 | tf_op jit(solution)/shard_map/ppermute | solution.py:285
  35.5 13.8 %collective-permute-start.10 = (bf16[3,96,256]{2,1,0:T(8,128)(2,1)S(1)}, bf16[3,96,256]{2,1,0:T(8,128)(2,1)S(1)}, u32[]{:S(2)}, u32[]{:S(2)}) collective-permute-start(bf16[3,96,256]{2,1,0:T(8,128)(2,1)S(1)} %add_convert_fusion.refs_0_), channel_id=1, source_target_pairs={{0,12},{4,8},{8,4},{12,0},{1,13},{5,9},{9,5},{13,1},{2,14},{6,10},... | collective-permute-start | bytes 442376 | tf_op jit(solution)/shard_map/ppermute | solution.py:285
  49.9 1.6 %collective-permute-start.11 = (bf16[3,128,256]{2,1,0:T(8,128)(2,1)S(1)}, bf16[3,128,256]{2,1,0:T(8,128)(2,1)S(1)}, u32[]{:S(2)}, u32[]{:S(2)}) collective-permute-start(bf16[3,128,256]{2,1,0:T(8,128)(2,1)S(1)} %get-tuple-element.53.small), channel_id=1, source_target_pairs={{0,1},{1,0},{2,3},{3,2},{4,5},{5,4},{6,7},{7,6},{8,9},{9,8},{10,11... | collective-permute-start | bytes 589832 | tf_op jit(solution)/shard_map/ppermute | solution.py:293
  51.6 8.5 %collective-permute-start.12 = (bf16[3,256,256]{2,1,0:T(8,128)(2,1)S(1)}, bf16[3,256,256]{2,1,0:T(8,128)(2,1)S(1)}, u32[]{:S(2)}, u32[]{:S(2)}) collective-permute-start(bf16[3,256,256]{2,1,0:T(8,128)(2,1)S(1)} %get-tuple-element.54.large), channel_id=1, source_target_pairs={{1,3},{3,1},{5,7},{7,5},{9,11},{11,9},{13,15},{15,13},{17,19},{19,... | collective-permute-start | bytes 1179656 | tf_op jit(solution)/shard_map/ppermute | solution.py:295
  64.0 2.4 %collective-permute-start.13 = (bf16[512,256]{1,0:T(8,128)(2,1)S(1)}, bf16[512,256]{1,0:T(8,128)(2,1)S(1)}, u32[]{:S(2)}, u32[]{:S(2)}) collective-permute-start(bf16[512,256]{1,0:T(8,128)(2,1)S(1)} %get-tuple-element.59), channel_id=1, source_target_pairs={{0,2},{2,0},{4,6},{6,4},{8,10},{10,8},{12,14},{14,12},{16,18},{18,... | collective-permute-start | bytes 786440 | tf_op jit(solution)/shard_map/ppermute | solution.py:304
  66.3 1.4 %collective-permute-start.14 = (bf16[256,256]{1,0:T(8,128)(2,1)S(1)}, bf16[256,256]{1,0:T(8,128)(2,1)S(1)}, u32[]{:S(2)}, u32[]{:S(2)}) collective-permute-start(bf16[256,256]{1,0:T(8,128)(2,1)S(1)} %get-tuple-element.61), channel_id=1, source_target_pairs={{0,1},{1,0},{2,3},{3,2},{4,5},{5,4},{6,7},{7,6},{8,9},{9,8},{10,11... | collective-permute-start | bytes 393224 | tf_op jit(solution)/shard_map/ppermute | solution.py:311
  66.4 1.5 %collective-permute-start.15 = (bf16[256,256]{1,0:T(8,128)(2,1)S(1)}, bf16[256,256]{1,0:T(8,128)(2,1)S(1)}, u32[]{:S(2)}, u32[]{:S(2)}) collective-permute-start(bf16[256,256]{1,0:T(8,128)(2,1)S(1)} %slice.11), channel_id=1, source_target_pairs={{0,1},{1,0},{2,3},{3,2},{4,5},{5,4},{6,7},{7,6},{8,9},{9,8},{10,11... | collective-permute-start | bytes 393224 | tf_op jit(solution)/shard_map/ppermute | solution.py:313

commit v7 on v6

--- a/solution.py
+++ b/solution.py
@@ -48,7 +48,7 @@
     scaled[...] = (rate * mm(rows, w_v[...])).astype(BF)
 
 
-def add_gradient(keys, scaled, fast, acc):
+def gradient(keys, scaled, fast, begun, acc):
     gate_pre = mm(fast[0], keys, NT)
     up_pre = mm(fast[1], keys, NT)
     back = mm(fast[2], scaled, NT)
@@ -57,42 +57,34 @@
     hidden = (act * up_pre).astype(BF)
     d_gate = (back * up_pre * sig * (1.0 + gate_pre * (1.0 - sig))).astype(BF)
     d_up = (back * act).astype(BF)
-    acc[0] += mm(d_gate, keys)
-    acc[1] += mm(d_up, keys)
-    acc[2] += mm(hidden, scaled)
-
-
-def add_segments(where, toks, weights, accs, keys, scaled):
+    for kind, (left, right) in enumerate(((d_gate, keys), (d_up, keys), (hidden, scaled))):
+        product = mm(left, right)
+        acc[kind] = product if begun is None else begun[kind] + product
+
+
+def segments(where, toks, weights, begun, accs, keys, scaled):
     w_rate, *weights = weights
     large, small = weights[:3], weights[3:]
-    both = [(tok, at) for tok in toks for at in range(0, tok.shape[0], HD)]
-    for i, (tok, at) in enumerate(both):
-        rows = tok[at : at + HD]
-        project(rows, where[6], *large[:2], w_rate, keys.at[i], scaled.at[i])
-        add_gradient(keys[i], scaled[i], large[2], accs[0])
+    rows = jnp.concatenate([tok[...] for tok in toks])
+    project(rows, where[6], *large[:2], w_rate, keys, scaled)
+    gradient(keys[...], scaled[...], large[2], begun[0], accs[0])
 
     @pl.when(where[8] != 0)
     def _():
-        for i, (tok, at) in enumerate(both):
-            project(tok[at : at + HD], where[7], *small[:2], w_rate, keys.at[i], scaled.at[i])
-
-    for i in range(len(both)):
-        add_gradient(keys[i], scaled[i], small[2], accs[1])
+        project(rows, where[7], *small[:2], w_rate, keys, scaled)
+
+    gradient(keys[...], scaled[...], small[2], begun[1], accs[1])
 
 
 def first_kernel(n_tok, where, *refs):
     toks, weights, accs, rows = refs[:n_tok], refs[n_tok:-4], refs[-4:-2], refs[-2:]
-    for acc in accs:
-        acc[...] = jnp.zeros_like(acc)
-    add_segments(where, toks, weights, accs, *rows)
+    segments(where, toks, weights, (None, None), accs, *rows)
 
 
 def second_kernel(n_tok, n_patch, where, *refs):
     toks, weights, begun = refs[:n_tok], refs[n_tok : n_tok + 7], refs[n_tok + 7 : n_tok + 9]
     outs, accs, rows = refs[n_tok + 9 : -4], refs[-4:-2], refs[-2:]
-    for acc, part in zip(accs, begun):
-        acc[...] = part[...]
-    add_segments(where, toks, weights, accs, *rows)
+    segments(where, toks, weights, begun, accs, *rows)
     for out, shift in zip(outs, exchange_order(n_patch)):
         chunk = where[1] ^ shift
         at = 0
@@ -103,13 +95,13 @@
 
 
 def collect_kernel(n_patch, where, *refs):
-    parts, segments = refs[:n_patch], refs[n_patch:]
+    parts, pieces = refs[:n_patch], refs[n_patch:]
     for part, shift in zip(parts, exchange_order(n_patch, True)):
         chunk = where[1] ^ shift
         at = 0
-        for segment in segments:
-            size = segment.shape[1] // n_patch
-            segment[:, pl.ds(pl.multiple_of(chunk * size, size), size)] = part[:, at : at + size]
+        for piece in pieces:
+            size = piece.shape[1] // n_patch
+            piece[:, pl.ds(pl.multiple_of(chunk * size, size), size)] = part[:, at : at + size]
             at += size
 
 
@@ -167,8 +159,7 @@
 
     @pl.when(where[8] == 0)
     def _():
-        for row in range(0, qry.shape[0], HD):
-            out[row : row + HD] = decode(qry[row : row + HD], fresh, gain)
+        out[...] = decode(qry[...], fresh, gain)
 
 
 def query_kernel(where, queries, w_query, own, message, other, heads):
@@ -251,7 +242,7 @@
     sums = [jax.ShapeDtypeStruct((3, size, HD), FP) for size in (LARGE, SMALL)]
 
     def held(toks):
-        return [pltpu.VMEM((len(toks) * n_tok // HD, HD, HD), BF)] * 2
+        return [pltpu.VMEM((len(toks) * n_tok, HD), BF)] * 2
 
     begun = list(call(functools.partial(first_kernel, len(near)), where, near + weights, sums, held(near)))
     late, _ = lax.optimization_barrier((queries, begun[0]))

time: 69.8 us -> 69.3 us (level)
  Pallas kernels: 16.8 us -> 16 us
    pallas_call x7, Pallas kernels: 16.8 us -> 16 us  [call(): pl.pallas_call(kernel, out_shape=outs, grid_spec=pltpu.PrefetchScalarGrid...]
  transfers between devices with their start and end apart: 16 -> 16, of which waited for: 12 -> 12; matrix products, arithmetic and copies ran while one was open for 3% -> 3% of each run, Pallas kernels for 15% -> 14%
where the time goes in v7:
time: 69.3 us; the launch traced here: 69.1 us
  waiting for transfers between devices  36.7 us (53%)
  Pallas kernels  16 us (23%)
  starting transfers between devices  13.7 us (20%)
  local copies, waits for them, and re-layouts  2.42 us (3%)
    pallas_call x7, Pallas kernels, call(): pl.pallas_call(kernel, out_shape=outs, grid_spec=pltpu.PrefetchScalarGrid...  16 us
    ppermute x3, waiting for transfers between devices, local(): lax.ppermute(own, 'patch', pairs(s))  13.5 us
    ppermute x3, waiting for transfers between devices, local(): lax.ppermute(chunks[k], 'patch', pairs(order[k]))  9.96 us
    ppermute x1, waiting for transfers between devices, local(): half = lax.ppermute(large, every, seconds)  6.25 us
    ppermute x1, waiting for transfers between devices, local(): lax.ppermute(tokens, 'view', rotate(n_view, s))  3.58 us
    ppermute x3, starting transfers between devices, local(): lax.ppermute(chunks[k], 'patch', pairs(order[k]))  3.56 us
    ppermute x3, starting transfers between devices, local(): lax.ppermute(own, 'patch', pairs(s))  3.24 us
    ppermute x1, starting transfers between devices, local(): half = lax.ppermute(large, every, seconds)  2.16 us
  transfers between devices with their start and end apart: 16, of which 12 were waited for; matrix products, arithmetic and copies ran while one was open for 3% of the time, Pallas kernels for 14%

profile of v7, /device:TPU:11, one launch (start us, length us, event | category | flops | bytes accessed | tf_op | source)
XLA Modules:
  0.0 69.1 jit_solution(9474953664649850430)
XLA Ops:
  0.0 0.7 %collective-permute-start = (bf16[256,768]{1,0:T(8,128)(2,1)}, bf16[256,768]{1,0:T(8,128)(2,1)S(1)}, u32[]{:S(2)}, u32[]{:S(2)}) collective-permute-start(bf16[256,768]{1,0:T(8,128)(2,1)} %refs_0_.1), channel_id=1, source_target_pairs={{0,1},{1,0},{2,3},{3,2},{4,5},{5,4},{6,7},{7,6},{8,9},{9,8},{10,11... | collective-permute-start | bytes 1179656 | tf_op jit(solution)/shard_map/ppermute | solution.py:233
  0.8 0.3 collective-permute-start.1
  1.0 0.1 stack.37.where
  1.1 0.6 copy-done
  1.7 0.0 copy-start.2
  1.7 0.0 copy-start.3
  1.8 1.6 %constant_dynamic-slice_fusion = (bf16[768,256]{1,0:T(8,128)(2,1)S(1)}, bf16[768,256]{1,0:T(8,128)(2,1)S(1)}, bf16[768,256]{1,0:T(8,128)(2,1)S(1)}, bf16[768,256]{1,0:T(8,128)(2,1)S(1)}) fusion(bf16[768,1536]{1,0:T(8,128)(2,1)} %param.9, s32[]{:T(128)S(6)} %select_n.59, s32[]{:T(128)S(6)} %select_n.54, s32[]{:T(128)S(6)} %select_n.53, s32[]{:T(128)S(6)} %select_n.58), kind=kLoop, calls=%fused_computation.5 | loop fusion | bytes 3145744 | tf_op jit(solution)/shard_map/dynamic_slice | solution.py:239
  3.4 0.0 collective-permute-done.refs_1_
  3.4 0.0 copy-done.4
  3.4 3.5 %shard_map.82 = (f32[3,256,256]{2,1,0:T(8,128)S(1)}, f32[3,128,256]{2,1,0:T(8,128)S(1)}) custom-call(s32[10]{0:T(128)S(1)} %stack.37.where, bf16[256,768]{1,0:T(8,128)(2,1)S(1)} %copy-done.4, bf16[256,768]{1,0:T(8,128)(2,1)S(1)} %collective-permute-done.refs_1_, bf16[3,768]{1,0:T(4,128)(2,1)S(1)} %copy-done.5, ...), custom_call_target="tpu_custom_call" | custom-call | tf_op jit(solution)/shard_map/pallas_call | solution.py:189
  6.9 1.1 %shard_map.83 = (bf16[256,256]{1,0:T(8,128)(2,1)S(1)}, bf16[512,256]{1,0:T(8,128)(2,1)S(1)}, bf16[256,256]{1,0:T(8,128)(2,1)S(1)}) custom-call(s32[10]{0:T(128)S(1)} %stack.37.where, bf16[256,768]{1,0:T(8,128)(2,1)S(1)} %copy-done.3, bf16[768,768]{1,0:T(8,128)(2,1)S(1)} %copy-done.2), custom_call_target="tpu_custom_call" | custom-call | tf_op jit(solution)/shard_map/pallas_call | solution.py:189
  8.1 3.6 %collective-permute-done.1.refs_0_ = bf16[256,768]{1,0:T(8,128)(2,1)S(1)} collective-permute-done((bf16[256,768]{1,0:T(8,128)(2,1)}, bf16[256,768]{1,0:T(8,128)(2,1)S(1)}, u32[]{:S(2)}, u32[]{:S(2)}) %collective-permute-start.1) | collective-permute-done | bytes 393248 | tf_op jit(solution)/shard_map/ppermute | solution.py:232
  11.7 0.8 %collective-permute-start.2 = (bf16[256,768]{1,0:T(8,128)(2,1)S(1)}, bf16[256,768]{1,0:T(8,128)(2,1)S(1)}, u32[]{:S(2)}, u32[]{:S(2)}) collective-permute-start(bf16[256,768]{1,0:T(8,128)(2,1)S(1)} %collective-permute-done.1.refs_0_), channel_id=1, source_target_pairs={{0,1},{1,0},{2,3},{3,2},{4,5},{5,4},{6,7},{7,6},{8,9},{9,8},{10,11... | collective-permute-start | bytes 1179656 | tf_op jit(solution)/shard_map/ppermute | solution.py:257
  12.5 1.3 %collective-permute-done.2.refs_1_ = bf16[256,768]{1,0:T(8,128)(2,1)S(1)} collective-permute-done((bf16[256,768]{1,0:T(8,128)(2,1)S(1)}, bf16[256,768]{1,0:T(8,128)(2,1)S(1)}, u32[]{:S(2)}, u32[]{:S(2)}) %collective-permute-start.2) | collective-permute-done | bytes 393248 | tf_op jit(solution)/shard_map/ppermute | solution.py:257
  13.9 0.4 collective-permute-start.3
  14.2 3.6 %shard_map.84 = (f32[3,96,256]{2,1,0:T(8,128)S(1)}, bf16[3,96,256]{2,1,0:T(8,128)(2,1)S(1)}, bf16[3,96,256]{2,1,0:T(8,128)(2,1)S(1)}, bf16[3,96,256]{2,1,0:T(8,128)(2,1)S(1)}) custom-call(s32[10]{0:T(128)S(1)} %stack.37.where, bf16[256,768]{1,0:T(8,128)(2,1)S(1)} %collective-permute-done.1.refs_0_, bf16[256,768]{1,0:T(8,128)(2,1)S(1)} %collective-permute-done.2.refs_1_, ...), custom_call_target="tpu_custom_call" | custom-call | tf_op jit(solution)/shard_map/pallas_call | solution.py:189
  17.8 1.4 %collective-permute-start.6 = (bf16[3,96,256]{2,1,0:T(8,128)(2,1)S(1)}, bf16[3,96,256]{2,1,0:T(8,128)(2,1)S(1)}, u32[]{:S(2)}, u32[]{:S(2)}) collective-permute-start(bf16[3,96,256]{2,1,0:T(8,128)(2,1)S(1)} %get-tuple-element.49), channel_id=1, source_target_pairs={{0,12},{4,8},{8,4},{12,0},{1,13},{5,9},{9,5},{13,1},{2,14},{6,10},... | collective-permute-start | bytes 442376 | tf_op jit(solution)/shard_map/ppermute | solution.py:269
  19.2 2.2 %collective-permute-start.5 = (bf16[3,96,256]{2,1,0:T(8,128)(2,1)S(1)}, bf16[3,96,256]{2,1,0:T(8,128)(2,1)S(1)}, u32[]{:S(2)}, u32[]{:S(2)}) collective-permute-start(bf16[3,96,256]{2,1,0:T(8,128)(2,1)S(1)} %get-tuple-element.48), channel_id=1, source_target_pairs={{0,4},{4,0},{8,12},{12,8},{1,5},{5,1},{9,13},{13,9},{2,6},{6,2},{1... | collective-permute-start | bytes 442376 | tf_op jit(solution)/shard_map/ppermute | solution.py:269
  21.4 0.0 collective-permute-start.4
  21.4 0.0 collective-permute-done.3
  21.4 0.7 collective-permute-start.8
  22.1 4.8 %collective-permute-done.6 = bf16[3,96,256]{2,1,0:T(8,128)(2,1)S(1)} collective-permute-done((bf16[3,96,256]{2,1,0:T(8,128)(2,1)S(1)}, bf16[3,96,256]{2,1,0:T(8,128)(2,1)S(1)}, u32[]{:S(2)}, u32[]{:S(2)}) %collective-permute-start.6) | collective-permute-done | bytes 147488 | tf_op jit(solution)/shard_map/ppermute | solution.py:269
  26.9 2.1 %collective-permute-done.5 = bf16[3,96,256]{2,1,0:T(8,128)(2,1)S(1)} collective-permute-done((bf16[3,96,256]{2,1,0:T(8,128)(2,1)S(1)}, bf16[3,96,256]{2,1,0:T(8,128)(2,1)S(1)}, u32[]{:S(2)}, u32[]{:S(2)}) %collective-permute-start.5) | collective-permute-done | bytes 147488 | tf_op jit(solution)/shard_map/ppermute | solution.py:269
  29.0 3.1 %collective-permute-done.4 = bf16[3,96,256]{2,1,0:T(8,128)(2,1)S(1)} collective-permute-done((bf16[3,96,256]{2,1,0:T(8,128)(2,1)S(1)}, bf16[3,96,256]{2,1,0:T(8,128)(2,1)S(1)}, u32[]{:S(2)}, u32[]{:S(2)}) %collective-permute-start.4) | collective-permute-done | bytes 147488 | tf_op jit(solution)/shard_map/ppermute | solution.py:269
  32.1 0.1 add_convert_fusion.refs_0_
  32.1 0.0 copy-start.1
  32.1 2.9 %collective-permute-start.7 = (bf16[3,96,256]{2,1,0:T(8,128)(2,1)S(1)}, bf16[3,96,256]{2,1,0:T(8,128)(2,1)S(1)}, u32[]{:S(2)}, u32[]{:S(2)}) collective-permute-start(bf16[3,96,256]{2,1,0:T(8,128)(2,1)S(1)} %add_convert_fusion.refs_0_), channel_id=1, source_target_pairs={{0,8},{4,12},{8,0},{12,4},{1,9},{5,13},{9,1},{13,5},{2,10},{6,14},... | collective-permute-start | bytes 442376 | tf_op jit(solution)/shard_map/ppermute | solution.py:276
  35.0 0.0 collective-permute-start.9
  35.0 0.4 collective-permute-start.10
  35.4 5.5 %collective-permute-done.7.refs_1_ = bf16[3,96,256]{2,1,0:T(8,128)(2,1)S(1)} collective-permute-done((bf16[3,96,256]{2,1,0:T(8,128)(2,1)S(1)}, bf16[3,96,256]{2,1,0:T(8,128)(2,1)S(1)}, u32[]{:S(2)}, u32[]{:S(2)}) %collective-permute-start.7) | collective-permute-done | bytes 147488 | tf_op jit(solution)/shard_map/ppermute | solution.py:276
  40.9 0.0 collective-permute-done.8.qry
  40.9 0.1 collective-permute-done.9.refs_2_
  41.0 7.9 %collective-permute-done.10.refs_3_ = bf16[3,96,256]{2,1,0:T(8,128)(2,1)S(1)} collective-permute-done((bf16[3,96,256]{2,1,0:T(8,128)(2,1)S(1)}, bf16[3,96,256]{2,1,0:T(8,128)(2,1)S(1)}, u32[]{:S(2)}, u32[]{:S(2)}) %collective-permute-start.10) | collective-permute-done | bytes 147488 | tf_op jit(solution)/shard_map/ppermute | solution.py:276
  48.9 0.6 shard_map.85
  49.5 0.5 collective-permute-start.11
  50.0 1.1 %collective-permute-done.11.rest = bf16[3,128,256]{2,1,0:T(8,128)(2,1)S(1)} collective-permute-done((bf16[3,128,256]{2,1,0:T(8,128)(2,1)S(1)}, bf16[3,128,256]{2,1,0:T(8,128)(2,1)S(1)}, u32[]{:S(2)}, u32[]{:S(2)}) %collective-permute-start.11) | collective-permute-done | bytes 196640 | tf_op jit(solution)/shard_map/ppermute | solution.py:284
  51.1 2.2 %collective-permute-start.12 = (bf16[3,256,256]{2,1,0:T(8,128)(2,1)S(1)}, bf16[3,256,256]{2,1,0:T(8,128)(2,1)S(1)}, u32[]{:S(2)}, u32[]{:S(2)}) collective-permute-start(bf16[3,256,256]{2,1,0:T(8,128)(2,1)S(1)} %get-tuple-element.54.large), channel_id=1, source_target_pairs={{1,3},{3,1},{5,7},{7,5},{9,11},{11,9},{13,15},{15,13},{17,19},{19,... | collective-permute-start | bytes 1179656 | tf_op jit(solution)/shard_map/ppermute | solution.py:286
  53.3 0.1 dynamic-slice_bitcast_fusion.fast
  53.3 6.3 %collective-permute-done.12.half = bf16[3,256,256]{2,1,0:T(8,128)(2,1)S(1)} collective-permute-done((bf16[3,256,256]{2,1,0:T(8,128)(2,1)S(1)}, bf16[3,256,256]{2,1,0:T(8,128)(2,1)S(1)}, u32[]{:S(2)}, u32[]{:S(2)}) %collective-permute-start.12) | collective-permute-done | bytes 393248 | tf_op jit(solution)/shard_map/ppermute | solution.py:286
  59.6 3.9 %shard_map.86 = (bf16[512,256]{1,0:T(8,128)(2,1)S(1)}, bf16[3,512,256]{2,1,0:T(8,128)(2,1)S(1)}) custom-call(s32[10]{0:T(128)S(1)} %stack.37.where, bf16[3,256,256]{2,1,0:T(8,128)(2,1)S(1)} %get-tuple-element.54.large, bf16[3,128,256]{2,1,0:T(8,128)(2,1)S(1)} %get-tuple-element.53.small, bf16[3,128,256]{2,1,0:T(8,128)(2,1)S(1)} %collective-permute-done.11.rest, ...), custom_call_target="tpu_custom_call" | custom-call | tf_op jit(solution)/shard_map/pallas_call | solution.py:189
  63.5 0.7 collective-permute-start.13
  64.2 1.6 %shard_map.87 = (bf16[256,256]{1,0:T(8,128)(2,1)S(1)}, f32[256,768]{1,0:T(8,128)S(1)}) custom-call(s32[10]{0:T(128)S(1)} %stack.37.where, bf16[256,256]{1,0:T(8,128)(2,1)S(1)} %get-tuple-element.36.own, bf16[256,256]{1,0:T(8,128)(2,1)S(1)} %get-tuple-element.68.other, bf16[3,512,256]{2,1,0:T(8,128)(2,1)S(1)} %get-tuple-element.57.fresh, ...), custom_call_target="tpu_custom_call" | custom-call | tf_op jit(solution)/shard_map/pallas_call | solution.py:189
  65.8 0.1 collective-permute-start.14
  65.9 0.0 collective-permute-done.13.back
  65.9 0.6 collective-permute-start.15
  66.4 0.8 %collective-permute-done.14.near = bf16[256,256]{1,0:T(8,128)(2,1)S(1)} collective-permute-done((bf16[256,256]{1,0:T(8,128)(2,1)S(1)}, bf16[256,256]{1,0:T(8,128)(2,1)S(1)}, u32[]{:S(2)}, u32[]{:S(2)}) %collective-permute-start.14) | collective-permute-done | bytes 131104 | tf_op jit(solution)/shard_map/ppermute | solution.py:302
  67.2 0.2 collective-permute-done.15.relayed
  67.4 1.7 %shard_map.88 = bf16[256,768]{1,0:T(8,128)(2,1)} custom-call(s32[10]{0:T(128)S(1)} %stack.37.where, f32[256,768]{1,0:T(8,128)S(1)} %get-tuple-element.60.begun, bf16[256,256]{1,0:T(8,128)(2,1)S(1)} %collective-permute-done.14.near, bf16[512,256]{1,0:T(8,128)(2,1)S(1)} %collective-permute-done.13.back, bf16[256,256]{1,0:T(8,128)(2,1)S(1)} %collective-permute-done.15.relayed, ...), custom_call_target="tpu_custom_call" | custom-call | tf_op jit(solution)/shard_map/pallas_call | solution.py:189
  (15 shorter events, 0.1 us)
Async XLA Ops:
  0.0 1.7 %copy-start = (bf16[512,3,3,256]{3,0,2,1:T(8,128)(2,1)S(1)}, bf16[512,3,3,256]{3,0,2,1:T(8,128)(2,1)}, u32[]{:S(2)}) copy-start(bf16[512,3,3,256]{3,0,2,1:T(8,128)(2,1)} %param.11) | copy-start | bytes 7077892
  0.0 3.4 %copy-start.4 = (bf16[256,768]{1,0:T(8,128)(2,1)S(1)}, bf16[256,768]{1,0:T(8,128)(2,1)}, u32[]{:S(2)}) copy-start(bf16[256,768]{1,0:T(8,128)(2,1)} %refs_0_.1) | copy-start | bytes 1179652
  0.0 3.4 %copy-start.5 = (bf16[3,768]{1,0:T(4,128)(2,1)S(1)}, bf16[3,768]{1,0:T(4,128)(2,1)}, u32[]{:S(2)}) copy-start(bf16[3,768]{1,0:T(4,128)(2,1)} %refs_2_.3) | copy-start | bytes 13828
  0.0 3.3 %collective-permute-start = (bf16[256,768]{1,0:T(8,128)(2,1)}, bf16[256,768]{1,0:T(8,128)(2,1)S(1)}, u32[]{:S(2)}, u32[]{:S(2)}) collective-permute-start(bf16[256,768]{1,0:T(8,128)(2,1)} %refs_0_.1), channel_id=1, source_target_pairs={{0,1},{1,0},{2,3},{3,2},{4,5},{5,4},{6,7},{7,6},{8,9},{9,8},{10,11... | collective-permute-start | bytes 1179656 | tf_op jit(solution)/shard_map/ppermute | solution.py:233
  0.8 10.9 %collective-permute-start.1 = (bf16[256,768]{1,0:T(8,128)(2,1)}, bf16[256,768]{1,0:T(8,128)(2,1)S(1)}, u32[]{:S(2)}, u32[]{:S(2)}) collective-permute-start(bf16[256,768]{1,0:T(8,128)(2,1)} %refs_0_.1), channel_id=1, source_target_pairs={{0,2},{2,0},{1,3},{3,1},{4,6},{6,4},{5,7},{7,5},{8,10},{10,8},{9,1... | collective-permute-start | bytes 1179656 | tf_op jit(solution)/shard_map/ppermute | solution.py:232
  1.7 5.2 %copy-start.2 = (bf16[768,768]{1,0:T(8,128)(2,1)S(1)}, bf16[768,768]{1,0:T(8,128)(2,1)}, u32[]{:S(2)}) copy-start(bf16[768,768]{1,0:T(8,128)(2,1)} %w_query.1) | copy-start | bytes 3538948
  1.7 5.2 %copy-start.3 = (bf16[256,768]{1,0:T(8,128)(2,1)S(1)}, bf16[256,768]{1,0:T(8,128)(2,1)}, u32[]{:S(2)}) copy-start(bf16[256,768]{1,0:T(8,128)(2,1)} %queries) | copy-start | bytes 1179652
  11.7 2.2 %collective-permute-start.2 = (bf16[256,768]{1,0:T(8,128)(2,1)S(1)}, bf16[256,768]{1,0:T(8,128)(2,1)S(1)}, u32[]{:S(2)}, u32[]{:S(2)}) collective-permute-start(bf16[256,768]{1,0:T(8,128)(2,1)S(1)} %collective-permute-done.1.refs_0_), channel_id=1, source_target_pairs={{0,1},{1,0},{2,3},{3,2},{4,5},{5,4},{6,7},{7,6},{8,9},{9,8},{10,11... | collective-permute-start | bytes 1179656 | tf_op jit(solution)/shard_map/ppermute | solution.py:257
  13.9 7.5 %collective-permute-start.3 = (bf16[512,256]{1,0:T(8,128)(2,1)S(1)}, bf16[512,256]{1,0:T(8,128)(2,1)S(1)}, u32[]{:S(2)}, u32[]{:S(2)}) collective-permute-start(bf16[512,256]{1,0:T(8,128)(2,1)S(1)} %get-tuple-element.41), channel_id=1, source_target_pairs={{0,1},{1,0},{2,3},{3,2},{4,5},{5,4},{6,7},{7,6},{8,9},{9,8},{10,11... | collective-permute-start | bytes 786440 | tf_op jit(solution)/shard_map/ppermute | solution.py:259
  14.2 39.0 %copy-start.6 = (bf16[768]{0:T(1024)(128)(2,1)S(1)}, bf16[768]{0:T(1024)(128)(2,1)}, u32[]{:S(2)}) copy-start(bf16[768]{0:T(1024)(128)(2,1)} %param.14) | copy-start | bytes 4612
  17.8 9.1 %collective-permute-start.6 = (bf16[3,96,256]{2,1,0:T(8,128)(2,1)S(1)}, bf16[3,96,256]{2,1,0:T(8,128)(2,1)S(1)}, u32[]{:S(2)}, u32[]{:S(2)}) collective-permute-start(bf16[3,96,256]{2,1,0:T(8,128)(2,1)S(1)} %get-tuple-element.49), channel_id=1, source_target_pairs={{0,12},{4,8},{8,4},{12,0},{1,13},{5,9},{9,5},{13,1},{2,14},{6,10},... | collective-permute-start | bytes 442376 | tf_op jit(solution)/shard_map/ppermute | solution.py:269
  19.2 9.8 %collective-permute-start.5 = (bf16[3,96,256]{2,1,0:T(8,128)(2,1)S(1)}, bf16[3,96,256]{2,1,0:T(8,128)(2,1)S(1)}, u32[]{:S(2)}, u32[]{:S(2)}) collective-permute-start(bf16[3,96,256]{2,1,0:T(8,128)(2,1)S(1)} %get-tuple-element.48), channel_id=1, source_target_pairs={{0,4},{4,0},{8,12},{12,8},{1,5},{5,1},{9,13},{13,9},{2,6},{6,2},{1... | collective-permute-start | bytes 442376 | tf_op jit(solution)/shard_map/ppermute | solution.py:269
  21.4 10.7 %collective-permute-start.4 = (bf16[3,96,256]{2,1,0:T(8,128)(2,1)S(1)}, bf16[3,96,256]{2,1,0:T(8,128)(2,1)S(1)}, u32[]{:S(2)}, u32[]{:S(2)}) collective-permute-start(bf16[3,96,256]{2,1,0:T(8,128)(2,1)S(1)} %get-tuple-element.47), channel_id=1, source_target_pairs={{0,8},{4,12},{8,0},{12,4},{1,9},{5,13},{9,1},{13,5},{2,10},{6,14},... | collective-permute-start | bytes 442376 | tf_op jit(solution)/shard_map/ppermute | solution.py:269
  21.4 19.5 %collective-permute-start.8 = (bf16[512,256]{1,0:T(8,128)(2,1)S(1)}, bf16[512,256]{1,0:T(8,128)(2,1)S(1)}, u32[]{:S(2)}, u32[]{:S(2)}) collective-permute-start(bf16[512,256]{1,0:T(8,128)(2,1)S(1)} %pad_maximum_fusion), channel_id=1, source_target_pairs={{0,2},{2,0},{4,6},{6,4},{8,10},{10,8},{12,14},{14,12},{16,18},{18,... | collective-permute-start | bytes 786440 | tf_op jit(solution)/shard_map/ppermute | solution.py:274
  32.1 32.0 %copy-start.1 = (bf16[768,768]{1,0:T(8,128)(2,1)S(1)}, bf16[768,768]{1,0:T(8,128)(2,1)}, u32[]{:S(2)}) copy-start(bf16[768,768]{1,0:T(8,128)(2,1)} %w_out.3) | copy-start | bytes 3538948
  32.1 8.7 %collective-permute-start.7 = (bf16[3,96,256]{2,1,0:T(8,128)(2,1)S(1)}, bf16[3,96,256]{2,1,0:T(8,128)(2,1)S(1)}, u32[]{:S(2)}, u32[]{:S(2)}) collective-permute-start(bf16[3,96,256]{2,1,0:T(8,128)(2,1)S(1)} %add_convert_fusion.refs_0_), channel_id=1, source_target_pairs={{0,8},{4,12},{8,0},{12,4},{1,9},{5,13},{9,1},{13,5},{2,10},{6,14},... | collective-permute-start | bytes 442376 | tf_op jit(solution)/shard_map/ppermute | solution.py:276
  35.0 5.9 %collective-permute-start.9 = (bf16[3,96,256]{2,1,0:T(8,128)(2,1)S(1)}, bf16[3,96,256]{2,1,0:T(8,128)(2,1)S(1)}, u32[]{:S(2)}, u32[]{:S(2)}) collective-permute-start(bf16[3,96,256]{2,1,0:T(8,128)(2,1)S(1)} %add_convert_fusion.refs_0_), channel_id=1, source_target_pairs={{0,4},{4,0},{8,12},{12,8},{1,5},{5,1},{9,13},{13,9},{2,6},{6,2},{1... | collective-permute-start | bytes 442376 | tf_op jit(solution)/shard_map/ppermute | solution.py:276
  35.0 13.8 %collective-permute-start.10 = (bf16[3,96,256]{2,1,0:T(8,128)(2,1)S(1)}, bf16[3,96,256]{2,1,0:T(8,128)(2,1)S(1)}, u32[]{:S(2)}, u32[]{:S(2)}) collective-permute-start(bf16[3,96,256]{2,1,0:T(8,128)(2,1)S(1)} %add_convert_fusion.refs_0_), channel_id=1, source_target_pairs={{0,12},{4,8},{8,4},{12,0},{1,13},{5,9},{9,5},{13,1},{2,14},{6,10},... | collective-permute-start | bytes 442376 | tf_op jit(solution)/shard_map/ppermute | solution.py:276
  49.5 1.6 %collective-permute-start.11 = (bf16[3,128,256]{2,1,0:T(8,128)(2,1)S(1)}, bf16[3,128,256]{2,1,0:T(8,128)(2,1)S(1)}, u32[]{:S(2)}, u32[]{:S(2)}) collective-permute-start(bf16[3,128,256]{2,1,0:T(8,128)(2,1)S(1)} %get-tuple-element.53.small), channel_id=1, source_target_pairs={{0,1},{1,0},{2,3},{3,2},{4,5},{5,4},{6,7},{7,6},{8,9},{9,8},{10,11... | collective-permute-start | bytes 589832 | tf_op jit(solution)/shard_map/ppermute | solution.py:284
  51.1 8.5 %collective-permute-start.12 = (bf16[3,256,256]{2,1,0:T(8,128)(2,1)S(1)}, bf16[3,256,256]{2,1,0:T(8,128)(2,1)S(1)}, u32[]{:S(2)}, u32[]{:S(2)}) collective-permute-start(bf16[3,256,256]{2,1,0:T(8,128)(2,1)S(1)} %get-tuple-element.54.large), channel_id=1, source_target_pairs={{1,3},{3,1},{5,7},{7,5},{9,11},{11,9},{13,15},{15,13},{17,19},{19,... | collective-permute-start | bytes 1179656 | tf_op jit(solution)/shard_map/ppermute | solution.py:286
  63.5 2.4 %collective-permute-start.13 = (bf16[512,256]{1,0:T(8,128)(2,1)S(1)}, bf16[512,256]{1,0:T(8,128)(2,1)S(1)}, u32[]{:S(2)}, u32[]{:S(2)}) collective-permute-start(bf16[512,256]{1,0:T(8,128)(2,1)S(1)} %get-tuple-element.59), channel_id=1, source_target_pairs={{0,2},{2,0},{4,6},{6,4},{8,10},{10,8},{12,14},{14,12},{16,18},{18,... | collective-permute-start | bytes 786440 | tf_op jit(solution)/shard_map/ppermute | solution.py:295
  65.8 1.4 %collective-permute-start.14 = (bf16[256,256]{1,0:T(8,128)(2,1)S(1)}, bf16[256,256]{1,0:T(8,128)(2,1)S(1)}, u32[]{:S(2)}, u32[]{:S(2)}) collective-permute-start(bf16[256,256]{1,0:T(8,128)(2,1)S(1)} %get-tuple-element.61), channel_id=1, source_target_pairs={{0,1},{1,0},{2,3},{3,2},{4,5},{5,4},{6,7},{7,6},{8,9},{9,8},{10,11... | collective-permute-start | bytes 393224 | tf_op jit(solution)/shard_map/ppermute | solution.py:302
  65.9 1.5 %collective-permute-start.15 = (bf16[256,256]{1,0:T(8,128)(2,1)S(1)}, bf16[256,256]{1,0:T(8,128)(2,1)S(1)}, u32[]{:S(2)}, u32[]{:S(2)}) collective-permute-start(bf16[256,256]{1,0:T(8,128)(2,1)S(1)} %slice.11), channel_id=1, source_target_pairs={{0,1},{1,0},{2,3},{3,2},{4,5},{5,4},{6,7},{7,6},{8,9},{9,8},{10,11... | collective-permute-start | bytes 393224 | tf_op jit(solution)/shard_map/ppermute | solution.py:304

commit v8 on v7

--- a/solution.py
+++ b/solution.py
@@ -95,14 +95,13 @@
 
 
 def collect_kernel(n_patch, where, *refs):
-    parts, pieces = refs[:n_patch], refs[n_patch:]
-    for part, shift in zip(parts, exchange_order(n_patch, True)):
+    parts, (later, small) = refs[:n_patch], refs[n_patch:]
+    large, rest = LARGE // n_patch, SMALL // n_patch
+    for k, (part, shift) in enumerate(zip(parts, exchange_order(n_patch, True))):
+        if k:
+            later[:, (k - 1) * large : k * large] = part[:, :large]
         chunk = where[1] ^ shift
-        at = 0
-        for piece in pieces:
-            size = piece.shape[1] // n_patch
-            piece[:, pl.ds(pl.multiple_of(chunk * size, size), size)] = part[:, at : at + size]
-            at += size
+        small[:, pl.ds(pl.multiple_of(chunk * rest, rest), rest)] = part[:, large:]
 
 
 def decode(rows, fresh, gain):
@@ -125,18 +124,24 @@
     begun[...] = mm(decode(own[...], fresh, gain), product)
 
 
-def far_kernel(where, large, small, rest, half, fast, gains, qry, out, fresh, grads):
+def far_kernel(n_patch, where, own, later, own_other, later_other, small, rest, fast, gains, qry, out, fresh, grads):
+    size = LARGE // n_patch
+
+    def place(start, own, later):
+        for k, shift in enumerate(exchange_order(n_patch, True)):
+            rows = pl.ds(pl.multiple_of(start + (where[1] ^ shift) * size, size), size)
+            grads[:, rows] = later[:, (k - 1) * size : k * size] if k else own[...]
+
+    place(where[8] * where[9] * LARGE, own, later)
+
     @pl.when(where[8] == 0)
     def _():
-        grads[:, :LARGE] = large[...]
         grads[:, LARGE : LARGE + SMALL] = small[...]
         grads[:, LARGE + SMALL :] = rest[...]
 
     @pl.when(where[8] == 1)
     def _():
-        at = pl.multiple_of(where[9] * LARGE, LARGE)
-        grads[:, pl.ds(at, LARGE)] = large[...]
-        grads[:, pl.ds(pl.multiple_of(LARGE - at, LARGE), LARGE)] = half[...]
+        place((1 - where[9]) * LARGE, own_other, later_other)
 
     ortho = []
     for kind in range(3):
@@ -274,21 +279,23 @@
     across = lax.ppermute(jnp.concatenate([other, swapped[n_qry:]]), every, ours)
     own = own.astype(BF)
     parts = [lax.ppermute(own, "patch", pairs(s)) for s in exchange_order(n_patch, True)[1:]]
-    parts[0], across = lax.optimization_barrier((parts[0], across))
-    large, small = call(
+    own_large = own[:, : LARGE // n_patch]
+    own_other = lax.ppermute(own_large, every, seconds)
+    parts[0], across, own_other = lax.optimization_barrier((parts[0], across, own_other))
+    later, small = call(
         functools.partial(collect_kernel, n_patch),
         where,
         [own, *parts],
-        [jax.ShapeDtypeStruct(s.shape, BF) for s in sums],
+        [jax.ShapeDtypeStruct((3, n, HD), BF) for n in (LARGE - LARGE // n_patch, SMALL)],
     )
     rest = lax.ppermute(small, "head", swap)
-    large, rest = lax.optimization_barrier((large, rest))
-    half = lax.ppermute(large, every, seconds)
+    later, rest = lax.optimization_barrier((later, rest))
+    later_other = lax.ppermute(later, every, seconds)
     gains = out_gain.reshape(1, width)
     normed, fresh = call(
-        far_kernel,
-        where,
-        [large, small, rest, half, mine, gains, across],
+        functools.partial(far_kernel, n_patch),
+        where,
+        [own_large, later, own_other, later_other, small, rest, mine, gains, across],
         [jax.ShapeDtypeStruct((2 * n_qry, HD), BF), jax.ShapeDtypeStruct((3, FF, HD), BF)],
         [pltpu.VMEM((3, FF, HD), BF)],
     )

time: 69.3 us -> 68.2 us (0.984)
  waiting for transfers between devices: 36.7 us -> 33.5 us
  starting transfers between devices: 13.7 us -> 15.9 us
    ppermute x3, waiting for transfers between devices: 13.5 us -> 7.82 us  [local(): lax.ppermute(own, 'patch', pairs(s))]
    ppermute x1 -> x2, waiting for transfers between devices: 6.25 us -> 8.7 us  [the longest x1 5.21 us: local(): later_other = lax.ppermute(later, every, seconds)]
    ppermute x1 -> x2, starting transfers between devices: 2.16 us -> 4.3 us  [the longest x1 2.15 us: local(): own_other = lax.ppermute(own_large, every, seconds)]
  transfers between devices with their start and end apart: 16 -> 17, of which waited for: 12 -> 11; matrix products, arithmetic and copies ran while one was open for 3% -> 3% of each run, Pallas kernels for 14% -> 14%
where the time goes in v8:
time: 68.2 us; the launch traced here: 68 us
  waiting for transfers between devices  33.5 us (49%)
  starting transfers between devices  15.9 us (23%)
  Pallas kernels  15.9 us (23%)
  local copies, waits for them, and re-layouts  2.43 us (4%)
    pallas_call x7, Pallas kernels, call(): pl.pallas_call(kernel, out_shape=outs, grid_spec=pltpu.PrefetchScalarGrid...  15.9 us
    ppermute x3, waiting for transfers between devices, local(): lax.ppermute(chunks[k], 'patch', pairs(order[k]))  9.98 us
    ppermute x3, waiting for transfers between devices, local(): lax.ppermute(own, 'patch', pairs(s))  7.82 us
    ppermute x1, waiting for transfers between devices, local(): later_other = lax.ppermute(later, every, seconds)  5.21 us
    ppermute x1, waiting for transfers between devices, local(): lax.ppermute(tokens, 'view', rotate(n_view, s))  3.6 us
    ppermute x3, starting transfers between devices, local(): lax.ppermute(chunks[k], 'patch', pairs(order[k]))  3.56 us
    ppermute x1, waiting for transfers between devices, local(): own_other = lax.ppermute(own_large, every, seconds)  3.49 us
    ppermute x3, starting transfers between devices, local(): lax.ppermute(own, 'patch', pairs(s))  3.25 us
  transfers between devices with their start and end apart: 17, of which 11 were waited for; matrix products, arithmetic and copies ran while one was open for 3% of the time, Pallas kernels for 14%

profile of v8, /device:TPU:11, one launch (start us, length us, event | category | flops | bytes accessed | tf_op | source)
XLA Modules:
  0.0 68.0 jit_solution(9727121316433806640)
XLA Ops:
  0.0 0.7 %collective-permute-start = (bf16[256,768]{1,0:T(8,128)(2,1)}, bf16[256,768]{1,0:T(8,128)(2,1)S(1)}, u32[]{:S(2)}, u32[]{:S(2)}) collective-permute-start(bf16[256,768]{1,0:T(8,128)(2,1)} %refs_0_.1), channel_id=1, source_target_pairs={{0,1},{1,0},{2,3},{3,2},{4,5},{5,4},{6,7},{7,6},{8,9},{9,8},{10,11... | collective-permute-start | bytes 1179656 | tf_op jit(solution)/shard_map/ppermute | solution.py:238
  0.8 0.3 collective-permute-start.1
  1.0 0.1 stack.37.where
  1.1 0.6 copy-done
  1.7 0.0 copy-start.2
  1.7 0.0 copy-start.3
  1.8 1.6 %constant_dynamic-slice_fusion = (bf16[768,256]{1,0:T(8,128)(2,1)S(1)}, bf16[768,256]{1,0:T(8,128)(2,1)S(1)}, bf16[768,256]{1,0:T(8,128)(2,1)S(1)}, bf16[768,256]{1,0:T(8,128)(2,1)S(1)}) fusion(bf16[768,1536]{1,0:T(8,128)(2,1)} %param.9, s32[]{:T(128)S(6)} %select_n.59, s32[]{:T(128)S(6)} %select_n.54, s32[]{:T(128)S(6)} %select_n.53, s32[]{:T(128)S(6)} %select_n.58), kind=kLoop, calls=%fused_computation.5 | loop fusion | bytes 3145744 | tf_op jit(solution)/shard_map/dynamic_slice | solution.py:244
  3.4 0.0 collective-permute-done.refs_1_
  3.4 3.5 %shard_map.82 = (f32[3,256,256]{2,1,0:T(8,128)S(1)}, f32[3,128,256]{2,1,0:T(8,128)S(1)}) custom-call(s32[10]{0:T(128)S(1)} %stack.37.where, bf16[256,768]{1,0:T(8,128)(2,1)S(1)} %copy-done.4, bf16[256,768]{1,0:T(8,128)(2,1)S(1)} %collective-permute-done.refs_1_, bf16[3,768]{1,0:T(4,128)(2,1)S(1)} %copy-done.5, ...), custom_call_target="tpu_custom_call" | custom-call | tf_op jit(solution)/shard_map/pallas_call | solution.py:194
  6.9 1.1 %shard_map.83 = (bf16[256,256]{1,0:T(8,128)(2,1)S(1)}, bf16[512,256]{1,0:T(8,128)(2,1)S(1)}, bf16[256,256]{1,0:T(8,128)(2,1)S(1)}) custom-call(s32[10]{0:T(128)S(1)} %stack.37.where, bf16[256,768]{1,0:T(8,128)(2,1)S(1)} %copy-done.3, bf16[768,768]{1,0:T(8,128)(2,1)S(1)} %copy-done.2), custom_call_target="tpu_custom_call" | custom-call | tf_op jit(solution)/shard_map/pallas_call | solution.py:194
  8.1 3.6 %collective-permute-done.1.refs_0_ = bf16[256,768]{1,0:T(8,128)(2,1)S(1)} collective-permute-done((bf16[256,768]{1,0:T(8,128)(2,1)}, bf16[256,768]{1,0:T(8,128)(2,1)S(1)}, u32[]{:S(2)}, u32[]{:S(2)}) %collective-permute-start.1) | collective-permute-done | bytes 393248 | tf_op jit(solution)/shard_map/ppermute | solution.py:237
  11.7 0.8 %collective-permute-start.2 = (bf16[256,768]{1,0:T(8,128)(2,1)S(1)}, bf16[256,768]{1,0:T(8,128)(2,1)S(1)}, u32[]{:S(2)}, u32[]{:S(2)}) collective-permute-start(bf16[256,768]{1,0:T(8,128)(2,1)S(1)} %collective-permute-done.1.refs_0_), channel_id=1, source_target_pairs={{0,1},{1,0},{2,3},{3,2},{4,5},{5,4},{6,7},{7,6},{8,9},{9,8},{10,11... | collective-permute-start | bytes 1179656 | tf_op jit(solution)/shard_map/ppermute | solution.py:262
  12.5 1.3 %collective-permute-done.2.refs_1_ = bf16[256,768]{1,0:T(8,128)(2,1)S(1)} collective-permute-done((bf16[256,768]{1,0:T(8,128)(2,1)S(1)}, bf16[256,768]{1,0:T(8,128)(2,1)S(1)}, u32[]{:S(2)}, u32[]{:S(2)}) %collective-permute-start.2) | collective-permute-done | bytes 393248 | tf_op jit(solution)/shard_map/ppermute | solution.py:262
  13.9 0.4 collective-permute-start.3
  14.2 3.5 %shard_map.84 = (f32[3,96,256]{2,1,0:T(8,128)S(1)}, bf16[3,96,256]{2,1,0:T(8,128)(2,1)S(1)}, bf16[3,96,256]{2,1,0:T(8,128)(2,1)S(1)}, bf16[3,96,256]{2,1,0:T(8,128)(2,1)S(1)}) custom-call(s32[10]{0:T(128)S(1)} %stack.37.where, bf16[256,768]{1,0:T(8,128)(2,1)S(1)} %collective-permute-done.1.refs_0_, bf16[256,768]{1,0:T(8,128)(2,1)S(1)} %collective-permute-done.2.refs_1_, ...), custom_call_target="tpu_custom_call" | custom-call | tf_op jit(solution)/shard_map/pallas_call | solution.py:194
  17.7 0.0 copy-start.6
  17.8 1.4 %collective-permute-start.6 = (bf16[3,96,256]{2,1,0:T(8,128)(2,1)S(1)}, bf16[3,96,256]{2,1,0:T(8,128)(2,1)S(1)}, u32[]{:S(2)}, u32[]{:S(2)}) collective-permute-start(bf16[3,96,256]{2,1,0:T(8,128)(2,1)S(1)} %get-tuple-element.50), channel_id=1, source_target_pairs={{0,12},{4,8},{8,4},{12,0},{1,13},{5,9},{9,5},{13,1},{2,14},{6,10},... | collective-permute-start | bytes 442376 | tf_op jit(solution)/shard_map/ppermute | solution.py:274
  19.1 2.2 %collective-permute-start.5 = (bf16[3,96,256]{2,1,0:T(8,128)(2,1)S(1)}, bf16[3,96,256]{2,1,0:T(8,128)(2,1)S(1)}, u32[]{:S(2)}, u32[]{:S(2)}) collective-permute-start(bf16[3,96,256]{2,1,0:T(8,128)(2,1)S(1)} %get-tuple-element.49), channel_id=1, source_target_pairs={{0,4},{4,0},{8,12},{12,8},{1,5},{5,1},{9,13},{13,9},{2,6},{6,2},{1... | collective-permute-start | bytes 442376 | tf_op jit(solution)/shard_map/ppermute | solution.py:274
  21.3 0.0 collective-permute-start.4
  21.3 0.0 collective-permute-done.3
  21.4 0.7 collective-permute-start.8
  22.1 4.8 %collective-permute-done.6 = bf16[3,96,256]{2,1,0:T(8,128)(2,1)S(1)} collective-permute-done((bf16[3,96,256]{2,1,0:T(8,128)(2,1)S(1)}, bf16[3,96,256]{2,1,0:T(8,128)(2,1)S(1)}, u32[]{:S(2)}, u32[]{:S(2)}) %collective-permute-start.6) | collective-permute-done | bytes 147488 | tf_op jit(solution)/shard_map/ppermute | solution.py:274
  26.9 2.1 %collective-permute-done.5 = bf16[3,96,256]{2,1,0:T(8,128)(2,1)S(1)} collective-permute-done((bf16[3,96,256]{2,1,0:T(8,128)(2,1)S(1)}, bf16[3,96,256]{2,1,0:T(8,128)(2,1)S(1)}, u32[]{:S(2)}, u32[]{:S(2)}) %collective-permute-start.5) | collective-permute-done | bytes 147488 | tf_op jit(solution)/shard_map/ppermute | solution.py:274
  28.9 3.1 %collective-permute-done.4 = bf16[3,96,256]{2,1,0:T(8,128)(2,1)S(1)} collective-permute-done((bf16[3,96,256]{2,1,0:T(8,128)(2,1)S(1)}, bf16[3,96,256]{2,1,0:T(8,128)(2,1)S(1)}, u32[]{:S(2)}, u32[]{:S(2)}) %collective-permute-start.4) | collective-permute-done | bytes 147488 | tf_op jit(solution)/shard_map/ppermute | solution.py:274
  32.0 0.1 add_convert_fusion.refs_0_
  32.1 0.0 copy-start.1
  32.1 2.9 %collective-permute-start.7 = (bf16[3,96,256]{2,1,0:T(8,128)(2,1)S(1)}, bf16[3,96,256]{2,1,0:T(8,128)(2,1)S(1)}, u32[]{:S(2)}, u32[]{:S(2)}) collective-permute-start(bf16[3,96,256]{2,1,0:T(8,128)(2,1)S(1)} %add_convert_fusion.refs_0_), channel_id=1, source_target_pairs={{0,8},{4,12},{8,0},{12,4},{1,9},{5,13},{9,1},{13,5},{2,10},{6,14},... | collective-permute-start | bytes 442376 | tf_op jit(solution)/shard_map/ppermute | solution.py:281
  35.0 0.0 collective-permute-start.10
  35.0 0.4 collective-permute-start.11
  35.4 2.2 %collective-permute-start.9 = (bf16[3,64,256]{2,1,0:T(8,128)(2,1)S(1)}, bf16[3,64,256]{2,1,0:T(8,128)(2,1)S(1)}, u32[]{:S(2)}, u32[]{:S(2)}) collective-permute-start(bf16[3,64,256]{2,1,0:T(8,128)(2,1)S(1)} %slice.16.own), channel_id=1, source_target_pairs={{1,3},{3,1},{5,7},{7,5},{9,11},{11,9},{13,15},{15,13},{17,19},{19,... | collective-permute-start | bytes 294920 | tf_op jit(solution)/shard_map/ppermute | solution.py:283
  37.5 3.5 %collective-permute-done.9.own_other = bf16[3,64,256]{2,1,0:T(8,128)(2,1)S(1)} collective-permute-done((bf16[3,64,256]{2,1,0:T(8,128)(2,1)S(1)}, bf16[3,64,256]{2,1,0:T(8,128)(2,1)S(1)}, u32[]{:S(2)}, u32[]{:S(2)}) %collective-permute-start.9) | collective-permute-done | bytes 98336 | tf_op jit(solution)/shard_map/ppermute | solution.py:283
  41.0 0.0 collective-permute-done.7.refs_1_
  41.0 0.0 collective-permute-done.8.qry
  41.0 7.8 %collective-permute-done.11.refs_3_ = bf16[3,96,256]{2,1,0:T(8,128)(2,1)S(1)} collective-permute-done((bf16[3,96,256]{2,1,0:T(8,128)(2,1)S(1)}, bf16[3,96,256]{2,1,0:T(8,128)(2,1)S(1)}, u32[]{:S(2)}, u32[]{:S(2)}) %collective-permute-start.11) | collective-permute-done | bytes 147488 | tf_op jit(solution)/shard_map/ppermute | solution.py:281
  48.9 0.6 shard_map.85
  49.4 0.5 collective-permute-start.12
  50.0 1.1 %collective-permute-done.12.rest = bf16[3,128,256]{2,1,0:T(8,128)(2,1)S(1)} collective-permute-done((bf16[3,128,256]{2,1,0:T(8,128)(2,1)S(1)}, bf16[3,128,256]{2,1,0:T(8,128)(2,1)S(1)}, u32[]{:S(2)}, u32[]{:S(2)}) %collective-permute-start.12) | collective-permute-done | bytes 196640 | tf_op jit(solution)/shard_map/ppermute | solution.py:291
  51.1 2.1 %collective-permute-start.13 = (bf16[3,192,256]{2,1,0:T(8,128)(2,1)S(1)}, bf16[3,192,256]{2,1,0:T(8,128)(2,1)S(1)}, u32[]{:S(2)}, u32[]{:S(2)}) collective-permute-start(bf16[3,192,256]{2,1,0:T(8,128)(2,1)S(1)} %get-tuple-element.55.later), channel_id=1, source_target_pairs={{1,3},{3,1},{5,7},{7,5},{9,11},{11,9},{13,15},{15,13},{17,19},{19,... | collective-permute-start | bytes 884744 | tf_op jit(solution)/shard_map/ppermute | solution.py:293
  53.2 0.1 dynamic-slice_bitcast_fusion.fast
  53.3 5.2 %collective-permute-done.13.later_other = bf16[3,192,256]{2,1,0:T(8,128)(2,1)S(1)} collective-permute-done((bf16[3,192,256]{2,1,0:T(8,128)(2,1)S(1)}, bf16[3,192,256]{2,1,0:T(8,128)(2,1)S(1)}, u32[]{:S(2)}, u32[]{:S(2)}) %collective-permute-start.13) | collective-permute-done | bytes 294944 | tf_op jit(solution)/shard_map/ppermute | solution.py:293
  58.5 3.9 %shard_map.86 = (bf16[512,256]{1,0:T(8,128)(2,1)S(1)}, bf16[3,512,256]{2,1,0:T(8,128)(2,1)S(1)}) custom-call(s32[10]{0:T(128)S(1)} %stack.37.where, bf16[3,64,256]{2,1,0:T(8,128)(2,1)S(1)} %slice.16.own, bf16[3,192,256]{2,1,0:T(8,128)(2,1)S(1)} %get-tuple-element.55.later, bf16[3,64,256]{2,1,0:T(8,128)(2,1)S(1)} %collective-permute-done.9.own_other, ...), custom_call_target="tpu_custom_call" | custom-call | tf_op jit(solution)/shard_map/pallas_call | solution.py:194
  62.4 0.7 collective-permute-start.14
  63.1 1.6 %shard_map.87 = (bf16[256,256]{1,0:T(8,128)(2,1)S(1)}, f32[256,768]{1,0:T(8,128)S(1)}) custom-call(s32[10]{0:T(128)S(1)} %stack.37.where, bf16[256,256]{1,0:T(8,128)(2,1)S(1)} %get-tuple-element.37.own, bf16[256,256]{1,0:T(8,128)(2,1)S(1)} %get-tuple-element.70.other, bf16[3,512,256]{2,1,0:T(8,128)(2,1)S(1)} %get-tuple-element.59.fresh, ...), custom_call_target="tpu_custom_call" | custom-call | tf_op jit(solution)/shard_map/pallas_call | solution.py:194
  64.7 0.1 collective-permute-start.15
  64.8 0.6 collective-permute-start.16
  65.4 0.8 %collective-permute-done.15.near = bf16[256,256]{1,0:T(8,128)(2,1)S(1)} collective-permute-done((bf16[256,256]{1,0:T(8,128)(2,1)S(1)}, bf16[256,256]{1,0:T(8,128)(2,1)S(1)}, u32[]{:S(2)}, u32[]{:S(2)}) %collective-permute-start.15) | collective-permute-done | bytes 131104 | tf_op jit(solution)/shard_map/ppermute | solution.py:309
  66.1 0.2 collective-permute-done.16.relayed
  66.4 1.7 %shard_map.88 = bf16[256,768]{1,0:T(8,128)(2,1)} custom-call(s32[10]{0:T(128)S(1)} %stack.37.where, f32[256,768]{1,0:T(8,128)S(1)} %get-tuple-element.62.begun, bf16[256,256]{1,0:T(8,128)(2,1)S(1)} %collective-permute-done.15.near, bf16[512,256]{1,0:T(8,128)(2,1)S(1)} %collective-permute-done.14.back, bf16[256,256]{1,0:T(8,128)(2,1)S(1)} %collective-permute-done.16.relayed, ...), custom_call_target="tpu_custom_call" | custom-call | tf_op jit(solution)/shard_map/pallas_call | solution.py:194
  (18 shorter events, 0.1 us)
Async XLA Ops:
  0.0 1.7 %copy-start = (bf16[512,3,3,256]{3,0,2,1:T(8,128)(2,1)S(1)}, bf16[512,3,3,256]{3,0,2,1:T(8,128)(2,1)}, u32[]{:S(2)}) copy-start(bf16[512,3,3,256]{3,0,2,1:T(8,128)(2,1)} %param.11) | copy-start | bytes 7077892
  0.0 3.4 %copy-start.4 = (bf16[256,768]{1,0:T(8,128)(2,1)S(1)}, bf16[256,768]{1,0:T(8,128)(2,1)}, u32[]{:S(2)}) copy-start(bf16[256,768]{1,0:T(8,128)(2,1)} %refs_0_.1) | copy-start | bytes 1179652
  0.0 3.4 %copy-start.5 = (bf16[3,768]{1,0:T(4,128)(2,1)S(1)}, bf16[3,768]{1,0:T(4,128)(2,1)}, u32[]{:S(2)}) copy-start(bf16[3,768]{1,0:T(4,128)(2,1)} %refs_2_.3) | copy-start | bytes 13828
  0.0 3.3 %collective-permute-start = (bf16[256,768]{1,0:T(8,128)(2,1)}, bf16[256,768]{1,0:T(8,128)(2,1)S(1)}, u32[]{:S(2)}, u32[]{:S(2)}) collective-permute-start(bf16[256,768]{1,0:T(8,128)(2,1)} %refs_0_.1), channel_id=1, source_target_pairs={{0,1},{1,0},{2,3},{3,2},{4,5},{5,4},{6,7},{7,6},{8,9},{9,8},{10,11... | collective-permute-start | bytes 1179656 | tf_op jit(solution)/shard_map/ppermute | solution.py:238
  0.8 10.9 %collective-permute-start.1 = (bf16[256,768]{1,0:T(8,128)(2,1)}, bf16[256,768]{1,0:T(8,128)(2,1)S(1)}, u32[]{:S(2)}, u32[]{:S(2)}) collective-permute-start(bf16[256,768]{1,0:T(8,128)(2,1)} %refs_0_.1), channel_id=1, source_target_pairs={{0,2},{2,0},{1,3},{3,1},{4,6},{6,4},{5,7},{7,5},{8,10},{10,8},{9,1... | collective-permute-start | bytes 1179656 | tf_op jit(solution)/shard_map/ppermute | solution.py:237
  1.7 5.2 %copy-start.2 = (bf16[768,768]{1,0:T(8,128)(2,1)S(1)}, bf16[768,768]{1,0:T(8,128)(2,1)}, u32[]{:S(2)}) copy-start(bf16[768,768]{1,0:T(8,128)(2,1)} %w_query.1) | copy-start | bytes 3538948
  1.7 5.2 %copy-start.3 = (bf16[256,768]{1,0:T(8,128)(2,1)S(1)}, bf16[256,768]{1,0:T(8,128)(2,1)}, u32[]{:S(2)}) copy-start(bf16[256,768]{1,0:T(8,128)(2,1)} %queries) | copy-start | bytes 1179652
  11.7 2.2 %collective-permute-start.2 = (bf16[256,768]{1,0:T(8,128)(2,1)S(1)}, bf16[256,768]{1,0:T(8,128)(2,1)S(1)}, u32[]{:S(2)}, u32[]{:S(2)}) collective-permute-start(bf16[256,768]{1,0:T(8,128)(2,1)S(1)} %collective-permute-done.1.refs_0_), channel_id=1, source_target_pairs={{0,1},{1,0},{2,3},{3,2},{4,5},{5,4},{6,7},{7,6},{8,9},{9,8},{10,11... | collective-permute-start | bytes 1179656 | tf_op jit(solution)/shard_map/ppermute | solution.py:262
  13.9 7.5 %collective-permute-start.3 = (bf16[512,256]{1,0:T(8,128)(2,1)S(1)}, bf16[512,256]{1,0:T(8,128)(2,1)S(1)}, u32[]{:S(2)}, u32[]{:S(2)}) collective-permute-start(bf16[512,256]{1,0:T(8,128)(2,1)S(1)} %get-tuple-element.42), channel_id=1, source_target_pairs={{0,1},{1,0},{2,3},{3,2},{4,5},{5,4},{6,7},{7,6},{8,9},{9,8},{10,11... | collective-permute-start | bytes 786440 | tf_op jit(solution)/shard_map/ppermute | solution.py:264
  17.7 35.5 %copy-start.6 = (bf16[768]{0:T(1024)(128)(2,1)S(1)}, bf16[768]{0:T(1024)(128)(2,1)}, u32[]{:S(2)}) copy-start(bf16[768]{0:T(1024)(128)(2,1)} %param.14) | copy-start | bytes 4612
  17.8 9.1 %collective-permute-start.6 = (bf16[3,96,256]{2,1,0:T(8,128)(2,1)S(1)}, bf16[3,96,256]{2,1,0:T(8,128)(2,1)S(1)}, u32[]{:S(2)}, u32[]{:S(2)}) collective-permute-start(bf16[3,96,256]{2,1,0:T(8,128)(2,1)S(1)} %get-tuple-element.50), channel_id=1, source_target_pairs={{0,12},{4,8},{8,4},{12,0},{1,13},{5,9},{9,5},{13,1},{2,14},{6,10},... | collective-permute-start | bytes 442376 | tf_op jit(solution)/shard_map/ppermute | solution.py:274
  19.1 9.8 %collective-permute-start.5 = (bf16[3,96,256]{2,1,0:T(8,128)(2,1)S(1)}, bf16[3,96,256]{2,1,0:T(8,128)(2,1)S(1)}, u32[]{:S(2)}, u32[]{:S(2)}) collective-permute-start(bf16[3,96,256]{2,1,0:T(8,128)(2,1)S(1)} %get-tuple-element.49), channel_id=1, source_target_pairs={{0,4},{4,0},{8,12},{12,8},{1,5},{5,1},{9,13},{13,9},{2,6},{6,2},{1... | collective-permute-start | bytes 442376 | tf_op jit(solution)/shard_map/ppermute | solution.py:274
  21.3 10.7 %collective-permute-start.4 = (bf16[3,96,256]{2,1,0:T(8,128)(2,1)S(1)}, bf16[3,96,256]{2,1,0:T(8,128)(2,1)S(1)}, u32[]{:S(2)}, u32[]{:S(2)}) collective-permute-start(bf16[3,96,256]{2,1,0:T(8,128)(2,1)S(1)} %get-tuple-element.48), channel_id=1, source_target_pairs={{0,8},{4,12},{8,0},{12,4},{1,9},{5,13},{9,1},{13,5},{2,10},{6,14},... | collective-permute-start | bytes 442376 | tf_op jit(solution)/shard_map/ppermute | solution.py:274
  21.4 19.7 %collective-permute-start.8 = (bf16[512,256]{1,0:T(8,128)(2,1)S(1)}, bf16[512,256]{1,0:T(8,128)(2,1)S(1)}, u32[]{:S(2)}, u32[]{:S(2)}) collective-permute-start(bf16[512,256]{1,0:T(8,128)(2,1)S(1)} %pad_maximum_fusion), channel_id=1, source_target_pairs={{0,2},{2,0},{4,6},{6,4},{8,10},{10,8},{12,14},{14,12},{16,18},{18,... | collective-permute-start | bytes 786440 | tf_op jit(solution)/shard_map/ppermute | solution.py:279
  32.1 31.0 %copy-start.1 = (bf16[768,768]{1,0:T(8,128)(2,1)S(1)}, bf16[768,768]{1,0:T(8,128)(2,1)}, u32[]{:S(2)}) copy-start(bf16[768,768]{1,0:T(8,128)(2,1)} %w_out.3) | copy-start | bytes 3538948
  32.1 8.9 %collective-permute-start.7 = (bf16[3,96,256]{2,1,0:T(8,128)(2,1)S(1)}, bf16[3,96,256]{2,1,0:T(8,128)(2,1)S(1)}, u32[]{:S(2)}, u32[]{:S(2)}) collective-permute-start(bf16[3,96,256]{2,1,0:T(8,128)(2,1)S(1)} %add_convert_fusion.refs_0_), channel_id=1, source_target_pairs={{0,8},{4,12},{8,0},{12,4},{1,9},{5,13},{9,1},{13,5},{2,10},{6,14},... | collective-permute-start | bytes 442376 | tf_op jit(solution)/shard_map/ppermute | solution.py:281
  35.0 6.0 %collective-permute-start.10 = (bf16[3,96,256]{2,1,0:T(8,128)(2,1)S(1)}, bf16[3,96,256]{2,1,0:T(8,128)(2,1)S(1)}, u32[]{:S(2)}, u32[]{:S(2)}) collective-permute-start(bf16[3,96,256]{2,1,0:T(8,128)(2,1)S(1)} %add_convert_fusion.refs_0_), channel_id=1, source_target_pairs={{0,4},{4,0},{8,12},{12,8},{1,5},{5,1},{9,13},{13,9},{2,6},{6,2},{1... | collective-permute-start | bytes 442376 | tf_op jit(solution)/shard_map/ppermute | solution.py:281
  35.0 13.8 %collective-permute-start.11 = (bf16[3,96,256]{2,1,0:T(8,128)(2,1)S(1)}, bf16[3,96,256]{2,1,0:T(8,128)(2,1)S(1)}, u32[]{:S(2)}, u32[]{:S(2)}) collective-permute-start(bf16[3,96,256]{2,1,0:T(8,128)(2,1)S(1)} %add_convert_fusion.refs_0_), channel_id=1, source_target_pairs={{0,12},{4,8},{8,4},{12,0},{1,13},{5,9},{9,5},{13,1},{2,14},{6,10},... | collective-permute-start | bytes 442376 | tf_op jit(solution)/shard_map/ppermute | solution.py:281
  35.4 5.7 %collective-permute-start.9 = (bf16[3,64,256]{2,1,0:T(8,128)(2,1)S(1)}, bf16[3,64,256]{2,1,0:T(8,128)(2,1)S(1)}, u32[]{:S(2)}, u32[]{:S(2)}) collective-permute-start(bf16[3,64,256]{2,1,0:T(8,128)(2,1)S(1)} %slice.16.own), channel_id=1, source_target_pairs={{1,3},{3,1},{5,7},{7,5},{9,11},{11,9},{13,15},{15,13},{17,19},{19,... | collective-permute-start | bytes 294920 | tf_op jit(solution)/shard_map/ppermute | solution.py:283
  49.4 1.6 %collective-permute-start.12 = (bf16[3,128,256]{2,1,0:T(8,128)(2,1)S(1)}, bf16[3,128,256]{2,1,0:T(8,128)(2,1)S(1)}, u32[]{:S(2)}, u32[]{:S(2)}) collective-permute-start(bf16[3,128,256]{2,1,0:T(8,128)(2,1)S(1)} %get-tuple-element.54.small), channel_id=1, source_target_pairs={{0,1},{1,0},{2,3},{3,2},{4,5},{5,4},{6,7},{7,6},{8,9},{9,8},{10,11... | collective-permute-start | bytes 589832 | tf_op jit(solution)/shard_map/ppermute | solution.py:291
  51.1 7.5 %collective-permute-start.13 = (bf16[3,192,256]{2,1,0:T(8,128)(2,1)S(1)}, bf16[3,192,256]{2,1,0:T(8,128)(2,1)S(1)}, u32[]{:S(2)}, u32[]{:S(2)}) collective-permute-start(bf16[3,192,256]{2,1,0:T(8,128)(2,1)S(1)} %get-tuple-element.55.later), channel_id=1, source_target_pairs={{1,3},{3,1},{5,7},{7,5},{9,11},{11,9},{13,15},{15,13},{17,19},{19,... | collective-permute-start | bytes 884744 | tf_op jit(solution)/shard_map/ppermute | solution.py:293
  62.4 2.4 %collective-permute-start.14 = (bf16[512,256]{1,0:T(8,128)(2,1)S(1)}, bf16[512,256]{1,0:T(8,128)(2,1)S(1)}, u32[]{:S(2)}, u32[]{:S(2)}) collective-permute-start(bf16[512,256]{1,0:T(8,128)(2,1)S(1)} %get-tuple-element.61), channel_id=1, source_target_pairs={{0,2},{2,0},{4,6},{6,4},{8,10},{10,8},{12,14},{14,12},{16,18},{18,... | collective-permute-start | bytes 786440 | tf_op jit(solution)/shard_map/ppermute | solution.py:302
  64.7 1.4 %collective-permute-start.15 = (bf16[256,256]{1,0:T(8,128)(2,1)S(1)}, bf16[256,256]{1,0:T(8,128)(2,1)S(1)}, u32[]{:S(2)}, u32[]{:S(2)}) collective-permute-start(bf16[256,256]{1,0:T(8,128)(2,1)S(1)} %get-tuple-element.63), channel_id=1, source_target_pairs={{0,1},{1,0},{2,3},{3,2},{4,5},{5,4},{6,7},{7,6},{8,9},{9,8},{10,11... | collective-permute-start | bytes 393224 | tf_op jit(solution)/shard_map/ppermute | solution.py:309
  64.8 1.5 %collective-permute-start.16 = (bf16[256,256]{1,0:T(8,128)(2,1)S(1)}, bf16[256,256]{1,0:T(8,128)(2,1)S(1)}, u32[]{:S(2)}, u32[]{:S(2)}) collective-permute-start(bf16[256,256]{1,0:T(8,128)(2,1)S(1)} %slice.15), channel_id=1, source_target_pairs={{0,1},{1,0},{2,3},{3,2},{4,5},{5,4},{6,7},{7,6},{8,9},{9,8},{10,11... | collective-permute-start | bytes 393224 | tf_op jit(solution)/shard_map/ppermute | solution.py:311
